TPU v7x, 32 devices: a whole 2x2x4 slice. The times are simulated.
32 devices in a mesh: shard: 4 (over z), context: 4 (over x, core), tensor: 2 (over y).
Axes of the slice: x: 2, y: 2, z: 4, core: 2. Of those that a mesh axis runs over, the one named last changes fastest.
Arguments:
- tokens: bfloat16 [8, 1024, 1408], P('shard', 'context'), may hold values from -6 to 6
- skip_in: bfloat16 [8, 1024, 1408], P('shard', 'context'), may hold values from -6 to 6
- text_in: bfloat16 [8, 333, 1408], P('shard'), may hold values from -6 to 6
- grid_pos: int32 [8, 1024, 2], P('shard', 'context'), may hold values from 0 to 63
- time_ids: int32 [8], P('shard'), may hold values from 0 to 999
- cotangent: bfloat16 [8, 1024, 1408], P('shard', 'context'), may hold values from -6 to 6
- skip_weight: bfloat16 [2, 1408, 1408], P(None, ('shard', 'tensor')), may hold values from -0.109375 to 0.109375
- shift_weight: bfloat16 [1408, 1408], P(('shard', 'tensor')), may hold values from -0.15625 to 0.15625
- triple_weight: bfloat16 [1408, 3, 1408], P('shard', None, 'tensor'), may hold values from -0.15625 to 0.15625
- self_out_weight: bfloat16 [1408, 1408], P('tensor', 'shard'), may hold values from -0.4375 to 0.4375
- cross_q_weight: bfloat16 [1408, 1408], P('shard', 'tensor'), may hold values from -0.15625 to 0.15625
- cross_kv_weight: bfloat16 [1408, 2, 1408], P('shard', None, 'tensor'), may hold values from -0.15625 to 0.15625
- cross_out_weight: bfloat16 [1408, 1408], P('tensor', 'shard'), may hold values from -0.3125 to 0.3125
- up_weight: bfloat16 [1408, 6144], P('shard', 'tensor'), may hold values from -0.15625 to 0.15625
- down_weight: bfloat16 [6144, 1408], P('tensor', 'shard'), may hold values from -0.078125 to 0.078125
- norm_gains: float32 [4, 1408], replicated, may hold values from 0.25 to 1.75
- norm_biases: float32 [4, 1408], replicated, may hold values from -1.5 to 1.5
- head_gains: float32 [4, 88], replicated, may hold values from 0.25 to 1.75
- head_biases: float32 [4, 88], replicated, may hold values from -1.5 to 1.5
- width_biases: float32 [5, 1408], replicated, may hold values from -1.5 to 1.5
- column_biases: float32 [6, 1408], replicated, may hold values from -1.5 to 1.5
- hidden_biases: float32 [6144], replicated, may hold values from -1.5 to 1.5
Outputs:
- output: float32 [8, 1024, 1408], P('shard', 'context')
- grad_tokens: float32 [8, 1024, 1408], P('shard', 'context')
- grad_skip: float32 [8, 1024, 1408], P('shard', 'context')
- grad_text: float32 [8, 333, 1408], P('shard', None, ('context', 'tensor'))
- grad_skip_weight: float32 [2, 1408, 1408], P(None, ('shard', 'tensor'))
- grad_shift_weight: float32 [1408, 1408], P(('shard', 'tensor'))
- grad_triple_weight: float32 [1408, 3, 1408], P('shard', None, 'tensor')
- grad_self_out_weight: float32 [1408, 1408], P('tensor', 'shard')
- grad_cross_q_weight: float32 [1408, 1408], P('shard', 'tensor')
- grad_cross_kv_weight: float32 [1408, 2, 1408], P('shard', None, 'tensor')
- grad_cross_out_weight: float32 [1408, 1408], P('tensor', 'shard')
- grad_up_weight: float32 [1408, 6144], P('shard', 'tensor')
- grad_down_weight: float32 [6144, 1408], P('tensor', 'shard')
- grad_norm_gains: float32 [4, 1408], replicated
- grad_norm_biases: float32 [4, 1408], replicated
- grad_head_gains: float32 [4, 88], replicated
- grad_head_biases: float32 [4, 88], replicated
- grad_width_biases: float32 [5, 1408], replicated
- grad_column_biases: float32 [6, 1408], replicated
- grad_hidden_biases: float32 [6144], replicated
All inputs are finite; a program needn't handle non-finite values.
Results may differ from a plain program's by a relative error of at most 0.02.
Values may be sent and summed in bfloat16 or wider, within the bound.
A program may use at most 320 MiB of HBM per device.

v0:
```python
import math

import jax
import jax.numpy as jnp
from jax import lax
from jax.sharding import PartitionSpec as P

epsilon = 1e-06


def matmul(left_side, right_side):
    return jnp.dot(left_side, right_side, preferred_element_type=jnp.float32)


def contract(form, left_side, right_side):
    return jnp.einsum(form, left_side, right_side, preferred_element_type=jnp.float32)


def contract_rows(left_side, right_side):
    return lax.dot_general(
        left_side, right_side, (((0,), (0,)), ((), ())), preferred_element_type=jnp.float32
    )


def contract_cols(left_side, right_side):
    return lax.dot_general(
        left_side, right_side, (((1,), (1,)), ((), ())), preferred_element_type=jnp.float32
    )


def layer_norm(values, scale_vec, offset):
    center = values - jnp.mean(values, -1, keepdims=True)
    spread = jnp.mean(center * center, -1, keepdims=True)
    return center * lax.rsqrt(spread + epsilon) * scale_vec + offset


def rotary_tables(grid_rows, head_size):
    quarter = head_size // 4
    frequencies = 1.0 / 10000.0 ** (jnp.arange(quarter, dtype=jnp.float32) * 2.0 / (head_size // 2))
    row_angle = grid_rows[:, 0:1].astype(jnp.float32) * frequencies
    col_angle = grid_rows[:, 1:2].astype(jnp.float32) * frequencies
    angles = jnp.concatenate([row_angle, row_angle, col_angle, col_angle], 1)
    return (jnp.cos(angles)[:, None, :], jnp.sin(angles)[:, None, :])


def rotate(values, cosine, sine_rows):
    quarter = values.shape[-1] // 4
    part_one = values[..., :quarter]
    part_two = values[..., quarter : 2 * quarter]
    part_three = values[..., 2 * quarter : 3 * quarter]
    part_four = values[..., 3 * quarter :]
    turned = jnp.concatenate([-part_two, part_one, -part_four, part_three], -1)
    return values * cosine + turned * sine_rows


def time_vector(time_stamp, model_width):
    half_width = model_width // 2
    frequencies = jnp.exp(
        -math.log(10000.0) * jnp.arange(half_width, dtype=jnp.float32) / half_width
    )
    angles = time_stamp.astype(jnp.float32) * frequencies
    return jnp.concatenate([jnp.cos(angles), jnp.sin(angles)])


def branch_total(values):
    return lax.psum(values, "tensor")


def input_total(values):
    return lax.psum(values, "tensor")


def attention_forward(queries, key_rows, value_rows):
    total_rows, head_count, head_size = queries.shape
    block_rows = min(512, total_rows)
    block_count = total_rows // block_rows
    score_scale = head_size ** (-0.5)

    def one_block(state_in, row_block):
        scores = contract("qhd,khd->hqk", row_block, key_rows) * score_scale
        row_max = jnp.max(scores, -1, keepdims=True)
        exponent = jnp.exp(scores - row_max)
        weight_sum = jnp.sum(exponent, -1, keepdims=True)
        weights_low = (exponent / weight_sum).astype(jnp.bfloat16)
        mixture = contract("hqk,khd->qhd", weights_low, value_rows)
        return (state_in, (mixture.astype(jnp.bfloat16), (row_max + jnp.log(weight_sum))[..., 0]))

    unused, (mixture, log_sums) = lax.scan(
        one_block, 0, queries.reshape(block_count, block_rows, head_count, head_size)
    )
    return (mixture.reshape(total_rows, head_count, head_size), log_sums)


def attention_backward(queries, key_rows, value_rows, log_sums, grad_mix):
    total_rows, head_count, head_size = queries.shape
    block_rows = min(512, total_rows)
    block_count = total_rows // block_rows
    score_scale = head_size ** (-0.5)

    def one_block(state_in, inputs_now):
        key_grad, value_grad = state_in
        row_block, grad_block, sums_block = inputs_now
        scores = contract("qhd,khd->hqk", row_block, key_rows) * score_scale
        weights_full = jnp.exp(scores - sums_block[..., None])
        grad_weights = contract("qhd,khd->hqk", grad_block, value_rows)
        inner = jnp.sum(weights_full * grad_weights, -1, keepdims=True)
        grad_scores = (weights_full * (grad_weights - inner)).astype(jnp.bfloat16)
        query_grad = contract("hqk,khd->qhd", grad_scores, key_rows) * score_scale
        key_grad = key_grad + contract("hqk,qhd->khd", grad_scores, row_block) * score_scale
        value_grad = value_grad + contract(
            "hqk,qhd->khd", weights_full.astype(jnp.bfloat16), grad_block
        )
        return ((key_grad, value_grad), query_grad)

    block_shape = (block_count, block_rows, head_count, head_size)
    start_state = (jnp.zeros(key_rows.shape, jnp.float32), jnp.zeros(value_rows.shape, jnp.float32))
    (key_grad, value_grad), query_grad = lax.scan(
        one_block,
        start_state,
        (queries.reshape(block_shape), grad_mix.reshape(block_shape), log_sums),
    )
    return (query_grad.reshape(total_rows, head_count, head_size), key_grad, value_grad)


def grad_shape(array, along, factor, divisor):
    shape = list(array.shape)
    shape[along] = shape[along] * factor // divisor
    return tuple(shape)


def on_device(
    tokens,
    skip_in,
    text_in,
    grid_pos,
    time_ids,
    cotangent,
    skip_weight,
    shift_weight,
    triple_weight,
    self_out_weight,
    cross_q_weight,
    cross_kv_weight,
    cross_out_weight,
    up_weight,
    down_weight,
    norm_gains,
    norm_biases,
    head_gains,
    head_biases,
    width_biases,
    column_biases,
    hidden_biases,
):
    local_len = tokens.shape[1]
    model_width = tokens.shape[2]
    text_len = text_in.shape[1]
    head_size = head_gains.shape[1]
    col_width = triple_weight.shape[2]
    hidden_cols = up_weight.shape[1]
    heads_local = col_width // head_size
    shard_count = lax.axis_size("shard")
    group_count = shard_count * lax.axis_size("context")
    tensor_count = lax.axis_size("tensor")
    tensor_rank = lax.axis_index("tensor")
    context_rank = lax.axis_index("context")
    keep_tensor = (tensor_rank == 0).astype(jnp.float32)
    col_start = tensor_rank * col_width
    hidden_start = tensor_rank * hidden_cols
    token_shape = (local_len, heads_local, head_size)
    text_shape = (text_len, heads_local, head_size)

    def own_columns(values):
        return lax.dynamic_slice_in_dim(values, col_start, col_width, values.ndim - 1)

    local_weights = (
        triple_weight,
        self_out_weight,
        cross_q_weight,
        cross_kv_weight,
        cross_out_weight,
        up_weight,
        down_weight,
        skip_weight,
        shift_weight,
    )
    weight_dims = (0, 1, 0, 0, 1, 0, 1, 1, 0)
    factors = (shard_count,) * 7 + (shard_count * tensor_count,) * 2
    weight_zero = tuple(
        (
            jnp.zeros(grad_shape(array, along, factor, group_count), jnp.float32)
            for array, along, factor in zip(local_weights, weight_dims, factors)
        )
    )
    vector_zero = tuple(
        (
            jnp.zeros(array.shape, jnp.float32)
            for array in (
                norm_gains,
                norm_biases,
                head_gains,
                head_biases,
                width_biases,
                column_biases,
                hidden_biases,
            )
        )
    )

    def micro_step(state_in, inputs_now):
        weight_acc, vector_acc = state_in
        tok_rows, skip_rows, text_rows, grid_rows, time_stamp, cot_rows = inputs_now
        (
            triple_full,
            self_out_full,
            cross_q_full,
            cross_kv_full,
            cross_out_full,
            up_full,
            down_full,
        ) = (
            lax.all_gather(triple_weight, "shard", axis=0, tiled=True),
            lax.all_gather(self_out_weight, "shard", axis=1, tiled=True),
            lax.all_gather(cross_q_weight, "shard", axis=0, tiled=True),
            lax.all_gather(cross_kv_weight, "shard", axis=0, tiled=True),
            lax.all_gather(cross_out_weight, "shard", axis=1, tiled=True),
            lax.all_gather(up_weight, "shard", axis=0, tiled=True),
            lax.all_gather(down_weight, "shard", axis=1, tiled=True),
        )
        skip_full, shift_full = (
            lax.all_gather(skip_weight, ("shard", "tensor"), axis=1, tiled=True),
            lax.all_gather(shift_weight, ("shard", "tensor"), axis=0, tiled=True),
        )
        cosine, sine_rows = rotary_tables(grid_rows, head_size)
        silu_low = jax.nn.silu(time_vector(time_stamp, model_width)).astype(jnp.bfloat16)
        summed = matmul(tok_rows, skip_full[0]) + matmul(skip_rows, skip_full[1]) + width_biases[0]
        shift_row = matmul(silu_low[None, :], shift_full)[0] + width_biases[1]

        def first_piece(summed_in, shift_in, gain_rows, bias_rows):
            resid_out = layer_norm(summed_in, gain_rows[0], bias_rows[0])
            return (resid_out, layer_norm(resid_out, gain_rows[1], bias_rows[1]) + shift_in)

        (resid_zero, normed_one), pull_first = jax.vjp(
            first_piece, summed, shift_row, norm_gains, norm_biases
        )
        normed_one_low = normed_one.astype(jnp.bfloat16)
        triple = contract("td,dcn->tcn", normed_one_low, triple_full) + own_columns(
            column_biases[0:3]
        )

        def self_piece(triple_in, gain_rows, bias_rows):
            queries = rotate(
                layer_norm(triple_in[:, 0].reshape(token_shape), gain_rows[0], bias_rows[0]),
                cosine,
                sine_rows,
            )
            key_rows = rotate(
                layer_norm(triple_in[:, 1].reshape(token_shape), gain_rows[1], bias_rows[1]),
                cosine,
                sine_rows,
            )
            return (queries, key_rows, triple_in[:, 2].reshape(token_shape))

        (query_tok, key_tok, value_tok), pull_self = jax.vjp(
            self_piece, triple, head_gains, head_biases
        )
        query_head, key_head, value_head = (
            lax.all_to_all(
                query_tok.astype(jnp.bfloat16), "context", split_axis=1, concat_axis=0, tiled=True
            ),
            lax.all_to_all(
                key_tok.astype(jnp.bfloat16), "context", split_axis=1, concat_axis=0, tiled=True
            ),
            lax.all_to_all(
                value_tok.astype(jnp.bfloat16), "context", split_axis=1, concat_axis=0, tiled=True
            ),
        )
        mix_head, self_sums = attention_forward(query_head, key_head, value_head)
        mix_tok = lax.all_to_all(
            mix_head, "context", split_axis=0, concat_axis=1, tiled=True
        ).reshape(local_len, col_width)
        resid_one = resid_zero + (branch_total(matmul(mix_tok, self_out_full)) + width_biases[2])

        def second_piece(resid_in, gain_rows, bias_rows):
            return layer_norm(resid_in, gain_rows[2], bias_rows[2])

        normed_two, pull_second = jax.vjp(second_piece, resid_one, norm_gains, norm_biases)
        normed_two_low = normed_two.astype(jnp.bfloat16)
        cross_raw = matmul(normed_two_low, cross_q_full) + own_columns(column_biases[3])
        pair_raw = contract("td,dcn->tcn", text_rows, cross_kv_full) + own_columns(
            column_biases[4:6]
        )

        def cross_piece(query_in, pair_in, gain_rows, bias_rows):
            queries = rotate(
                layer_norm(query_in.reshape(token_shape), gain_rows[2], bias_rows[2]),
                cosine,
                sine_rows,
            )
            key_rows = layer_norm(pair_in[:, 0].reshape(text_shape), gain_rows[3], bias_rows[3])
            return (queries, key_rows, pair_in[:, 1].reshape(text_shape))

        (cross_query, cross_key, cross_value), pull_cross = jax.vjp(
            cross_piece, cross_raw, pair_raw, head_gains, head_biases
        )
        cross_query_low = cross_query.astype(jnp.bfloat16)
        cross_key_low = cross_key.astype(jnp.bfloat16)
        cross_value_low = cross_value.astype(jnp.bfloat16)
        cross_mix, cross_sums = attention_forward(cross_query_low, cross_key_low, cross_value_low)
        cross_flat = cross_mix.reshape(local_len, col_width)
        resid_two = resid_one + (branch_total(matmul(cross_flat, cross_out_full)) + width_biases[3])

        def third_piece(resid_in, gain_rows, bias_rows):
            return layer_norm(resid_in, gain_rows[3], bias_rows[3])

        normed_three, pull_third = jax.vjp(third_piece, resid_two, norm_gains, norm_biases)
        normed_three_low = normed_three.astype(jnp.bfloat16)
        hidden = matmul(normed_three_low, up_full) + lax.dynamic_slice_in_dim(
            hidden_biases, hidden_start, hidden_cols, 0
        )

        def gelu_piece(hidden_in):
            return jax.nn.gelu(hidden_in, approximate=True)

        active, pull_gelu = jax.vjp(gelu_piece, hidden)
        active_low = active.astype(jnp.bfloat16)
        result = resid_two + (branch_total(matmul(active_low, down_full)) + width_biases[4])
        grad_out = cot_rows.astype(jnp.float32)
        down_grad = contract_rows(active_low, cot_rows)
        (hidden_grad,) = pull_gelu(contract_cols(cot_rows, down_full))
        hidden_grad_low = hidden_grad.astype(jnp.bfloat16)
        up_grad = contract_rows(normed_three_low, hidden_grad_low)
        third_grads = pull_third(input_total(contract_cols(hidden_grad_low, up_full)))
        resid_two_grad = grad_out + third_grads[0]
        grad_two_low = resid_two_grad.astype(jnp.bfloat16)
        cross_out_grad = contract_rows(cross_flat, grad_two_low)
        cross_mix_grad = (
            contract_cols(grad_two_low, cross_out_full).astype(jnp.bfloat16).reshape(token_shape)
        )
        cross_q_back, cross_k_back, cross_v_back = attention_backward(
            cross_query_low, cross_key_low, cross_value_low, cross_sums, cross_mix_grad
        )
        cross_grads = pull_cross((cross_q_back, cross_k_back, cross_v_back))
        cross_grad_low = cross_grads[0].astype(jnp.bfloat16)
        cross_q_grad = contract_rows(normed_two_low, cross_grad_low)
        pair_total = lax.psum_scatter(
            cross_grads[1].astype(jnp.bfloat16), "context", scatter_dimension=2, tiled=True
        )
        slice_width = pair_total.shape[2]
        slice_start = context_rank * slice_width
        cross_kv_grad = lax.dynamic_update_slice_in_dim(
            jnp.zeros(cross_kv_full.shape, jnp.float32),
            contract("td,tcn->dcn", text_rows, pair_total),
            slice_start,
            2,
        )
        text_part = contract(
            "tcn,dcn->td",
            pair_total,
            lax.dynamic_slice_in_dim(cross_kv_full, slice_start, slice_width, 2),
        )
        text_grad = lax.psum_scatter(
            text_part.astype(jnp.bfloat16), ("context", "tensor"), scatter_dimension=1, tiled=True
        ).astype(jnp.float32)
        second_grads = pull_second(input_total(contract_cols(cross_grad_low, cross_q_full)))
        resid_one_grad = resid_two_grad + second_grads[0]
        grad_one_low = resid_one_grad.astype(jnp.bfloat16)
        self_out_grad = contract_rows(mix_tok, grad_one_low)
        mix_grad = (
            contract_cols(grad_one_low, self_out_full).astype(jnp.bfloat16).reshape(token_shape)
        )
        mix_grad_head = lax.all_to_all(mix_grad, "context", split_axis=1, concat_axis=0, tiled=True)
        query_back, key_back, value_back = attention_backward(
            query_head, key_head, value_head, self_sums, mix_grad_head
        )
        query_tok_grad, key_tok_grad, value_tok_grad = (
            lax.all_to_all(
                query_back.astype(jnp.bfloat16), "context", split_axis=0, concat_axis=1, tiled=True
            ),
            lax.all_to_all(
                key_back.astype(jnp.bfloat16), "context", split_axis=0, concat_axis=1, tiled=True
            ),
            lax.all_to_all(
                value_back.astype(jnp.bfloat16), "context", split_axis=0, concat_axis=1, tiled=True
            ),
        )
        self_grads = pull_self(
            (
                query_tok_grad.astype(jnp.float32),
                key_tok_grad.astype(jnp.float32),
                value_tok_grad.astype(jnp.float32),
            )
        )
        triple_grad_low = self_grads[0].astype(jnp.bfloat16)
        triple_w_grad = contract("td,tcn->dcn", normed_one_low, triple_grad_low)
        first_grads = pull_first(
            (resid_one_grad, input_total(contract("tcn,dcn->td", triple_grad_low, triple_full)))
        )
        summed_low = first_grads[0].astype(jnp.bfloat16)
        skip_grad = jnp.stack(
            [contract_rows(tok_rows, summed_low), contract_rows(skip_rows, summed_low)]
        )
        tok_grad = contract_cols(summed_low, skip_full[0])
        skip_rows_grad = contract_cols(summed_low, skip_full[1])
        shift_grad = jnp.outer(silu_low.astype(jnp.float32), first_grads[1])
        gains_grad = (first_grads[2] + second_grads[1] + third_grads[1]) * keep_tensor
        biases_grad = (first_grads[3] + second_grads[2] + third_grads[2]) * keep_tensor
        head_gain_grad = self_grads[1] + cross_grads[2]
        head_bias_grad = self_grads[2] + cross_grads[3]
        width_grad = (
            jnp.stack(
                [
                    jnp.sum(summed_low.astype(jnp.float32), 0),
                    first_grads[1],
                    jnp.sum(grad_one_low.astype(jnp.float32), 0),
                    jnp.sum(grad_two_low.astype(jnp.float32), 0),
                    jnp.sum(grad_out, 0),
                ]
            )
            * keep_tensor
        )
        column_grad = jnp.zeros(column_biases.shape, jnp.float32)
        column_grad = lax.dynamic_update_slice(
            column_grad, jnp.sum(triple_grad_low.astype(jnp.float32), 0), (0, col_start)
        )
        column_grad = lax.dynamic_update_slice(
            column_grad, jnp.sum(cross_grad_low.astype(jnp.float32), 0)[None, :], (3, col_start)
        )
        column_grad = lax.dynamic_update_slice(
            column_grad, jnp.sum(pair_total.astype(jnp.float32), 0), (4, col_start + slice_start)
        )
        hidden_bias_grad = lax.dynamic_update_slice_in_dim(
            jnp.zeros(hidden_biases.shape, jnp.float32),
            jnp.sum(hidden_grad_low.astype(jnp.float32), 0),
            hidden_start,
            0,
        )
        vector_now = (
            gains_grad,
            biases_grad,
            head_gain_grad,
            head_bias_grad,
            width_grad,
            column_grad,
            hidden_bias_grad,
        )
        grads_now = (
            lax.psum_scatter(triple_w_grad, ("shard", "context"), scatter_dimension=0, tiled=True),
            lax.psum_scatter(self_out_grad, ("shard", "context"), scatter_dimension=1, tiled=True),
            lax.psum_scatter(cross_q_grad, ("shard", "context"), scatter_dimension=0, tiled=True),
            lax.psum_scatter(cross_kv_grad, ("shard", "context"), scatter_dimension=0, tiled=True),
            lax.psum_scatter(cross_out_grad, ("shard", "context"), scatter_dimension=1, tiled=True),
            lax.psum_scatter(up_grad, ("shard", "context"), scatter_dimension=0, tiled=True),
            lax.psum_scatter(down_grad, ("shard", "context"), scatter_dimension=1, tiled=True),
            lax.psum_scatter(skip_grad, ("shard", "context"), scatter_dimension=1, tiled=True),
            lax.psum_scatter(shift_grad, ("shard", "context"), scatter_dimension=0, tiled=True),
        )
        weight_acc = jax.tree.map(jnp.add, weight_acc, tuple(grads_now))
        vector_acc = jax.tree.map(jnp.add, vector_acc, vector_now)
        return ((weight_acc, vector_acc), (result, tok_grad, skip_rows_grad, text_grad))

    (weight_acc, vector_acc), (results, grad_tokens, grad_skips, grad_texts) = lax.scan(
        micro_step,
        (weight_zero, vector_zero),
        (tokens, skip_in, text_in, grid_pos, time_ids, cotangent),
    )
    regathered = (
        lax.all_gather(weight_acc[0].astype(jnp.bfloat16), "context", axis=0, tiled=True).astype(
            jnp.float32
        ),
        lax.all_gather(weight_acc[1].astype(jnp.bfloat16), "context", axis=1, tiled=True).astype(
            jnp.float32
        ),
        lax.all_gather(weight_acc[2].astype(jnp.bfloat16), "context", axis=0, tiled=True).astype(
            jnp.float32
        ),
        lax.all_gather(weight_acc[3].astype(jnp.bfloat16), "context", axis=0, tiled=True).astype(
            jnp.float32
        ),
        lax.all_gather(weight_acc[4].astype(jnp.bfloat16), "context", axis=1, tiled=True).astype(
            jnp.float32
        ),
        lax.all_gather(weight_acc[5].astype(jnp.bfloat16), "context", axis=0, tiled=True).astype(
            jnp.float32
        ),
        lax.all_gather(weight_acc[6].astype(jnp.bfloat16), "context", axis=1, tiled=True).astype(
            jnp.float32
        ),
        lax.all_gather(weight_acc[7].astype(jnp.bfloat16), "context", axis=1, tiled=True).astype(
            jnp.float32
        ),
        lax.all_gather(weight_acc[8].astype(jnp.bfloat16), "context", axis=0, tiled=True).astype(
            jnp.float32
        ),
    )
    skip_rows_count = skip_weight.shape[1]
    shift_rows_count = shift_weight.shape[0]
    skip_grad_out = lax.dynamic_slice_in_dim(
        regathered[7], tensor_rank * skip_rows_count, skip_rows_count, 1
    )
    shift_grad_out = lax.dynamic_slice_in_dim(
        regathered[8], tensor_rank * shift_rows_count, shift_rows_count, 0
    )
    vectors_out = lax.psum(
        (
            vector_acc[0],
            vector_acc[1],
            vector_acc[2],
            vector_acc[3],
            vector_acc[4],
            vector_acc[5],
            vector_acc[6],
        ),
        ("shard", "context", "tensor"),
    )
    return (
        results,
        grad_tokens,
        grad_skips,
        grad_texts,
        skip_grad_out,
        shift_grad_out,
        regathered[0],
        regathered[1],
        regathered[2],
        regathered[3],
        regathered[4],
        regathered[5],
        regathered[6],
        vectors_out[0],
        vectors_out[1],
        vectors_out[2],
        vectors_out[3],
        vectors_out[4],
        vectors_out[5],
        vectors_out[6],
    )


def solution(mesh):
    placed = (
        P("shard", "context", None),
        P("shard", "context", None),
        P("shard", None, None),
        P("shard", "context", None),
        P("shard"),
        P("shard", "context", None),
        P(None, ("shard", "tensor"), None),
        P(("shard", "tensor"), None),
        P("shard", None, "tensor"),
        P("tensor", "shard"),
        P("shard", "tensor"),
        P("shard", None, "tensor"),
        P("tensor", "shard"),
        P("shard", "tensor"),
        P("tensor", "shard"),
        P(),
        P(),
        P(),
        P(),
        P(),
        P(),
        P(),
    )
    return jax.shard_map(
        on_device,
        mesh=mesh,
        in_specs=placed,
        out_specs=(
            P("shard", "context", None),
            P("shard", "context", None),
            P("shard", "context", None),
            P("shard", None, ("context", "tensor")),
            P(None, ("shard", "tensor"), None),
            P(("shard", "tensor"), None),
            P("shard", None, "tensor"),
            P("tensor", "shard"),
            P("shard", "tensor"),
            P("shard", None, "tensor"),
            P("tensor", "shard"),
            P("shard", "tensor"),
            P("tensor", "shard"),
            P(),
            P(),
            P(),
            P(),
            P(),
            P(),
            P(),
        ),
        check_vma=False,
    )
```

profile of v0, /device:TPU:0, one launch (start us, length us, event | category | flops | bytes accessed | tf_op | source)
XLA Modules:
  0.0 5530.2 jit_solution(7408619517854613042)
XLA Ops:
  21.9 5336.6 %while.120 = (s32[]{:T(128)}, f32[88,3,704]{2,0,1:T(8,128)}, f32[704,88]{0,1:T(8,128)}, f32[88,704]{1,0:T(8,128)}, f32[88,2,704]{2,1,0:T(2,128)}, /*index=5*/f32...) while((s32[]{:T(128)}, f32[88,3,704]{2,0,1:T(8,128)}, ...), condition=%wide.region_84.85_spmd.clone, body=%wide.region_0.84_spmd.clone.sunk | while | flops 32699170816 | bytes 1547458560 | solution.py:462
  35.7 61.9 %all-gather.22.cloned.1.call-done = bf16[1408,1408]{1,0:T(8,128)(2,1)} async-done(((bf16[176,1408]{1,0:T(8,128)(2,1)}), bf16[1408,1408]{1,0:T(8,128)(2,1)}) %all-gather.22.cloned.1.call-update) | async-done | bytes 3964944 | tf_op jit(solution)/shard_map/while/body/eval_jaxpr/all_gather | solution.py:232
  100.4 116.9 %all-gather.24.cloned.1.call-done = bf16[2,1408,1408]{2,1,0:T(8,128)(2,1)} async-done(((bf16[2,176,1408]{2,1,0:T(8,128)(2,1)}), bf16[2,1408,1408]{2,1,0:T(8,128)(2,1)}) %all-gather.24.cloned.1.call-update) | async-done | bytes 7929872 | tf_op jit(solution)/shard_map/while/body/eval_jaxpr/all_gather | solution.py:231
  225.9 145.7 %all-gather.26.cloned.1.call-done = bf16[1408,3,704]{2,1,0:T(4,128)(2,1)} async-done(((bf16[352,3,704]{2,1,0:T(4,128)(2,1)}), bf16[1408,3,704]{2,1,0:T(4,128)(2,1)}) %all-gather.26.cloned.1.call-update) | async-done | bytes 5947408 | tf_op jit(solution)/shard_map/while/body/eval_jaxpr/all_gather | solution.py:222
  442.6 59.0 %all-gather.32.cloned.1.call-done = bf16[1408,2,704]{2,0,1:T(8,128)(2,1)} async-done(((bf16[352,2,704]{2,0,1:T(8,128)(2,1)}), bf16[1408,2,704]{2,0,1:T(8,128)(2,1)}) %all-gather.32.cloned.1.call-update) | async-done | bytes 3964944 | tf_op jit(solution)/shard_map/while/body/eval_jaxpr/all_gather | solution.py:225
  514.5 37.0 all-reduce.51.cloned.1.call-done
  555.9 43.9 all-gather.30.cloned.1.call-done
  612.7 34.3 all-gather.36.cloned.1.call-done
  652.2 46.1 all-reduce.53.cloned.1.call-done
  701.7 151.9 %all-gather.34.cloned.1.call-done = bf16[1408,3072]{1,0:T(8,128)(2,1)} async-done(((bf16[352,3072]{1,0:T(8,128)(2,1)}), bf16[1408,3072]{1,0:T(8,128)(2,1)}) %all-gather.34.cloned.1.call-update) | async-done | bytes 8650768 | tf_op jit(solution)/shard_map/while/body/eval_jaxpr/all_gather | solution.py:227
  861.9 145.4 %all-gather.38.cloned.1.call-done = bf16[3072,1408]{0,1:T(8,128)(2,1)} async-done(((bf16[3072,352]{0,1:T(8,128)(2,1)}), bf16[3072,1408]{0,1:T(8,128)(2,1)}) %all-gather.38.cloned.1.call-update) | async-done | bytes 8650768 | tf_op jit(solution)/shard_map/while/body/eval_jaxpr/all_gather | solution.py:228
  1022.0 46.7 all-reduce.55.cloned.1.call-done
  1096.9 37.9 all-reduce.57.cloned.1.call-done
  1156.2 24.6 while.122
  1249.6 64.4 %dynamic_update_slice.109 = f32[1408,2,704]{2,1,0:T(2,128)} dynamic-update-slice(f32[1408,2,704]{2,1,0:T(2,128)} %broadcast.1309, f32[1408,2,176]{2,1,0:T(2,128)} %copy.264, s32[]{:T(128)} %constant.318.clone.1..sunk, s32[]{:T(128)} %constant.318.clone.1..sunk, s32[]{:T(128)} %get-tuple-element.2621) | dynamic-update-slice | bytes 3964932 | tf_op jit(solution)/shard_map/while/body/eval_jaxpr/dynamic_update_slice | solution.py:351
  1397.2 263.5 %all-reduce.59.cloned.1.call-done = f32[1408,2,704]{2,1,0:T(2,128)} async-done(((f32[1408,2,704]{2,1,0:T(2,128)}), f32[1408,2,704]{2,1,0:T(2,128)}) %all-reduce.59.cloned.1.call-update) | async-done | bytes 7929872 | tf_op jit(solution)/shard_map/while
  1662.4 76.5 %reduce-scatter.19.cloned.1.call-done = f32[88,704]{1,0:T(8,128)} async-done(((f32[1408,704]{1,0:T(8,128)}), f32[88,704]{1,0:T(8,128)}) %reduce-scatter.19.cloned.1.call-update) | async-done | bytes 247824 | tf_op jit(solution)/shard_map/while/body/eval_jaxpr/reduce_scatter | solution.py:450
  1740.0 75.5 %reduce-scatter.23.cloned.1.call-done = f32[704,88]{0,1:T(8,128)} async-done(((f32[704,1408]{0,1:T(8,128)}), f32[704,88]{0,1:T(8,128)}) %reduce-scatter.23.cloned.1.call-update) | async-done | bytes 247824 | tf_op jit(solution)/shard_map/while/body/eval_jaxpr/reduce_scatter | solution.py:452
  1816.6 76.0 %reduce-scatter.17.cloned.1.call-done = f32[704,88]{0,1:T(8,128)} async-done(((f32[704,1408]{0,1:T(8,128)}), f32[704,88]{0,1:T(8,128)}) %reduce-scatter.17.cloned.1.call-update) | async-done | bytes 247824 | tf_op jit(solution)/shard_map/while/body/eval_jaxpr/reduce_scatter | solution.py:449
  1893.6 104.8 %reduce-scatter.31.cloned.1.call-done = f32[88,1408]{1,0:T(8,128)} async-done(((f32[1408,1408]{1,0:T(8,128)}), f32[88,1408]{1,0:T(8,128)}) %reduce-scatter.31.cloned.1.call-update) | async-done | bytes 495632 | tf_op jit(solution)/shard_map/while
  1999.7 140.4 %reduce-scatter.15.cloned.1.call-done = f32[88,3,704]{2,0,1:T(8,128)} async-done(((f32[1408,3,704]{2,0,1:T(8,128)}), f32[88,3,704]{2,0,1:T(8,128)}) %reduce-scatter.15.cloned.1.call-update) | async-done | bytes 743440 | tf_op jit(solution)/shard_map/while/body/eval_jaxpr/reduce_scatter | solution.py:448
  2141.5 184.0 %reduce-scatter.25.cloned.1.call-done = f32[88,3072]{1,0:T(8,128)} async-done(((f32[1408,3072]{1,0:T(8,128)}), f32[88,3072]{1,0:T(8,128)}) %reduce-scatter.25.cloned.1.call-update) | async-done | bytes 1081360 | tf_op jit(solution)/shard_map/while/body/eval_jaxpr/reduce_scatter | solution.py:453
  2327.1 183.4 %reduce-scatter.27.cloned.1.call-done = f32[3072,88]{0,1:T(8,128)} async-done(((f32[3072,1408]{0,1:T(8,128)}), f32[3072,88]{0,1:T(8,128)}) %reduce-scatter.27.cloned.1.call-update) | async-done | bytes 1081360 | tf_op jit(solution)/shard_map/while/body/eval_jaxpr/reduce_scatter | solution.py:454
  2512.2 175.3 %reduce-scatter.29.cloned.1.call-done = f32[2,88,1408]{2,1,0:T(8,128)} async-done(((f32[2,1408,1408]{2,1,0:T(8,128)}), f32[2,88,1408]{2,1,0:T(8,128)}) %reduce-scatter.29.cloned.1.call-update) | async-done | bytes 991248 | tf_op jit(solution)/shard_map/while/body/eval_jaxpr/reduce_scatter | solution.py:455
  2704.0 58.1 %all-gather.22.cloned.1.call-done = bf16[1408,1408]{1,0:T(8,128)(2,1)} async-done(((bf16[176,1408]{1,0:T(8,128)(2,1)}), bf16[1408,1408]{1,0:T(8,128)(2,1)}) %all-gather.22.cloned.1.call-update) | async-done | bytes 3964944 | tf_op jit(solution)/shard_map/while/body/eval_jaxpr/all_gather | solution.py:232
  2764.8 116.7 %all-gather.24.cloned.1.call-done = bf16[2,1408,1408]{2,1,0:T(8,128)(2,1)} async-done(((bf16[2,176,1408]{2,1,0:T(8,128)(2,1)}), bf16[2,1408,1408]{2,1,0:T(8,128)(2,1)}) %all-gather.24.cloned.1.call-update) | async-done | bytes 7929872 | tf_op jit(solution)/shard_map/while/body/eval_jaxpr/all_gather | solution.py:231
  2890.1 145.6 %all-gather.26.cloned.1.call-done = bf16[1408,3,704]{2,1,0:T(4,128)(2,1)} async-done(((bf16[352,3,704]{2,1,0:T(4,128)(2,1)}), bf16[1408,3,704]{2,1,0:T(4,128)(2,1)}) %all-gather.26.cloned.1.call-update) | async-done | bytes 5947408 | tf_op jit(solution)/shard_map/while/body/eval_jaxpr/all_gather | solution.py:222
  3106.7 59.4 %all-gather.32.cloned.1.call-done = bf16[1408,2,704]{2,0,1:T(8,128)(2,1)} async-done(((bf16[352,2,704]{2,0,1:T(8,128)(2,1)}), bf16[1408,2,704]{2,0,1:T(8,128)(2,1)}) %all-gather.32.cloned.1.call-update) | async-done | bytes 3964944 | tf_op jit(solution)/shard_map/while/body/eval_jaxpr/all_gather | solution.py:225
  3178.9 37.1 all-reduce.51.cloned.1.call-done
  3220.5 43.9 all-gather.30.cloned.1.call-done
  3277.3 34.1 all-gather.36.cloned.1.call-done
  3316.9 45.8 all-reduce.53.cloned.1.call-done
  3366.2 152.1 %all-gather.34.cloned.1.call-done = bf16[1408,3072]{1,0:T(8,128)(2,1)} async-done(((bf16[352,3072]{1,0:T(8,128)(2,1)}), bf16[1408,3072]{1,0:T(8,128)(2,1)}) %all-gather.34.cloned.1.call-update) | async-done | bytes 8650768 | tf_op jit(solution)/shard_map/while/body/eval_jaxpr/all_gather | solution.py:227
  3526.5 145.2 %all-gather.38.cloned.1.call-done = bf16[3072,1408]{0,1:T(8,128)(2,1)} async-done(((bf16[3072,352]{0,1:T(8,128)(2,1)}), bf16[3072,1408]{0,1:T(8,128)(2,1)}) %all-gather.38.cloned.1.call-update) | async-done | bytes 8650768 | tf_op jit(solution)/shard_map/while/body/eval_jaxpr/all_gather | solution.py:228
  3686.4 46.7 all-reduce.55.cloned.1.call-done
  3761.3 37.9 all-reduce.57.cloned.1.call-done
  3820.5 24.6 while.122
  3914.0 64.4 %dynamic_update_slice.109 = f32[1408,2,704]{2,1,0:T(2,128)} dynamic-update-slice(f32[1408,2,704]{2,1,0:T(2,128)} %broadcast.1309, f32[1408,2,176]{2,1,0:T(2,128)} %copy.264, s32[]{:T(128)} %constant.318.clone.1..sunk, s32[]{:T(128)} %constant.318.clone.1..sunk, s32[]{:T(128)} %get-tuple-element.2621) | dynamic-update-slice | bytes 3964932 | tf_op jit(solution)/shard_map/while/body/eval_jaxpr/dynamic_update_slice | solution.py:351
  4061.6 263.5 %all-reduce.59.cloned.1.call-done = f32[1408,2,704]{2,1,0:T(2,128)} async-done(((f32[1408,2,704]{2,1,0:T(2,128)}), f32[1408,2,704]{2,1,0:T(2,128)}) %all-reduce.59.cloned.1.call-update) | async-done | bytes 7929872 | tf_op jit(solution)/shard_map/while
  4326.8 76.4 %reduce-scatter.19.cloned.1.call-done = f32[88,704]{1,0:T(8,128)} async-done(((f32[1408,704]{1,0:T(8,128)}), f32[88,704]{1,0:T(8,128)}) %reduce-scatter.19.cloned.1.call-update) | async-done | bytes 247824 | tf_op jit(solution)/shard_map/while/body/eval_jaxpr/reduce_scatter | solution.py:450
  4404.2 75.7 %reduce-scatter.23.cloned.1.call-done = f32[704,88]{0,1:T(8,128)} async-done(((f32[704,1408]{0,1:T(8,128)}), f32[704,88]{0,1:T(8,128)}) %reduce-scatter.23.cloned.1.call-update) | async-done | bytes 247824 | tf_op jit(solution)/shard_map/while/body/eval_jaxpr/reduce_scatter | solution.py:452
  4481.0 76.0 %reduce-scatter.17.cloned.1.call-done = f32[704,88]{0,1:T(8,128)} async-done(((f32[704,1408]{0,1:T(8,128)}), f32[704,88]{0,1:T(8,128)}) %reduce-scatter.17.cloned.1.call-update) | async-done | bytes 247824 | tf_op jit(solution)/shard_map/while/body/eval_jaxpr/reduce_scatter | solution.py:449
  4558.0 104.6 %reduce-scatter.31.cloned.1.call-done = f32[88,1408]{1,0:T(8,128)} async-done(((f32[1408,1408]{1,0:T(8,128)}), f32[88,1408]{1,0:T(8,128)}) %reduce-scatter.31.cloned.1.call-update) | async-done | bytes 495632 | tf_op jit(solution)/shard_map/while
  4663.9 140.3 %reduce-scatter.15.cloned.1.call-done = f32[88,3,704]{2,0,1:T(8,128)} async-done(((f32[1408,3,704]{2,0,1:T(8,128)}), f32[88,3,704]{2,0,1:T(8,128)}) %reduce-scatter.15.cloned.1.call-update) | async-done | bytes 743440 | tf_op jit(solution)/shard_map/while/body/eval_jaxpr/reduce_scatter | solution.py:448
  4805.5 183.8 %reduce-scatter.25.cloned.1.call-done = f32[88,3072]{1,0:T(8,128)} async-done(((f32[1408,3072]{1,0:T(8,128)}), f32[88,3072]{1,0:T(8,128)}) %reduce-scatter.25.cloned.1.call-update) | async-done | bytes 1081360 | tf_op jit(solution)/shard_map/while/body/eval_jaxpr/reduce_scatter | solution.py:453
  4991.0 183.3 %reduce-scatter.27.cloned.1.call-done = f32[3072,88]{0,1:T(8,128)} async-done(((f32[3072,1408]{0,1:T(8,128)}), f32[3072,88]{0,1:T(8,128)}) %reduce-scatter.27.cloned.1.call-update) | async-done | bytes 1081360 | tf_op jit(solution)/shard_map/while/body/eval_jaxpr/reduce_scatter | solution.py:454
  5176.0 175.8 %reduce-scatter.29.cloned.1.call-done = f32[2,88,1408]{2,1,0:T(8,128)} async-done(((f32[2,1408,1408]{2,1,0:T(8,128)}), f32[2,88,1408]{2,1,0:T(8,128)}) %reduce-scatter.29.cloned.1.call-update) | async-done | bytes 991248 | tf_op jit(solution)/shard_map/while/body/eval_jaxpr/reduce_scatter | solution.py:455
  5464.5 48.5 all-reduce.49.cloned.1.call-done
  (1680 shorter events, 929.9 us)
Async XLA Ops:
  22.7 194.6 %all-gather.24.cloned.1.call-start = ((), (), s32[]{:S(2)}) async-start(), calls=%async_computation.24 | async-start | bytes 8921088 | tf_op jit(solution)/shard_map/while/body/eval_jaxpr/all_gather | solution.py:231
  23.4 348.1 %all-gather.26.cloned.1.call-start = ((), (), s32[]{:S(2)}) async-start(), calls=%async_computation.25 | async-start | bytes 10813440 | tf_op jit(solution)/shard_map/while/body/eval_jaxpr/all_gather | solution.py:222
  24.2 412.5 %all-gather.28.cloned.1.call-start = ((), (), s32[]{:S(2)}) async-start(), calls=%async_computation.26 | async-start | bytes 2703360 | tf_op jit(solution)/shard_map/while/body/eval_jaxpr/all_gather | solution.py:223
  24.8 476.8 %all-gather.32.cloned.1.call-start = ((), (), s32[]{:S(2)}) async-start(), calls=%async_computation.29 | async-start | bytes 5406720 | tf_op jit(solution)/shard_map/while/body/eval_jaxpr/all_gather | solution.py:225
  406.8 144.7 %all-reduce.51.cloned.1.call-start = ((), (), s32[]{:S(2)}) async-start(), calls=%async_computation.28 | async-start | bytes 2883584 | tf_op jit(solution)/shard_map/while/body/eval_jaxpr/psum | solution.py:66
  440.4 159.5 %all-gather.30.cloned.1.call-start = ((), (), s32[]{:S(2)}) async-start(), calls=%async_computation.27 | async-start | bytes 2703360 | tf_op jit(solution)/shard_map/while/body/eval_jaxpr/all_gather | solution.py:224
  441.1 205.8 %all-gather.36.cloned.1.call-start = ((), (), s32[]{:S(2)}) async-start(), calls=%async_computation.31 | async-start | bytes 2703360 | tf_op jit(solution)/shard_map/while/body/eval_jaxpr/all_gather | solution.py:226
  441.9 256.4 %all-reduce.53.cloned.1.call-start = ((), (), s32[]{:S(2)}) async-start(), calls=%async_computation.32 | async-start | bytes 2883584 | tf_op jit(solution)/shard_map/while/body/eval_jaxpr/psum | solution.py:66
  650.7 203.0 %all-gather.34.cloned.1.call-start = ((), (), s32[]{:S(2)}) async-start(), calls=%async_computation.30 | async-start | bytes 10813440 | tf_op jit(solution)/shard_map/while/body/eval_jaxpr/all_gather | solution.py:227
  651.3 356.0 %all-gather.38.cloned.1.call-start = ((), (), s32[]{:S(2)}) async-start(), calls=%async_computation.33 | async-start | bytes 10813440 | tf_op jit(solution)/shard_map/while/body/eval_jaxpr/all_gather | solution.py:228
  652.0 416.7 %all-reduce.55.cloned.1.call-start = ((), (), s32[]{:S(2)}) async-start(), calls=%async_computation.34 | async-start | bytes 2883584 | tf_op jit(solution)/shard_map/while/body/eval_jaxpr/psum | solution.py:70
  1021.7 113.1 %all-reduce.57.cloned.1.call-start = ((), (), s32[]{:S(2)}) async-start(), calls=%async_computation.35 | async-start | bytes 2883584 | tf_op jit(solution)/shard_map/while/body/eval_jaxpr/psum | solution.py:70
  1212.5 114.3 %all-reduce.61.cloned.1.call-start = ((), (), s32[]{:S(2)}) async-start(), calls=%async_computation.44 | async-start | bytes 5767168 | tf_op jit(solution)/shard_map/while/body/eval_jaxpr/psum | solution.py:70
  1234.0 150.0 %reduce-scatter.33.cloned.1.call-start = ((), (), s32[]{:S(2)}) async-start(), calls=%async_computation.47 | async-start | bytes 1216512 | tf_op jit(solution)/shard_map/while/body/eval_jaxpr/reduce_scatter | solution.py:362
  1238.5 422.3 %all-reduce.59.cloned.1.call-start = ((), (), s32[]{:S(2)}) async-start(), calls=%async_computation.40 | async-start | bytes 17301504 | tf_op jit(solution)/shard_map/while
  1314.1 424.8 %reduce-scatter.19.cloned.1.call-start = ((), (), s32[]{:S(2)}) async-start(), calls=%async_computation.38 | async-start | bytes 4595712 | tf_op jit(solution)/shard_map/while/body/eval_jaxpr/reduce_scatter | solution.py:450
  1318.4 497.1 %reduce-scatter.23.cloned.1.call-start = ((), (), s32[]{:S(2)}) async-start(), calls=%async_computation.41 | async-start | bytes 4595712 | tf_op jit(solution)/shard_map/while/body/eval_jaxpr/reduce_scatter | solution.py:452
  1322.4 570.2 %reduce-scatter.17.cloned.1.call-start = ((), (), s32[]{:S(2)}) async-start(), calls=%async_computation.37 | async-start | bytes 4595712 | tf_op jit(solution)/shard_map/while/body/eval_jaxpr/reduce_scatter | solution.py:449
  1326.7 671.7 %reduce-scatter.31.cloned.1.call-start = ((), (), s32[]{:S(2)}) async-start(), calls=%async_computation.46 | async-start | bytes 8425472 | tf_op jit(solution)/shard_map/while
  1333.4 806.6 %reduce-scatter.15.cloned.1.call-start = ((), (), s32[]{:S(2)}) async-start(), calls=%async_computation.36 | async-start | bytes 13787136 | tf_op jit(solution)/shard_map/while/body/eval_jaxpr/reduce_scatter | solution.py:448
  1342.0 983.4 %reduce-scatter.25.cloned.1.call-start = ((), (), s32[]{:S(2)}) async-start(), calls=%async_computation.42 | async-start | bytes 18382848 | tf_op jit(solution)/shard_map/while/body/eval_jaxpr/reduce_scatter | solution.py:453
  1353.3 1157.2 %reduce-scatter.27.cloned.1.call-start = ((), (), s32[]{:S(2)}) async-start(), calls=%async_computation.43 | async-start | bytes 18382848 | tf_op jit(solution)/shard_map/while/body/eval_jaxpr/reduce_scatter | solution.py:454
  1364.0 1323.5 %reduce-scatter.29.cloned.1.call-start = ((), (), s32[]{:S(2)}) async-start(), calls=%async_computation.45 | async-start | bytes 16850944 | tf_op jit(solution)/shard_map/while/body/eval_jaxpr/reduce_scatter | solution.py:455
  2690.9 190.6 %all-gather.24.cloned.1.call-start = ((), (), s32[]{:S(2)}) async-start(), calls=%async_computation.24 | async-start | bytes 8921088 | tf_op jit(solution)/shard_map/while/body/eval_jaxpr/all_gather | solution.py:231
  2691.5 344.3 %all-gather.26.cloned.1.call-start = ((), (), s32[]{:S(2)}) async-start(), calls=%async_computation.25 | async-start | bytes 10813440 | tf_op jit(solution)/shard_map/while/body/eval_jaxpr/all_gather | solution.py:222
  2692.3 408.7 %all-gather.28.cloned.1.call-start = ((), (), s32[]{:S(2)}) async-start(), calls=%async_computation.26 | async-start | bytes 2703360 | tf_op jit(solution)/shard_map/while/body/eval_jaxpr/all_gather | solution.py:223
  2693.0 473.0 %all-gather.32.cloned.1.call-start = ((), (), s32[]{:S(2)}) async-start(), calls=%async_computation.29 | async-start | bytes 5406720 | tf_op jit(solution)/shard_map/while/body/eval_jaxpr/all_gather | solution.py:225
  3071.1 145.0 %all-reduce.51.cloned.1.call-start = ((), (), s32[]{:S(2)}) async-start(), calls=%async_computation.28 | async-start | bytes 2883584 | tf_op jit(solution)/shard_map/while/body/eval_jaxpr/psum | solution.py:66
  3104.7 159.8 %all-gather.30.cloned.1.call-start = ((), (), s32[]{:S(2)}) async-start(), calls=%async_computation.27 | async-start | bytes 2703360 | tf_op jit(solution)/shard_map/while/body/eval_jaxpr/all_gather | solution.py:224
  3105.4 206.0 %all-gather.36.cloned.1.call-start = ((), (), s32[]{:S(2)}) async-start(), calls=%async_computation.31 | async-start | bytes 2703360 | tf_op jit(solution)/shard_map/while/body/eval_jaxpr/all_gather | solution.py:226
  3106.0 256.7 %all-reduce.53.cloned.1.call-start = ((), (), s32[]{:S(2)}) async-start(), calls=%async_computation.32 | async-start | bytes 2883584 | tf_op jit(solution)/shard_map/while/body/eval_jaxpr/psum | solution.py:66
  3315.1 203.1 %all-gather.34.cloned.1.call-start = ((), (), s32[]{:S(2)}) async-start(), calls=%async_computation.30 | async-start | bytes 10813440 | tf_op jit(solution)/shard_map/while/body/eval_jaxpr/all_gather | solution.py:227
  3315.9 355.9 %all-gather.38.cloned.1.call-start = ((), (), s32[]{:S(2)}) async-start(), calls=%async_computation.33 | async-start | bytes 10813440 | tf_op jit(solution)/shard_map/while/body/eval_jaxpr/all_gather | solution.py:228
  3316.4 416.7 %all-reduce.55.cloned.1.call-start = ((), (), s32[]{:S(2)}) async-start(), calls=%async_computation.34 | async-start | bytes 2883584 | tf_op jit(solution)/shard_map/while/body/eval_jaxpr/psum | solution.py:70
  3686.1 113.1 %all-reduce.57.cloned.1.call-start = ((), (), s32[]{:S(2)}) async-start(), calls=%async_computation.35 | async-start | bytes 2883584 | tf_op jit(solution)/shard_map/while/body/eval_jaxpr/psum | solution.py:70
  3876.9 114.2 %all-reduce.61.cloned.1.call-start = ((), (), s32[]{:S(2)}) async-start(), calls=%async_computation.44 | async-start | bytes 5767168 | tf_op jit(solution)/shard_map/while/body/eval_jaxpr/psum | solution.py:70
  3898.3 150.0 %reduce-scatter.33.cloned.1.call-start = ((), (), s32[]{:S(2)}) async-start(), calls=%async_computation.47 | async-start | bytes 1216512 | tf_op jit(solution)/shard_map/while/body/eval_jaxpr/reduce_scatter | solution.py:362
  3902.8 422.3 %all-reduce.59.cloned.1.call-start = ((), (), s32[]{:S(2)}) async-start(), calls=%async_computation.40 | async-start | bytes 17301504 | tf_op jit(solution)/shard_map/while
  3978.4 424.7 %reduce-scatter.19.cloned.1.call-start = ((), (), s32[]{:S(2)}) async-start(), calls=%async_computation.38 | async-start | bytes 4595712 | tf_op jit(solution)/shard_map/while/body/eval_jaxpr/reduce_scatter | solution.py:450
  3982.8 497.1 %reduce-scatter.23.cloned.1.call-start = ((), (), s32[]{:S(2)}) async-start(), calls=%async_computation.41 | async-start | bytes 4595712 | tf_op jit(solution)/shard_map/while/body/eval_jaxpr/reduce_scatter | solution.py:452
  3986.8 570.2 %reduce-scatter.17.cloned.1.call-start = ((), (), s32[]{:S(2)}) async-start(), calls=%async_computation.37 | async-start | bytes 4595712 | tf_op jit(solution)/shard_map/while/body/eval_jaxpr/reduce_scatter | solution.py:449
  3991.1 671.6 %reduce-scatter.31.cloned.1.call-start = ((), (), s32[]{:S(2)}) async-start(), calls=%async_computation.46 | async-start | bytes 8425472 | tf_op jit(solution)/shard_map/while
  3997.8 806.4 %reduce-scatter.15.cloned.1.call-start = ((), (), s32[]{:S(2)}) async-start(), calls=%async_computation.36 | async-start | bytes 13787136 | tf_op jit(solution)/shard_map/while/body/eval_jaxpr/reduce_scatter | solution.py:448
  4006.3 983.0 %reduce-scatter.25.cloned.1.call-start = ((), (), s32[]{:S(2)}) async-start(), calls=%async_computation.42 | async-start | bytes 18382848 | tf_op jit(solution)/shard_map/while/body/eval_jaxpr/reduce_scatter | solution.py:453
  4017.6 1156.7 %reduce-scatter.27.cloned.1.call-start = ((), (), s32[]{:S(2)}) async-start(), calls=%async_computation.43 | async-start | bytes 18382848 | tf_op jit(solution)/shard_map/while/body/eval_jaxpr/reduce_scatter | solution.py:454
  4028.3 1323.5 %reduce-scatter.29.cloned.1.call-start = ((), (), s32[]{:S(2)}) async-start(), calls=%async_computation.45 | async-start | bytes 16850944 | tf_op jit(solution)/shard_map/while/body/eval_jaxpr/reduce_scatter | solution.py:455
  5362.9 97.4 %all-gather.20.cloned.1.call-start = ((), (), s32[]{:S(2)}) async-start(), calls=%async_computation.21 | async-start | bytes 2703360 | tf_op jit(solution)/shard_map/all_gather | solution.py:486
  5363.8 149.2 %all-reduce.49.cloned.1.call-start = ((), (), s32[]{:S(2)}) async-start(), calls=%async_computation.22 | async-start | bytes 327680 | tf_op jit(solution)/shard_map/psum | solution.py:504
  (520 other events, 24949.2 us)
Sparse Core Ops, SparseCore 0:
  24.9 72.6 all-gather.21
  99.9 117.3 all-gather.23
  219.4 152.0 all-gather.25
  372.9 44.9 all-gather.27
  419.9 81.6 all-gather.31
  504.3 47.1 all-reduce.50
  553.1 46.7 all-gather.29
  601.4 45.5 all-gather.35
  650.8 47.4 all-reduce.52
  699.7 153.8 all-gather.33
  855.2 152.0 all-gather.37
  1021.8 46.8 all-reduce.54
  1086.1 48.6 all-reduce.56
  1234.1 79.2 all-reduce.60
  1356.2 304.5 all-reduce.58
  1665.0 73.8 reduce-scatter.18
  1742.8 72.6 reduce-scatter.22
  1819.8 72.7 reduce-scatter.16
  1896.6 101.7 reduce-scatter.30
  2002.5 137.4 reduce-scatter.14
  2144.2 181.1 reduce-scatter.24
  2329.4 181.0 reduce-scatter.26
  2514.5 172.9 reduce-scatter.28
  2693.0 68.9 all-gather.21
  2764.1 117.3 all-gather.23
  2883.7 152.0 all-gather.25
  3037.4 44.9 all-gather.27
  3084.3 81.6 all-gather.31
  3168.9 47.1 all-reduce.50
  3217.7 46.7 all-gather.29
  3265.8 45.5 all-gather.35
  3315.2 47.4 all-reduce.52
  3364.3 153.8 all-gather.33
  3519.6 152.0 all-gather.37
  3686.3 46.8 all-reduce.54
  3750.5 48.6 all-reduce.56
  3898.4 79.2 all-reduce.60
  3981.0 36.1 reduce-scatter.32
  4020.9 304.1 all-reduce.58
  4329.4 73.7 reduce-scatter.18
  4407.0 72.8 reduce-scatter.22
  4484.1 72.8 reduce-scatter.16
  4560.9 101.7 reduce-scatter.30
  4666.6 137.4 reduce-scatter.14
  4808.1 181.1 reduce-scatter.24
  4993.3 180.9 reduce-scatter.26
  5178.3 173.4 reduce-scatter.28
  5371.9 141.0 all-reduce.48
  (3 shorter events, 86.9 us)
Sparse Core Ops, SparseCore 1:
  5361.2 22.9 all-gather.15
  5386.2 23.7 all-gather.13
  5412.0 23.9 all-gather.17
  5437.5 22.8 all-gather.19
where the time goes:
time: 5550 us; the launch traced here: 5530 us
  waiting for transfers between devices  4540 us (82%)
  matrix products  320 us (6%)
  local copies, waits for them, and re-layouts  312 us (6%)
  other arithmetic  183 us (3%)
  blocking collectives  94.7 us (2%)
    while x54, waiting for transfers between devices  748 us
    reduce_scatter x2, waiting for transfers between devices, micro_step(): lax.psum_scatter(up_grad, ('shard', 'context'), scatter_dimension=0, tile...  368 us
    reduce_scatter x2, waiting for transfers between devices, micro_step(): lax.psum_scatter(down_grad, ('shard', 'context'), scatter_dimension=1, ti...  367 us
    reduce_scatter x2, waiting for transfers between devices, micro_step(): lax.psum_scatter(skip_grad, ('shard', 'context'), scatter_dimension=1, ti...  351 us
    all_gather x2, waiting for transfers between devices, micro_step(): lax.all_gather(up_weight, 'shard', axis=0, tiled=True)  304 us
    all_gather x2, waiting for transfers between devices, micro_step(): lax.all_gather(triple_weight, 'shard', axis=0, tiled=True)  291 us
    all_gather x2, waiting for transfers between devices, micro_step(): lax.all_gather(down_weight, 'shard', axis=1, tiled=True)  291 us
    reduce_scatter x2, waiting for transfers between devices, micro_step(): lax.psum_scatter(triple_w_grad, ('shard', 'context'), scatter_dimension=0...  281 us
  transfers between devices with their start and end apart: 67, of which 57 were waited for; matrix products, arithmetic and copies ran while one was open for 11% of the time, Pallas kernels for 0%

commit v1 on v0

v1 whole, which is shorter than its diff:
```python
import math

import jax
import jax.numpy as jnp
from jax import lax
from jax.sharding import PartitionSpec as P

epsilon = 1e-06
BF = jnp.bfloat16
F32 = jnp.float32


def matmul(left_side, right_side):
    return jnp.dot(left_side, right_side, preferred_element_type=F32)


def contract(form, left_side, right_side):
    return jnp.einsum(form, left_side, right_side, preferred_element_type=F32)


def contract_rows(left_side, right_side):
    return lax.dot_general(left_side, right_side, (((0,), (0,)), ((), ())), preferred_element_type=F32)


def contract_cols(left_side, right_side):
    return lax.dot_general(left_side, right_side, (((1,), (1,)), ((), ())), preferred_element_type=F32)


def layer_norm(values, scale_vec, offset):
    center = values - jnp.mean(values, -1, keepdims=True)
    spread = jnp.mean(center * center, -1, keepdims=True)
    return center * lax.rsqrt(spread + epsilon) * scale_vec + offset


def rotary_tables(grid_rows, head_size):
    quarter = head_size // 4
    frequencies = 1.0 / 10000.0 ** (jnp.arange(quarter, dtype=F32) * 2.0 / (head_size // 2))
    row_angle = grid_rows[:, 0:1].astype(F32) * frequencies
    col_angle = grid_rows[:, 1:2].astype(F32) * frequencies
    angles = jnp.concatenate([row_angle, row_angle, col_angle, col_angle], 1)
    return (jnp.cos(angles)[:, None, :], jnp.sin(angles)[:, None, :])


def rotate(values, cosine, sine_rows):
    quarter = values.shape[-1] // 4
    one = values[..., :quarter]
    two = values[..., quarter : 2 * quarter]
    three = values[..., 2 * quarter : 3 * quarter]
    four = values[..., 3 * quarter :]
    turned = jnp.concatenate([-two, one, -four, three], -1)
    return values * cosine + turned * sine_rows


def time_silu(stamps, model_width):
    half_width = model_width // 2
    frequencies = jnp.exp(-math.log(10000.0) * jnp.arange(half_width, dtype=F32) / half_width)
    angles = stamps.astype(F32)[:, None] * frequencies
    return jax.nn.silu(jnp.concatenate([jnp.cos(angles), jnp.sin(angles)], 1)).astype(BF)


def attention_forward(queries, key_rows, value_rows):
    score_scale = queries.shape[-1] ** (-0.5)
    scores = contract("qhd,khd->hqk", queries, key_rows) * score_scale
    row_max = jnp.max(scores, -1, keepdims=True)
    exponent = jnp.exp(scores - row_max)
    weight_sum = jnp.sum(exponent, -1, keepdims=True)
    weights_low = (exponent / weight_sum).astype(BF)
    mixture = contract("hqk,khd->qhd", weights_low, value_rows)
    return (mixture.astype(BF), (row_max + jnp.log(weight_sum))[..., 0])


def attention_backward(queries, key_rows, value_rows, log_sums, grad_mix):
    score_scale = queries.shape[-1] ** (-0.5)
    scores = contract("qhd,khd->hqk", queries, key_rows) * score_scale
    weights_full = jnp.exp(scores - log_sums[..., None])
    grad_weights = contract("qhd,khd->hqk", grad_mix, value_rows)
    inner = jnp.sum(weights_full * grad_weights, -1, keepdims=True)
    grad_scores = (weights_full * (grad_weights - inner)).astype(BF)
    query_grad = contract("hqk,khd->qhd", grad_scores, key_rows) * score_scale
    key_grad = contract("hqk,qhd->khd", grad_scores, queries) * score_scale
    value_grad = contract("hqk,qhd->khd", weights_full.astype(BF), grad_mix)
    return (query_grad, key_grad, value_grad)


def on_device(
    tokens, skip_in, text_in, grid_pos, time_ids, cotangent,
    skip_weight, shift_weight, triple_weight, self_out_weight, cross_q_weight,
    cross_kv_weight, cross_out_weight, up_weight, down_weight,
    norm_gains, norm_biases, head_gains, head_biases, width_biases, column_biases, hidden_biases,
):
    batch, local_len, width = tokens.shape
    text_len = text_in.shape[1]
    head_size = head_gains.shape[1]
    z = lax.axis_index("shard")
    k = lax.axis_index("context")
    y = lax.axis_index("tensor")
    nz, nk, ny = lax.axis_size("shard"), lax.axis_size("context"), lax.axis_size("tensor")
    assert batch == ny == 2
    rows_z = triple_weight.shape[0]
    half_cols = triple_weight.shape[2]
    half_hidden = up_weight.shape[1]
    cb = half_cols // nk
    hb = half_hidden // nk
    eb = width // nk
    hh = cb // head_size
    heads = ny * hh
    length = local_len * nk
    sequences = batch * nz
    swap = [(0, 1), (1, 0)]

    def mine(values):
        return lax.dynamic_index_in_dim(values, y, 0, keepdims=False)

    def block(values, size, axis):
        return lax.dynamic_slice_in_dim(values, k * size, size, axis)

    def other(values):
        return lax.ppermute(values, "tensor", swap)

    def pair(values):
        return (values, other(values))

    def gather_rows(values):
        return lax.all_gather(values, "context", axis=0, tiled=True)

    def scatter_rows(values):
        return lax.psum_scatter(values.astype(BF), "context", scatter_dimension=0, tiled=True).astype(F32)

    def by_batch(own, theirs):
        first = jnp.where(y == 0, own, theirs)
        second = jnp.where(y == 0, theirs, own)
        return jnp.stack([first, second])

    def gather_first(values):
        return pair(lax.all_gather(values, "shard", axis=0, tiled=True))

    def gather_last(values):
        got = lax.all_gather(values, "shard", axis=0, tiled=False)
        return pair(jnp.transpose(got, (1, 0, 2)).reshape(values.shape[0], -1))

    skip_block = lax.all_gather(block(skip_weight, eb, 2), ("shard", "tensor"), axis=1, tiled=True).reshape(2 * width, eb)
    triple_full = gather_first(block(triple_weight, cb, 2).reshape(rows_z, 3 * cb))
    self_out_full = gather_last(block(self_out_weight, cb, 0))
    cross_q_full = gather_first(block(cross_q_weight, cb, 1))
    cross_kv_full = gather_first(block(cross_kv_weight, cb, 2).reshape(rows_z, 2 * cb))
    cross_out_full = gather_last(block(cross_out_weight, cb, 0))
    up_full = gather_first(block(up_weight, hb, 1))
    down_full = gather_last(block(down_weight, hb, 0))

    def own_columns(values, size, half):
        last = values.ndim - 1
        first = lax.dynamic_slice_in_dim(values, y * half + k * size, size, last)
        second = lax.dynamic_slice_in_dim(values, (1 - y) * half + k * size, size, last)
        return (first, second)

    tok_rows, skip_rows, cot_rows = mine(tokens), mine(skip_in), mine(cotangent)
    text_rows = mine(text_in)
    grid_all = gather_rows(mine(grid_pos))
    cosine, sine_rows = rotary_tables(grid_all, head_size)
    times = lax.all_gather(time_ids, "shard", axis=0, tiled=True)
    silu_all = time_silu(times, width)
    shift_rows_count = shift_weight.shape[0]
    silu_rows = lax.dynamic_slice_in_dim(silu_all, (z * ny + y) * shift_rows_count, shift_rows_count, 1)
    shift_row = lax.psum_scatter(matmul(silu_rows, shift_weight), ("shard", "tensor"), scatter_dimension=0, tiled=True)[0]
    shift_row = shift_row + width_biases[1]

    tok_all = gather_rows(jnp.concatenate([tok_rows, skip_rows], 1))
    summed_block = matmul(tok_all, skip_block)
    summed = lax.all_to_all(summed_block, "context", split_axis=0, concat_axis=1, tiled=True) + width_biases[0]

    def first_piece(summed_in, shift_in, gain_rows, bias_rows):
        resid_out = layer_norm(summed_in, gain_rows[0], bias_rows[0])
        return (resid_out, layer_norm(resid_out, gain_rows[1], bias_rows[1]) + shift_in)

    (resid_zero, normed_one), pull_first = jax.vjp(first_piece, summed, shift_row, norm_gains, norm_biases)
    normed_one_all = gather_rows(normed_one.astype(BF))
    triple_bias = own_columns(column_biases[0:3], cb, half_cols)

    def to_heads(parts, count):
        return jnp.concatenate([p.reshape(p.shape[0], count, hh, head_size) for p in parts], 2)

    def from_heads(values):
        rows, count = values.shape[0], values.shape[1]
        return (values[:, :, :hh].reshape(rows, count * cb), values[:, :, hh:].reshape(rows, count * cb))

    triple = to_heads([matmul(normed_one_all, w) + b.reshape(1, -1) for w, b in zip(triple_full, triple_bias)], 3)

    def self_piece(triple_in, gain_rows, bias_rows):
        queries = rotate(layer_norm(triple_in[:, 0], gain_rows[0], bias_rows[0]), cosine, sine_rows)
        key_rows = rotate(layer_norm(triple_in[:, 1], gain_rows[1], bias_rows[1]), cosine, sine_rows)
        return (queries, key_rows, triple_in[:, 2])

    (query, key, value), pull_self = jax.vjp(self_piece, triple, head_gains, head_biases)
    query, key, value = query.astype(BF), key.astype(BF), value.astype(BF)
    mix, self_sums = attention_forward(query, key, value)
    mix_parts = from_heads(mix[:, None])
    resid_one = resid_zero + (
        scatter_rows(matmul(mix_parts[0], self_out_full[0]) + matmul(mix_parts[1], self_out_full[1])) + width_biases[2]
    )

    def second_piece(resid_in, gain_rows, bias_rows):
        return layer_norm(resid_in, gain_rows[2], bias_rows[2])

    normed_two, pull_second = jax.vjp(second_piece, resid_one, norm_gains, norm_biases)
    normed_two_all = gather_rows(normed_two.astype(BF))
    cq_bias = own_columns(column_biases[3], cb, half_cols)
    kv_bias = own_columns(column_biases[4:6], cb, half_cols)
    cross_raw = to_heads([matmul(normed_two_all, w) + b.reshape(1, -1) for w, b in zip(cross_q_full, cq_bias)], 1)
    pair_raw = to_heads([matmul(text_rows, w) + b.reshape(1, -1) for w, b in zip(cross_kv_full, kv_bias)], 2)

    def cross_piece(query_in, pair_in, gain_rows, bias_rows):
        queries = rotate(layer_norm(query_in[:, 0], gain_rows[2], bias_rows[2]), cosine, sine_rows)
        key_rows = layer_norm(pair_in[:, 0], gain_rows[3], bias_rows[3])
        return (queries, key_rows, pair_in[:, 1])

    (cq, ck, cv), pull_cross = jax.vjp(cross_piece, cross_raw, pair_raw, head_gains, head_biases)
    cq, ck, cv = cq.astype(BF), ck.astype(BF), cv.astype(BF)
    cross_mix, cross_sums = attention_forward(cq, ck, cv)
    cross_parts = from_heads(cross_mix[:, None])
    resid_two = resid_one + (
        scatter_rows(matmul(cross_parts[0], cross_out_full[0]) + matmul(cross_parts[1], cross_out_full[1])) + width_biases[3]
    )

    def third_piece(resid_in, gain_rows, bias_rows):
        return layer_norm(resid_in, gain_rows[3], bias_rows[3])

    normed_three, pull_third = jax.vjp(third_piece, resid_two, norm_gains, norm_biases)
    normed_three_all = gather_rows(normed_three.astype(BF))
    hidden_bias = own_columns(hidden_biases, hb, half_hidden)

    def gelu_piece(hidden_in):
        return jax.nn.gelu(hidden_in, approximate=True)

    active, pull_gelu = [], []
    for w, b in zip(up_full, hidden_bias):
        act, pull = jax.vjp(gelu_piece, matmul(normed_three_all, w) + b)
        active.append(act.astype(BF))
        pull_gelu.append(pull)
    result = resid_two + (
        scatter_rows(matmul(active[0], down_full[0]) + matmul(active[1], down_full[1])) + width_biases[4]
    )
    result_low = result.astype(BF)
    result_out = by_batch(result_low, other(result_low)).astype(F32)

    def reduce_first(parts, scale_rows=None):
        total = parts[0] + other(parts[1].astype(BF)).astype(F32)
        return lax.psum_scatter(total.astype(BF), "shard", scatter_dimension=0, tiled=True)

    def reduce_last(parts):
        total = parts[0] + other(parts[1].astype(BF)).astype(F32)
        rows = total.shape[0]
        total = jnp.transpose(total.astype(BF).reshape(rows, nz, rows_z), (1, 0, 2))
        return lax.psum_scatter(total, "shard", scatter_dimension=0, tiled=True)[0]

    def spread(values):
        return lax.all_gather(values, "context", axis=0, tiled=False)

    def spread_last(values, count):
        got = spread(values).reshape(nk, values.shape[0], count, -1)
        got = jnp.transpose(got, (1, 2, 0, 3)).reshape(values.shape[0], count, -1)
        return got.astype(F32)

    cot_all = gather_rows(cot_rows)
    grad_out = cot_rows.astype(F32)
    down_grad = reduce_last([contract_rows(a, cot_all) for a in active])
    hidden_grad = [pull(contract_cols(cot_all, w))[0].astype(BF) for pull, w in zip(pull_gelu, down_full)]
    up_grad = reduce_first([contract_rows(normed_three_all, h) for h in hidden_grad])
    third_grads = pull_third(
        scatter_rows(contract_cols(hidden_grad[0], up_full[0]) + contract_cols(hidden_grad[1], up_full[1]))
    )
    resid_two_grad = grad_out + third_grads[0]
    grad_two_low = resid_two_grad.astype(BF)
    grad_two_all = gather_rows(grad_two_low)
    cross_out_grad = reduce_last([contract_rows(p, grad_two_all) for p in cross_parts])
    cross_mix_grad = to_heads([contract_cols(grad_two_all, w).astype(BF) for w in cross_out_full], 1)[:, 0]
    cq_back, ck_back, cv_back = attention_backward(cq, ck, cv, cross_sums, cross_mix_grad)
    cross_grads = pull_cross((cq_back, ck_back, cv_back))
    cross_grad_low = from_heads(cross_grads[0].astype(BF))
    pair_low = from_heads(cross_grads[1].astype(BF))
    cross_q_grad = reduce_first([contract_rows(normed_two_all, g) for g in cross_grad_low])
    cross_kv_grad = reduce_first([contract_rows(text_rows, g) for g in pair_low])
    text_part = contract_cols(pair_low[0], cross_kv_full[0]) + contract_cols(pair_low[1], cross_kv_full[1])
    text_part = lax.psum_scatter(text_part.astype(BF), "context", scatter_dimension=1, tiled=True)
    text_cols = text_part.shape[1] // ny
    text_mine = lax.dynamic_slice_in_dim(text_part, y * text_cols, text_cols, 1)
    text_theirs = other(lax.dynamic_slice_in_dim(text_part, (1 - y) * text_cols, text_cols, 1))
    text_grad = by_batch(text_mine, text_theirs).astype(F32)
    second_grads = pull_second(
        scatter_rows(contract_cols(cross_grad_low[0], cross_q_full[0]) + contract_cols(cross_grad_low[1], cross_q_full[1]))
    )
    resid_one_grad = resid_two_grad + second_grads[0]
    grad_one_low = resid_one_grad.astype(BF)
    grad_one_all = gather_rows(grad_one_low)
    self_out_grad = reduce_last([contract_rows(p, grad_one_all) for p in mix_parts])
    mix_grad = to_heads([contract_cols(grad_one_all, w).astype(BF) for w in self_out_full], 1)[:, 0]
    q_back, k_back, v_back = attention_backward(query, key, value, self_sums, mix_grad)
    self_grads = pull_self(
        (q_back.astype(BF).astype(F32), k_back.astype(BF).astype(F32), v_back.astype(BF).astype(F32))
    )
    triple_low = from_heads(self_grads[0].astype(BF))
    triple_grad = reduce_first([contract_rows(normed_one_all, g) for g in triple_low])
    first_grads = pull_first(
        (
            resid_one_grad,
            scatter_rows(contract_cols(triple_low[0], triple_full[0]) + contract_cols(triple_low[1], triple_full[1])),
        )
    )
    summed_low = first_grads[0].astype(BF)
    summed_cols = lax.all_to_all(summed_low, "context", split_axis=1, concat_axis=0, tiled=True)
    skip_part = contract_rows(tok_all, summed_cols).reshape(2, nz, ny, -1, eb)
    keep = lax.dynamic_index_in_dim(skip_part, y, 2, keepdims=False)
    give = lax.dynamic_index_in_dim(skip_part, 1 - y, 2, keepdims=False)
    skip_total = (keep + other(give.astype(BF)).astype(F32)).astype(BF)
    skip_grad = lax.psum_scatter(jnp.transpose(skip_total, (1, 0, 2, 3)), "shard", scatter_dimension=0, tiled=True)[0]
    skip_grad_out = jnp.transpose(spread(skip_grad), (1, 2, 0, 3)).reshape(2, -1, width).astype(F32)

    skip_all = jnp.transpose(spread(skip_block), (1, 0, 2)).reshape(2 * width, width)
    both_low = by_batch(summed_low, other(summed_low)).reshape(batch * local_len, width)
    both_grad = contract_cols(both_low, skip_all).reshape(batch, local_len, 2, width)

    def place(parts, size, half, total):
        out = jnp.zeros(parts[0].shape[:-1] + (total,), F32)
        at = out.ndim - 1
        out = lax.dynamic_update_slice_in_dim(out, parts[0], y * half + k * size, at)
        return lax.dynamic_update_slice_in_dim(out, parts[1], (1 - y) * half + k * size, at)

    def col_sums(values, count=1):
        return jnp.sum(values.astype(F32), 0).reshape(count, -1)

    gains_grad = first_grads[2] + second_grads[1] + third_grads[1]
    biases_grad = first_grads[3] + second_grads[2] + third_grads[2]
    head_gain_grad = self_grads[1] + cross_grads[2]
    head_bias_grad = self_grads[2] + cross_grads[3]
    width_grad = jnp.stack(
        [
            jnp.sum(summed_low.astype(F32), 0),
            first_grads[1],
            jnp.sum(grad_one_low.astype(F32), 0),
            jnp.sum(grad_two_low.astype(F32), 0),
            jnp.sum(grad_out, 0),
        ]
    )
    column_parts = [
        jnp.concatenate([col_sums(t, 3), col_sums(c, 1), col_sums(p, 2)], 0)
        for t, c, p in zip(triple_low, cross_grad_low, pair_low)
    ]
    column_grad = place(column_parts, cb, half_cols, width)
    hidden_grad_sum = place([col_sums(h)[0] for h in hidden_grad], hb, half_hidden, hidden_biases.shape[0])
    shift_slots = lax.dynamic_update_slice_in_dim(
        jnp.zeros((sequences, width), F32), first_grads[1][None], z * ny + y, 0
    )
    vectors = lax.psum(
        (gains_grad, biases_grad, head_gain_grad, head_bias_grad, width_grad, column_grad, hidden_grad_sum, shift_slots),
        ("shard", "context", "tensor"),
    )
    shift_grad_out = lax.dot_general(
        silu_rows.astype(F32), vectors[7], (((0,), (0,)), ((), ())), precision=lax.Precision.HIGHEST
    )

    def spread_rows(values):
        return lax.all_gather(values, "context", axis=0, tiled=True).astype(F32)

    return (
        result_out,
        both_grad[:, :, 0],
        both_grad[:, :, 1],
        text_grad,
        skip_grad_out,
        shift_grad_out,
        spread_last(triple_grad, 3),
        spread_rows(self_out_grad),
        spread_last(cross_q_grad, 1)[:, 0],
        spread_last(cross_kv_grad, 2),
        spread_rows(cross_out_grad),
        spread_last(up_grad, 1)[:, 0],
        spread_rows(down_grad),
    ) + tuple(vectors[:7])


def solution(mesh):
    placed = (
        P("shard", "context", None),
        P("shard", "context", None),
        P("shard", None, None),
        P("shard", "context", None),
        P("shard"),
        P("shard", "context", None),
        P(None, ("shard", "tensor"), None),
        P(("shard", "tensor"), None),
        P("shard", None, "tensor"),
        P("tensor", "shard"),
        P("shard", "tensor"),
        P("shard", None, "tensor"),
        P("tensor", "shard"),
        P("shard", "tensor"),
        P("tensor", "shard"),
    ) + (P(),) * 7
    return jax.shard_map(
        on_device,
        mesh=mesh,
        in_specs=placed,
        out_specs=(
            P("shard", "context", None),
            P("shard", "context", None),
            P("shard", "context", None),
            P("shard", None, ("context", "tensor")),
        )
        + placed[6:15]
        + (P(),) * 7,
        check_vma=False,
    )
```

time: 5550 us -> 1500 us (0.27)
  waiting for transfers between devices: 4540 us -> 737 us
  local copies, waits for them, and re-layouts: 312 us -> 201 us
  matrix products: 320 us -> 226 us
  other arithmetic: 183 us -> 102 us
  blocking collectives: 94.7 us -> 164 us
    reduce_scatter x18 -> x11, waiting for transfers between devices: 1820 us -> 161 us  [the longest x6 128 us: scatter_rows(): lax.psum_scatter(values.astype(BF), 'context', scatter_dimension=0, tiled...]
    all_gather x22 -> x15, waiting for transfers between devices: 1540 us -> 251 us  [the longest x7 119 us: gather_rows(): return lax.all_gather(values, 'context', axis=0, tiled=True)]
    while x54 -> x0, waiting for transfers between devices: 748 us -> none
    psum x11 -> x1, waiting for transfers between devices: 384 us -> 114 us  [on_device(): lax.psum((gains_grad, biases_grad, head_gain_grad, head_bias_grad, width_...]
    ppermute x0 -> x18, waiting for transfers between devices: none -> 156 us  [other(): return lax.ppermute(values, 'tensor', swap)]
    dynamic_update_slice x8 -> x5, local copies, waits for them, and re-layouts: 131 us -> 1.32 us  [the longest x2 0.62 us: place(): lax.dynamic_update_slice_in_dim(out, parts[1], (1 - y) * half + k * size,...]
    dot_general x66 -> x29, matrix products: 199 us -> 117 us  [the longest x12 58 us: contract(): return jnp.einsum(form, left_side, right_side, preferred_element_type=F32)]
    while x980 -> x0, local copies, waits for them, and re-layouts: 73.1 us -> none
  transfers between devices with their start and end apart: 67 -> 51, of which waited for: 57 -> 21; matrix products, arithmetic and copies ran while one was open for 11% -> 29% of each run, Pallas kernels for 0% -> 0%
where the time goes in v1:
time: 1500 us; the launch traced here: 1480 us
  waiting for transfers between devices  737 us (49%)
  matrix products  226 us (15%)
  local copies, waits for them, and re-layouts  201 us (13%)
  blocking collectives  164 us (11%)
  other arithmetic  102 us (7%)
  starting transfers between devices  32.4 us (2%)
  between operations  19.8 us (1%)
    ppermute x18, waiting for transfers between devices, other(): return lax.ppermute(values, 'tensor', swap)  156 us
    reduce_scatter x6, waiting for transfers between devices, scatter_rows(): lax.psum_scatter(values.astype(BF), 'context', scatter_dimension=0, tiled...  128 us
    all_gather x7, waiting for transfers between devices, gather_rows(): return lax.all_gather(values, 'context', axis=0, tiled=True)  119 us
    psum x1, waiting for transfers between devices, on_device(): lax.psum((gains_grad, biases_grad, head_gain_grad, head_bias_grad, width_...  114 us
    unnamed x441, local copies, waits for them, and re-layouts  63.9 us
    dot_general x15, matrix products, contract_cols(): lax.dot_general(left_side, right_side, (((1,), (1,)), ((), ())), preferre...  61.5 us
    dot_general x12, matrix products, contract(): return jnp.einsum(form, left_side, right_side, preferred_element_type=F32)  58 us
    dot_general x16, matrix products, matmul(): return jnp.dot(left_side, right_side, preferred_element_type=F32)  56.9 us
  transfers between devices with their start and end apart: 51, of which 21 were waited for; matrix products, arithmetic and copies ran while one was open for 29% of the time, Pallas kernels for 0%

profile of v1, /device:TPU:0, one launch (start us, length us, event | category | flops | bytes accessed | tf_op | source)
XLA Modules:
  0.0 1482.7 jit_solution(5748155056957155887)
XLA Ops:
  13.0 51.2 %all-gather.34.cloned.1.call-done = bf16[2,1408,352]{2,1,0:T(8,128)(2,1)} async-done(((bf16[2,176,352]{2,1,0:T(8,128)(2,1)}), bf16[2,1408,352]{2,1,0:T(8,128)(2,1)}) %all-gather.34.cloned.1.call-update) | async-done | bytes 1982480 | tf_op jit(solution)/shard_map/all_gather | solution.py:141
  64.2 44.1 %all-gather.32.cloned.1.call-done = bf16[1024,2816]{1,0:T(8,128)(2,1)} async-done(((bf16[256,2816]{1,0:T(8,128)(2,1)}), bf16[1024,2816]{1,0:T(8,128)(2,1)}) %all-gather.32.cloned.1.call-update) | async-done | bytes 5767184 | tf_op jit(solution)/shard_map/all_gather | solution.py:124
  108.3 6.7 fusion.163
  123.5 8.3 all-reduce.33
  133.4 37.7 %all-reduce.34 = f32[8,1408]{1,0:T(8,128)S(1)} all-reduce(f32[8,1408]{1,0:T(8,128)S(1)} %fusion.131), channel_id=14, replica_groups=mesh['shard'=4,'context'=4,'tensor'=2] {'shard','tensor'}, use_global_device_ids=true, to_apply=%region_4.5.clone | all-reduce | flops 11264 | bytes 90112
  187.8 14.7 all-gather.1
  226.0 25.2 %collective-permute-done = bf16[1408,528]{0,1:T(8,128)(2,1)} collective-permute-done((bf16[1408,528]{0,1:T(8,128)(2,1)}, bf16[1408,528]{0,1:T(8,128)(2,1)}, u32[]{:S(2)}, u32[]{:S(2)}) %collective-permute-start) | collective-permute-done | bytes 1486880 | tf_op jit(solution)/shard_map/ppermute | solution.py:118
  259.1 8.2 multiply_reduce_fusion.1
  267.4 8.5 fusion
  275.9 8.1 fusion.88
  288.9 35.0 %reduce-scatter.24.cloned.1.call-done = bf16[256,1408]{1,0:T(8,128)(2,1)} async-done(((bf16[1024,1408]{1,0:T(8,128)(2,1)}), bf16[256,1408]{1,0:T(8,128)(2,1)}) %reduce-scatter.24.cloned.1.call-update) | async-done | bytes 720912 | tf_op jit(solution)/shard_map/reduce_scatter | solution.py:127
  329.7 15.5 %all-gather.13 = bf16[4,352,176]{1,2,0:T(8,128)(2,1)S(1)} all-gather(bf16[1,352,176]{1,2,0:T(8,128)(2,1)S(1)} %bitcast.567), channel_id=1, replica_groups=mesh['shard'=4,'context'=4,'tensor'=2] {'shard'}, dimensions={0}, use_global_device_ids=true | all-gather | bytes 619520 | tf_op jit(solution)/shard_map/all_gather | solution.py:135
  350.7 21.0 %all_gather.107 = bf16[1408,352]{1,0:T(8,128)(2,1)S(1)} all-gather(bf16[352,352]{1,0:T(8,128)(2,1)S(1)} %copy.277), channel_id=1, replica_groups=mesh['shard'=4,'context'=4,'tensor'=2] {'shard'}, dimensions={0}, use_global_device_ids=true | all-gather | bytes 1239040 | tf_op jit(solution)/shard_map/all_gather | solution.py:135
  375.0 15.1 %all-gather.2 = bf16[704,352]{1,0:T(8,128)(2,1)S(1)} all-gather(bf16[176,352]{1,0:T(8,128)(2,1)S(1)} %constant_dynamic-slice_fusion.5), channel_id=4, replica_groups=mesh['shard'=4,'context'=4,'tensor'=2] {'shard'}, dimensions={0}, use_global_device_ids=true | all-gather | bytes 619520 | tf_op jit(solution)/shard_map/all_gather | solution.py:138
  431.2 32.0 %reduce-scatter.26.cloned.1.call-done = bf16[256,1408]{1,0:T(8,128)(2,1)} async-done(((bf16[1024,1408]{1,0:T(8,128)(2,1)}), bf16[256,1408]{1,0:T(8,128)(2,1)}) %reduce-scatter.26.cloned.1.call-update) | async-done | bytes 720912 | tf_op jit(solution)/shard_map/reduce_scatter | solution.py:127
  470.5 41.5 %all-gather.50.cloned.1.call-done = bf16[3072,352]{0,1:T(8,128)(2,1)} async-done(((bf16[768,352]{0,1:T(8,128)(2,1)}), bf16[3072,352]{0,1:T(8,128)(2,1)}) %all-gather.50.cloned.1.call-update) | async-done | bytes 2162704 | tf_op jit(solution)/shard_map/all_gather | solution.py:138
  521.3 38.4 %all-gather.42.cloned.1.call-done = bf16[1408,768]{1,0:T(8,128)(2,1)} async-done(((bf16[352,768]{1,0:T(8,128)(2,1)}), bf16[1408,768]{1,0:T(8,128)(2,1)}) %all-gather.42.cloned.1.call-update) | async-done | bytes 2162704 | tf_op jit(solution)/shard_map/all_gather | solution.py:135
  561.1 26.2 %all-gather.40.cloned.1.call-done = bf16[1024,1408]{1,0:T(8,128)(2,1)} async-done(((bf16[256,1408]{1,0:T(8,128)(2,1)}), bf16[1024,1408]{1,0:T(8,128)(2,1)}) %all-gather.40.cloned.1.call-update) | async-done | bytes 2883600 | tf_op jit(solution)/shard_map/all_gather | solution.py:124
  587.3 6.7 fusion.166
  594.1 22.2 %all-gather.52.cloned.1.call-done = bf16[1,1024,1408]{2,1,0:T(8,128)(2,1)} async-done(((bf16[1,256,1408]{2,1,0:T(8,128)(2,1)}), bf16[1,1024,1408]{2,1,0:T(8,128)(2,1)}) %all-gather.52.cloned.1.call-update) | async-done | bytes 2883600 | tf_op jit(solution)/shard_map/all_gather | solution.py:124
  616.3 8.3 convert_reduce_fusion.1
  631.7 7.7 convert_reduce_fusion
  640.5 6.0 add_convert_fusion.2
  652.3 6.0 add_convert_fusion.3
  658.3 24.6 %reduce-scatter.30.cloned.1.call-done = bf16[256,1408]{1,0:T(8,128)(2,1)} async-done(((bf16[1024,1408]{1,0:T(8,128)(2,1)}), bf16[256,1408]{1,0:T(8,128)(2,1)}) %reduce-scatter.30.cloned.1.call-update) | async-done | bytes 720912 | tf_op jit(solution)/shard_map/reduce_scatter | solution.py:127
  685.6 36.5 %reduce-scatter.28.cloned.1.call-done = bf16[256,1408]{1,0:T(8,128)(2,1)} async-done(((bf16[1024,1408]{1,0:T(8,128)(2,1)}), bf16[256,1408]{1,0:T(8,128)(2,1)}) %reduce-scatter.28.cloned.1.call-update) | async-done | bytes 720912 | tf_op jit(solution)/shard_map/reduce_scatter | solution.py:127
  727.6 26.9 %all-gather.44.cloned.1.call-done = bf16[1024,1408]{1,0:T(8,128)(2,1)} async-done(((bf16[256,1408]{1,0:T(8,128)(2,1)}), bf16[1024,1408]{1,0:T(8,128)(2,1)}) %all-gather.44.cloned.1.call-update) | async-done | bytes 2883600 | tf_op jit(solution)/shard_map/all_gather | solution.py:124
  784.4 47.7 %collective-permute-done.16 = bf16[1408,768]{1,0:T(8,128)(2,1)S(1)} collective-permute-done((bf16[1408,768]{1,0:T(8,128)(2,1)S(1)}, bf16[1408,768]{1,0:T(8,128)(2,1)S(1)}, u32[]{:S(2)}, u32[]{:S(2)}) %collective-permute-start.16) | collective-permute-done | bytes 2162720 | tf_op jit(solution)/shard_map/ppermute | solution.py:118
  844.1 46.8 %collective-permute-done.17 = bf16[768,1408]{1,0:T(8,128)(2,1)S(1)} collective-permute-done((bf16[768,1408]{1,0:T(8,128)(2,1)S(1)}, bf16[768,1408]{1,0:T(8,128)(2,1)S(1)}, u32[]{:S(2)}, u32[]{:S(2)}) %collective-permute-start.17) | collective-permute-done | bytes 2162720 | tf_op jit(solution)/shard_map/ppermute | solution.py:118
  911.0 32.8 %reduce-scatter.42.cloned.1.call-done = bf16[1,768,352]{1,2,0:T(8,128)(2,1)} async-done(((bf16[4,768,352]{1,2,0:T(8,128)(2,1)}), bf16[1,768,352]{1,2,0:T(8,128)(2,1)}) %reduce-scatter.42.cloned.1.call-update) | async-done | bytes 540688 | tf_op jit(solution)/shard_map/reduce_scatter | solution.py:253
  952.8 18.8 %collective-permute-done.13 = bf16[1408,176]{0,1:T(8,128)(2,1)S(1)} collective-permute-done((bf16[1408,176]{0,1:T(8,128)(2,1)S(1)}, bf16[1408,176]{0,1:T(8,128)(2,1)S(1)}, u32[]{:S(2)}, u32[]{:S(2)}) %collective-permute-start.13) | collective-permute-done | bytes 495648 | tf_op jit(solution)/shard_map/ppermute | solution.py:118
  991.2 8.6 copy.290
  999.8 16.1 %dot_general.226 = bf16[2,1408,1408]{1,0,2:T(2,128)(2,1)} reshape(bf16[2816,4,352]{0,2,1:T(8,128)(2,1)} %bitcast.514) | data formatting | bytes 15859712 | tf_op jit(solution)/shard_map/dot_general | solution.py:26
  1015.9 21.9 %copy.289 = bf16[2,1408,1408]{2,1,0:T(8,128)(2,1)} copy(bf16[2,1408,1408]{1,0,2:T(2,128)(2,1)} %dot_general.226) | data formatting | bytes 15859712 | tf_op jit(solution)/shard_map/dot_general | solution.py:26
  1053.8 14.2 multiply_reduce_fusion
  1070.5 8.0 multiply_convert_fusion
  1083.5 6.2 bitcast_multiply_fusion.2
  1097.1 7.7 fusion.84
  1140.8 7.8 all-gather.15
  1148.7 11.1 all-gather.9
  1172.3 9.9 all-gather.8
  1209.1 7.1 all-gather.6
  1231.6 15.6 %reduce-scatter.46.cloned.1.call-done = bf16[352,528]{1,0:T(8,128)(2,1)} async-done(((bf16[1408,528]{1,0:T(8,128)(2,1)}), bf16[352,528]{1,0:T(8,128)(2,1)}) %reduce-scatter.46.cloned.1.call-update) | async-done | bytes 371728
  1250.7 113.6 %all-reduce.42.cloned.1.call-done = (f32[8,1408]{1,0:T(8,128)}, f32[4,1408]{1,0:T(4,128)}, f32[4,1408]{1,0:T(4,128)}, f32[4,88]{1,0:T(4,128)}, f32[4,88]{1,0:T(4...) async-done(((f32[8,1408]{1,0:T(8,128)}, f32[4,1408]{1,0:T(4,128)}, f32[4,1408]{1,0:T(4,128)}, f32[4,88]{1,0:T(4,128)}, f32[4,88]{1,0:T(4,128)}, ...) | async-done | bytes 179472 | tf_op jit(solution)/shard_map/psum | solution.py:352
  1374.8 9.8 fusion.5
  1384.6 13.9 collective-permute-done.10
  1414.0 39.4 %all-reduce.40.cloned.1.call-done = bf16[4,2,176,352]{3,2,0,1:T(8,128)(2,1)} async-done(((bf16[4,2,176,352]{3,2,0,1:T(8,128)(2,1)}), bf16[4,2,176,352]{3,2,0,1:T(8,128)(2,1)}) %all-reduce.40.cloned.1.call-update) | async-done | bytes 991248
  1455.0 10.2 all_gather.120
  (825 shorter events, 413.4 us)
Async XLA Ops:
  8.0 56.2 %all-gather.34.cloned.1.call-start = ((), (), s32[]{:S(2)}) async-start(), calls=%async_computation.17 | async-start | bytes 2433024 | tf_op jit(solution)/shard_map/all_gather | solution.py:141
  10.1 98.2 %all-gather.32.cloned.1.call-start = ((), (), s32[]{:S(2)}) async-start(), calls=%async_computation.16 | async-start | bytes 7208960 | tf_op jit(solution)/shard_map/all_gather | solution.py:124
  115.0 58.4 %all-to-all-start = ((f32[4,256,352]{1,2,0:T(8,128)}), f32[4,256,352]{1,2,0:T(8,128)}, u32[]{:S(2)}, u32[]{:S(2)}) async-start(f32[4,256,352]{1,2,0:T(8,128)} %fusion.163), calls=%async_computation | async-start | bytes 2883584 | tf_op jit(solution)/shard_map/all_to_all | solution.py:169
  119.3 89.3 %all-gather.58.cloned.1.call-start = ((), (), s32[]{:S(2)}) async-start(), calls=%async_computation.39 | async-start | bytes 2027520 | tf_op jit(solution)/shard_map/all_gather | solution.py:135
  123.4 98.3 %all-gather.36.cloned.1.call-start = ((), (), s32[]{:S(2)}) async-start(), calls=%async_computation.18 | async-start | bytes 3604480 | tf_op jit(solution)/shard_map/all_gather | solution.py:124
  186.8 137.1 %reduce-scatter.24.cloned.1.call-start = ((), (), s32[]{:S(2)}) async-start(), calls=%async_computation.19 | async-start | bytes 3604480 | tf_op jit(solution)/shard_map/reduce_scatter | solution.py:127
  203.2 82.0 %collective-permute-start.1 = (bf16[176,1408]{1,0:T(8,128)(2,1)S(1)}, bf16[176,1408]{1,0:T(8,128)(2,1)}, u32[]{:S(2)}, u32[]{:S(2)}) collective-permute-start(bf16[176,1408]{1,0:T(8,128)(2,1)S(1)} %reshape.710), channel_id=1, source_target_pairs={{0,1},{1,0},{2,3},{3,2},{4,5},{5,4},{6,7},{7,6},{8,9},{9,8},{10,11... | collective-permute-start | bytes 1486856 | tf_op jit(solution)/shard_map/ppermute | solution.py:118
  215.9 35.4 %collective-permute-start = (bf16[1408,528]{0,1:T(8,128)(2,1)}, bf16[1408,528]{0,1:T(8,128)(2,1)}, u32[]{:S(2)}, u32[]{:S(2)}) collective-permute-start(bf16[1408,528]{0,1:T(8,128)(2,1)} %reshape.785), channel_id=1, source_target_pairs={{0,1},{1,0},{2,3},{3,2},{4,5},{5,4},{6,7},{7,6},{8,9},{9,8},{10,11... | collective-permute-start | bytes 4460552 | tf_op jit(solution)/shard_map/ppermute | solution.py:118
  288.9 120.0 %all-gather.38.cloned.1.call-start = ((), (), s32[]{:S(2)}) async-start(), calls=%async_computation.20 | async-start | bytes 3604480 | tf_op jit(solution)/shard_map/all_gather | solution.py:124
  328.4 134.8 %reduce-scatter.26.cloned.1.call-start = ((), (), s32[]{:S(2)}) async-start(), calls=%async_computation.21 | async-start | bytes 3604480 | tf_op jit(solution)/shard_map/reduce_scatter | solution.py:127
  346.6 65.4 %collective-permute-start.3 = (bf16[1408,176]{0,1:T(8,128)(2,1)}, bf16[1408,176]{0,1:T(8,128)(2,1)}, u32[]{:S(2)}, u32[]{:S(2)}) collective-permute-start(bf16[1408,176]{0,1:T(8,128)(2,1)} %reshape.787), channel_id=1, source_target_pairs={{0,1},{1,0},{2,3},{3,2},{4,5},{5,4},{6,7},{7,6},{8,9},{9,8},{10,11... | collective-permute-start | bytes 1486856 | tf_op jit(solution)/shard_map/ppermute | solution.py:118
  373.6 30.1 %collective-permute-start.2 = (bf16[1408,352]{0,1:T(8,128)(2,1)}, bf16[1408,352]{0,1:T(8,128)(2,1)}, u32[]{:S(2)}, u32[]{:S(2)}) collective-permute-start(bf16[1408,352]{0,1:T(8,128)(2,1)} %copy.279), channel_id=1, source_target_pairs={{0,1},{1,0},{2,3},{3,2},{4,5},{5,4},{6,7},{7,6},{8,9},{9,8},{10,11... | collective-permute-start | bytes 2973704 | tf_op jit(solution)/shard_map/ppermute | solution.py:118
  393.4 30.8 %collective-permute-start.4 = (bf16[176,1408]{1,0:T(8,128)(2,1)}, bf16[176,1408]{1,0:T(8,128)(2,1)}, u32[]{:S(2)}, u32[]{:S(2)}) collective-permute-start(bf16[176,1408]{1,0:T(8,128)(2,1)} %reshape.718), channel_id=1, source_target_pairs={{0,1},{1,0},{2,3},{3,2},{4,5},{5,4},{6,7},{7,6},{8,9},{9,8},{10,11... | collective-permute-start | bytes 1486856 | tf_op jit(solution)/shard_map/ppermute | solution.py:118
  428.2 83.9 %all-gather.50.cloned.1.call-start = ((), (), s32[]{:S(2)}) async-start(), calls=%async_computation.35 | async-start | bytes 2703360 | tf_op jit(solution)/shard_map/all_gather | solution.py:138
  429.1 130.5 %all-gather.42.cloned.1.call-start = ((), (), s32[]{:S(2)}) async-start(), calls=%async_computation.23 | async-start | bytes 2703360 | tf_op jit(solution)/shard_map/all_gather | solution.py:135
  431.2 156.1 %all-gather.40.cloned.1.call-start = ((), (), s32[]{:S(2)}) async-start(), calls=%async_computation.22 | async-start | bytes 3604480 | tf_op jit(solution)/shard_map/all_gather | solution.py:124
  466.9 149.3 %all-gather.52.cloned.1.call-start = ((), (), s32[]{:S(2)}) async-start(), calls=%async_computation.36 | async-start | bytes 3604480 | tf_op jit(solution)/shard_map/all_gather | solution.py:124
  469.7 213.2 %reduce-scatter.30.cloned.1.call-start = ((), (), s32[]{:S(2)}) async-start(), calls=%async_computation.25 | async-start | bytes 3604480 | tf_op jit(solution)/shard_map/reduce_scatter | solution.py:127
  519.8 111.8 %collective-permute-start.6 = (bf16[768,1408]{0,1:T(8,128)(2,1)}, bf16[768,1408]{0,1:T(8,128)(2,1)}, u32[]{:S(2)}, u32[]{:S(2)}) collective-permute-start(bf16[768,1408]{0,1:T(8,128)(2,1)} %bitcast.52), channel_id=1, source_target_pairs={{0,1},{1,0},{2,3},{3,2},{4,5},{5,4},{6,7},{7,6},{8,9},{9,8},{10,11... | collective-permute-start | bytes 6488072 | tf_op jit(solution)/shard_map/ppermute | solution.py:118
  559.6 67.6 %collective-permute-start.5 = (bf16[1408,768]{1,0:T(8,128)(2,1)}, bf16[1408,768]{1,0:T(8,128)(2,1)}, u32[]{:S(2)}, u32[]{:S(2)}) collective-permute-start(bf16[1408,768]{1,0:T(8,128)(2,1)} %all-gather.42.cloned.1.call-done), channel_id=1, source_target_pairs={{0,1},{1,0},{2,3},{3,2},{4,5},{5,4},{6,7},{7,6},{8,9},{9,8},{10,11... | collective-permute-start | bytes 6488072 | tf_op jit(solution)/shard_map/ppermute | solution.py:118
  646.5 75.5 %reduce-scatter.28.cloned.1.call-start = ((), (), s32[]{:S(2)}) async-start(), calls=%async_computation.24 | async-start | bytes 3604480 | tf_op jit(solution)/shard_map/reduce_scatter | solution.py:127
  658.2 96.2 %all-gather.44.cloned.1.call-start = ((), (), s32[]{:S(2)}) async-start(), calls=%async_computation.26 | async-start | bytes 3604480 | tf_op jit(solution)/shard_map/all_gather | solution.py:124
  727.3 176.0 %reduce-scatter.32.cloned.1.call-start = ((), (), s32[]{:S(2)}) async-start(), calls=%async_computation.27 | async-start | bytes 3604480 | tf_op jit(solution)/shard_map/reduce_scatter | solution.py:127
  777.7 133.3 %reduce-scatter.40.cloned.1.call-start = ((), (), s32[]{:S(2)}) async-start(), calls=%async_computation.33 | async-start | bytes 2703360 | tf_op jit(solution)/shard_map/reduce_scatter | solution.py:247
  782.9 49.2 %collective-permute-start.16 = (bf16[1408,768]{1,0:T(8,128)(2,1)S(1)}, bf16[1408,768]{1,0:T(8,128)(2,1)S(1)}, u32[]{:S(2)}, u32[]{:S(2)}) collective-permute-start(bf16[1408,768]{1,0:T(8,128)(2,1)S(1)} %convolution_convert_fusion.1), channel_id=1, source_target_pairs={{0,1},{1,0},{2,3},{3,2},{4,5},{5,4},{6,7},{7,6},{8,9},{9,8},{10,11... | collective-permute-start | bytes 6488072 | tf_op jit(solution)/shard_map/ppermute | solution.py:118
  836.1 107.8 %reduce-scatter.42.cloned.1.call-start = ((), (), s32[]{:S(2)}) async-start(), calls=%async_computation.34 | async-start | bytes 2703360 | tf_op jit(solution)/shard_map/reduce_scatter | solution.py:253
  842.5 48.4 %collective-permute-start.17 = (bf16[768,1408]{1,0:T(8,128)(2,1)S(1)}, bf16[768,1408]{1,0:T(8,128)(2,1)S(1)}, u32[]{:S(2)}, u32[]{:S(2)}) collective-permute-start(bf16[768,1408]{1,0:T(8,128)(2,1)S(1)} %convolution_convert_fusion), channel_id=1, source_target_pairs={{0,1},{1,0},{2,3},{3,2},{4,5},{5,4},{6,7},{7,6},{8,9},{9,8},{10,11... | collective-permute-start | bytes 6488072 | tf_op jit(solution)/shard_map/ppermute | solution.py:118
  899.1 100.7 %all-gather.48.cloned.1.call-start = ((), (), s32[]{:S(2)}) async-start(), calls=%async_computation.30 | async-start | bytes 9912320 | tf_op jit(solution)/shard_map/all_gather | solution.py:256
  903.3 141.9 %all-gather.46.cloned.1.call-start = ((), (), s32[]{:S(2)}) async-start(), calls=%async_computation.28 | async-start | bytes 3604480 | tf_op jit(solution)/shard_map/all_gather | solution.py:124
  910.4 214.2 %all-gather.54.cloned.1.call-start = ((), (), s32[]{:S(2)}) async-start(), calls=%async_computation.37 | async-start | bytes 2703360 | tf_op jit(solution)/shard_map/all_gather | solution.py:256
  911.0 221.3 %all-gather.56.cloned.1.call-start = ((), (), s32[]{:S(2)}) async-start(), calls=%async_computation.38 | async-start | bytes 2703360 | tf_op jit(solution)/shard_map/all_gather | solution.py:361
  943.9 195.8 %reduce-scatter.48.cloned.1.call-start = ((), (), s32[]{:S(2)}) async-start(), calls=%async_computation.43 | async-start | bytes 901120
  948.1 30.3 %collective-permute-start.15 = (bf16[176,1408]{1,0:T(8,128)(2,1)}, bf16[176,1408]{1,0:T(8,128)(2,1)}, u32[]{:S(2)}, u32[]{:S(2)}) collective-permute-start(bf16[176,1408]{1,0:T(8,128)(2,1)} %convolution_convert_fusion.5), channel_id=1, source_target_pairs={{0,1},{1,0},{2,3},{3,2},{4,5},{5,4},{6,7},{7,6},{8,9},{9,8},{10,11... | collective-permute-start | bytes 1486856 | tf_op jit(solution)/shard_map/ppermute | solution.py:118
  973.5 175.1 %reduce-scatter.38.cloned.1.call-start = ((), (), s32[]{:S(2)}) async-start(), calls=%async_computation.32 | async-start | bytes 675840 | tf_op jit(solution)/shard_map/reduce_scatter | solution.py:253
  981.9 179.0 %reduce-scatter.44.cloned.1.call-start = ((), (), s32[]{:S(2)}) async-start(), calls=%async_computation.41 | async-start | bytes 1351680
  987.4 184.8 %reduce-scatter.50.cloned.1.call-start = ((), (), s32[]{:S(2)}) async-start(), calls=%async_computation.44 | async-start | bytes 1351680 | tf_op jit(solution)/shard_map/reduce_scatter | solution.py:247
  989.2 52.4 %collective-permute-start.14 = (bf16[1408,352]{0,1:T(8,128)(2,1)}, bf16[1408,352]{0,1:T(8,128)(2,1)}, u32[]{:S(2)}, u32[]{:S(2)}) collective-permute-start(bf16[1408,352]{0,1:T(8,128)(2,1)} %convolution_convert_fusion.3), channel_id=1, source_target_pairs={{0,1},{1,0},{2,3},{3,2},{4,5},{5,4},{6,7},{7,6},{8,9},{9,8},{10,11... | collective-permute-start | bytes 2973704 | tf_op jit(solution)/shard_map/ppermute | solution.py:118
  1040.1 81.2 %collective-permute-start.7 = (bf16[256,1408]{1,0:T(8,128)(2,1)}, bf16[256,1408]{1,0:T(8,128)(2,1)}, u32[]{:S(2)}, u32[]{:S(2)}) collective-permute-start(bf16[256,1408]{1,0:T(8,128)(2,1)} %get-tuple-element.283), channel_id=1, source_target_pairs={{0,1},{1,0},{2,3},{3,2},{4,5},{5,4},{6,7},{7,6},{8,9},{9,8},{10,11... | collective-permute-start | bytes 2162696 | tf_op jit(solution)/shard_map/ppermute | solution.py:118
  1044.9 164.1 %reduce-scatter.36.cloned.1.call-start = ((), (), s32[]{:S(2)}) async-start(), calls=%async_computation.31 | async-start | bytes 675840 | tf_op jit(solution)/shard_map/reduce_scatter | solution.py:253
  1048.8 58.3 %collective-permute-start.12 = (bf16[176,1408]{1,0:T(8,128)(2,1)}, bf16[176,1408]{1,0:T(8,128)(2,1)}, u32[]{:S(2)}, u32[]{:S(2)}) collective-permute-start(bf16[176,1408]{1,0:T(8,128)(2,1)} %convolution_convert_fusion.6), channel_id=1, source_target_pairs={{0,1},{1,0},{2,3},{3,2},{4,5},{5,4},{6,7},{7,6},{8,9},{9,8},{10,11... | collective-permute-start | bytes 1486856 | tf_op jit(solution)/shard_map/ppermute | solution.py:118
  1111.4 104.7 %reduce-scatter.34.cloned.1.call-start = ((), (), s32[]{:S(2)}) async-start(), calls=%async_computation.29 | async-start | bytes 3604480 | tf_op jit(solution)/shard_map/reduce_scatter | solution.py:127
  1121.3 125.9 %reduce-scatter.46.cloned.1.call-start = ((), (), s32[]{:S(2)}) async-start(), calls=%async_computation.42 | async-start | bytes 2252800
  1167.5 35.1 %collective-permute-start.11 = (bf16[1408,528]{0,1:T(8,128)(2,1)}, bf16[1408,528]{0,1:T(8,128)(2,1)}, u32[]{:S(2)}, u32[]{:S(2)}) collective-permute-start(bf16[1408,528]{0,1:T(8,128)(2,1)} %convolution_convert_fusion.2), channel_id=1, source_target_pairs={{0,1},{1,0},{2,3},{3,2},{4,5},{5,4},{6,7},{7,6},{8,9},{9,8},{10,11... | collective-permute-start | bytes 4460552 | tf_op jit(solution)/shard_map/ppermute | solution.py:118
  1224.5 142.2 %all-to-all-start.1 = ((bf16[256,4,352]{0,2,1:T(8,128)(2,1)}), bf16[256,4,352]{0,2,1:T(8,128)(2,1)S(1)}, u32[]{:S(2)}, u32[]{:S(2)}) async-start(bf16[256,4,352]{0,2,1:T(8,128)(2,1)} %bitcast.94), calls=%async_computation.7 | async-start | bytes 1441792 | tf_op jit(solution)/shard_map/all_to_all | solution.py:309
  1228.0 136.3 %all-reduce.42.cloned.1.call-start = ((), (), s32[]{:S(2)}) async-start(), calls=%async_computation.46 | async-start | bytes 417792 | tf_op jit(solution)/shard_map/psum | solution.py:352
  1230.3 175.1 %all-gather.60.cloned.1.call-start = ((), (), s32[]{:S(2)}) async-start(), calls=%async_computation.40 | async-start | bytes 2027520 | tf_op jit(solution)/shard_map/all_gather | solution.py:256
  1249.1 204.3 %all-reduce.40.cloned.1.call-start = ((), (), s32[]{:S(2)}) async-start(), calls=%async_computation.45 | async-start | bytes 2162688
  1249.2 125.5 %collective-permute-start.8 = (bf16[256,1408]{1,0:T(8,128)(2,1)S(1)}, bf16[256,1408]{1,0:T(8,128)(2,1)S(1)}, u32[]{:S(2)}, u32[]{:S(2)}) collective-permute-start(bf16[256,1408]{1,0:T(8,128)(2,1)S(1)} %get-tuple-element.242), channel_id=1, source_target_pairs={{0,1},{1,0},{2,3},{3,2},{4,5},{5,4},{6,7},{7,6},{8,9},{9,8},{10,11... | collective-permute-start | bytes 2162696 | tf_op jit(solution)/shard_map/ppermute | solution.py:118
  (210 other events, 3369.9 us)
Sparse Core Ops, SparseCore 0:
  11.7 52.4 all-gather.33
  66.3 41.9 all-gather.31
  328.5 27.0 all-gather.37
  646.7 36.1 reduce-scatter.29
  685.8 36.1 reduce-scatter.27
  727.4 27.0 all-gather.43
  777.8 36.1 reduce-scatter.31
  836.2 44.6 reduce-scatter.39
  899.2 44.6 reduce-scatter.41
  973.7 22.5 reduce-scatter.47
  998.6 20.9 reduce-scatter.37
  1022.6 23.3 reduce-scatter.43
  1048.9 27.8 reduce-scatter.49
  1111.6 20.6 reduce-scatter.35
  1135.2 37.2 reduce-scatter.33
  1209.1 37.9 reduce-scatter.45
Sparse Core Ops, SparseCore 1:
  123.5 40.2 all-gather.57
  186.9 24.3 all-gather.35
  289.0 34.9 reduce-scatter.23
  428.3 34.9 reduce-scatter.25
  465.4 46.6 all-gather.49
  514.2 45.4 all-gather.41
  561.6 25.6 all-gather.39
  589.3 26.9 all-gather.51
  903.3 55.5 all-gather.47
  961.0 26.9 all-gather.45
  989.4 22.8 all-gather.53
  1013.8 22.8 all-gather.55
  1236.7 127.6 all-reduce.41
  1366.5 20.9 all-gather.59
  1399.9 53.5 all-reduce.39

commit v2 on v1

--- a/solution.py
+++ b/solution.py
@@ -120,32 +120,72 @@
     def pair(values):
         return (values, other(values))
 
+    bits = [1 << i for i in range(nk.bit_length() - 1)]
+    relative = jnp.arange(nk) ^ k
+
+    def flip(values, axis_name, bit):
+        count = lax.axis_size(axis_name)
+        return lax.ppermute(values, axis_name, [(i, i ^ bit) for i in range(count)])
+
     def gather_rows(values):
-        return lax.all_gather(values, "context", axis=0, tiled=True)
-
-    def scatter_rows(values):
-        return lax.psum_scatter(values.astype(BF), "context", scatter_dimension=0, tiled=True).astype(F32)
+        for bit in reversed(bits):
+            values = jnp.concatenate([values, flip(values, "context", bit)], 0)
+        return values
+
+    order = [sum(((p >> j) & 1) << (len(bits) - 1 - j) for j in range(len(bits))) for p in range(nk)]
+
+    def ranked(values, axis=0, back=False):
+        where = (jnp.asarray(order) ^ k) if back else jnp.asarray(order)[relative]
+        return jnp.take(values, where, axis=axis, indices_are_sorted=False, unique_indices=True)
+
+    def scatter_rows(pieces):
+        half = pieces[0][0].shape[0] // 2
+
+        def part(first):
+            total = None
+            for left, right, form in pieces:
+                now = form(left[:half] if first else left[half:], right)
+                total = now if total is None else total + now
+            return total
+
+        sent = flip(part(False).astype(BF), "context", bits[0])
+        total = part(True) + sent.astype(F32)
+        for bit in bits[1:]:
+            half = total.shape[0] // 2
+            total = total[:half] + flip(total[half:].astype(BF), "context", bit).astype(F32)
+        return total
 
     def by_batch(own, theirs):
         first = jnp.where(y == 0, own, theirs)
         second = jnp.where(y == 0, theirs, own)
         return jnp.stack([first, second])
 
-    def gather_first(values):
-        return pair(lax.all_gather(values, "shard", axis=0, tiled=True))
-
-    def gather_last(values):
-        got = lax.all_gather(values, "shard", axis=0, tiled=False)
-        return pair(jnp.transpose(got, (1, 0, 2)).reshape(values.shape[0], -1))
-
-    skip_block = lax.all_gather(block(skip_weight, eb, 2), ("shard", "tensor"), axis=1, tiled=True).reshape(2 * width, eb)
-    triple_full = gather_first(block(triple_weight, cb, 2).reshape(rows_z, 3 * cb))
-    self_out_full = gather_last(block(self_out_weight, cb, 0))
-    cross_q_full = gather_first(block(cross_q_weight, cb, 1))
-    cross_kv_full = gather_first(block(cross_kv_weight, cb, 2).reshape(rows_z, 2 * cb))
-    cross_out_full = gather_last(block(cross_out_weight, cb, 0))
-    up_full = gather_first(block(up_weight, hb, 1))
-    down_full = gather_last(block(down_weight, hb, 0))
+    def gathered(values):
+        return lax.all_gather(values, "shard", axis=0, tiled=True)
+
+    pin = lax.optimization_barrier
+    first_part = jnp.concatenate(
+        [
+            block(skip_weight, eb, 2).reshape(-1, eb),
+            block(triple_weight, cb, 2).reshape(rows_z, 3 * cb),
+            block(self_out_weight, cb, 0).T,
+        ],
+        1,
+    )
+    second_part = jnp.concatenate(
+        [
+            block(cross_q_weight, cb, 1),
+            block(cross_kv_weight, cb, 2).reshape(rows_z, 2 * cb),
+            block(cross_out_weight, cb, 0).T,
+        ],
+        1,
+    )
+    first_z = gathered(first_part)
+    second_z = gathered(second_part)
+    up_z = gathered(block(up_weight, hb, 1))
+    down_z = gathered(block(down_weight, hb, 0).T)
+    skip_z = first_z[:, :eb].reshape(nz, 2, -1, eb)
+    skip_block = jnp.transpose(by_batch(skip_z, other(skip_z)), (2, 1, 0, 3, 4)).reshape(2 * width, eb)
 
     def own_columns(values, size, half):
         last = values.ndim - 1
@@ -157,16 +197,24 @@
     text_rows = mine(text_in)
     grid_all = gather_rows(mine(grid_pos))
     cosine, sine_rows = rotary_tables(grid_all, head_size)
-    times = lax.all_gather(time_ids, "shard", axis=0, tiled=True)
+    times = lax.all_to_all(jnp.broadcast_to(time_ids, (nz, batch)), "shard", 0, 0, tiled=True).reshape(-1)
     silu_all = time_silu(times, width)
     shift_rows_count = shift_weight.shape[0]
     silu_rows = lax.dynamic_slice_in_dim(silu_all, (z * ny + y) * shift_rows_count, shift_rows_count, 1)
-    shift_row = lax.psum_scatter(matmul(silu_rows, shift_weight), ("shard", "tensor"), scatter_dimension=0, tiled=True)[0]
-    shift_row = shift_row + width_biases[1]
+    shift_part = matmul(silu_rows, shift_weight).reshape(nz, ny, width)
+    shift_mine = lax.dynamic_index_in_dim(shift_part, y, 1, keepdims=False)
+    shift_give = lax.dynamic_index_in_dim(shift_part, 1 - y, 1, keepdims=False)
+    shift_part = shift_mine + other(shift_give)
+    shift_row = jnp.sum(lax.all_to_all(shift_part, "shard", 0, 0, tiled=True), 0) + width_biases[1]
 
     tok_all = gather_rows(jnp.concatenate([tok_rows, skip_rows], 1))
-    summed_block = matmul(tok_all, skip_block)
-    summed = lax.all_to_all(summed_block, "context", split_axis=0, concat_axis=1, tiled=True) + width_biases[0]
+    summed_block = ranked(matmul(tok_all, skip_block).astype(BF).reshape(nk, local_len, eb)).reshape(length, eb)
+    summed = lax.all_to_all(summed_block, "context", split_axis=0, concat_axis=1, tiled=True).astype(F32) + width_biases[0]
+
+    summed, first_z = pin((summed, first_z[:, eb:]))
+    first_pair = pair(first_z)
+    triple_full = [w[:, : 3 * cb] for w in first_pair]
+    self_out_full = [w[:, 3 * cb :] for w in first_pair]
 
     def first_piece(summed_in, shift_in, gain_rows, bias_rows):
         resid_out = layer_norm(summed_in, gain_rows[0], bias_rows[0])
@@ -192,11 +240,19 @@
 
     (query, key, value), pull_self = jax.vjp(self_piece, triple, head_gains, head_biases)
     query, key, value = query.astype(BF), key.astype(BF), value.astype(BF)
+    query, key, value, second_z = pin((query, key, value, second_z))
+    second_pair = pair(second_z)
+    cross_q_full = [w[:, :cb] for w in second_pair]
+    cross_kv_full = [w[:, cb : 3 * cb] for w in second_pair]
+    cross_out_full = [w[:, 3 * cb :] for w in second_pair]
     mix, self_sums = attention_forward(query, key, value)
     mix_parts = from_heads(mix[:, None])
     resid_one = resid_zero + (
-        scatter_rows(matmul(mix_parts[0], self_out_full[0]) + matmul(mix_parts[1], self_out_full[1])) + width_biases[2]
-    )
+        scatter_rows([(mix_parts[0], self_out_full[0], contract_cols), (mix_parts[1], self_out_full[1], contract_cols)]) + width_biases[2]
+    )
+
+    resid_one, up_z = pin((resid_one, up_z))
+    up_full = pair(up_z)
 
     def second_piece(resid_in, gain_rows, bias_rows):
         return layer_norm(resid_in, gain_rows[2], bias_rows[2])
@@ -215,10 +271,12 @@
 
     (cq, ck, cv), pull_cross = jax.vjp(cross_piece, cross_raw, pair_raw, head_gains, head_biases)
     cq, ck, cv = cq.astype(BF), ck.astype(BF), cv.astype(BF)
+    cq, ck, cv, down_z = pin((cq, ck, cv, down_z))
+    down_full = pair(down_z)
     cross_mix, cross_sums = attention_forward(cq, ck, cv)
     cross_parts = from_heads(cross_mix[:, None])
     resid_two = resid_one + (
-        scatter_rows(matmul(cross_parts[0], cross_out_full[0]) + matmul(cross_parts[1], cross_out_full[1])) + width_biases[3]
+        scatter_rows([(cross_parts[0], cross_out_full[0], contract_cols), (cross_parts[1], cross_out_full[1], contract_cols)]) + width_biases[3]
     )
 
     def third_piece(resid_in, gain_rows, bias_rows):
@@ -237,48 +295,44 @@
         active.append(act.astype(BF))
         pull_gelu.append(pull)
     result = resid_two + (
-        scatter_rows(matmul(active[0], down_full[0]) + matmul(active[1], down_full[1])) + width_biases[4]
+        scatter_rows([(active[0], down_full[0], contract_cols), (active[1], down_full[1], contract_cols)]) + width_biases[4]
     )
     result_low = result.astype(BF)
     result_out = by_batch(result_low, other(result_low)).astype(F32)
 
-    def reduce_first(parts, scale_rows=None):
-        total = parts[0] + other(parts[1].astype(BF)).astype(F32)
+    def reduced(own, theirs):
+        total = own + other(theirs.astype(BF)).astype(F32)
         return lax.psum_scatter(total.astype(BF), "shard", scatter_dimension=0, tiled=True)
 
-    def reduce_last(parts):
-        total = parts[0] + other(parts[1].astype(BF)).astype(F32)
-        rows = total.shape[0]
-        total = jnp.transpose(total.astype(BF).reshape(rows, nz, rows_z), (1, 0, 2))
-        return lax.psum_scatter(total, "shard", scatter_dimension=0, tiled=True)[0]
-
     def spread(values):
-        return lax.all_gather(values, "context", axis=0, tiled=False)
-
-    def spread_last(values, count):
-        got = spread(values).reshape(nk, values.shape[0], count, -1)
-        got = jnp.transpose(got, (1, 2, 0, 3)).reshape(values.shape[0], count, -1)
-        return got.astype(F32)
+        return ranked(gather_rows(values[None]))
+
+    def columns_out(values, count):
+        got = values.reshape(nk, values.shape[1], count, -1)
+        return jnp.transpose(got, (1, 2, 0, 3)).reshape(values.shape[1], count, -1).astype(F32)
+
+    def rows_out(values):
+        return jnp.transpose(values, (0, 2, 1)).reshape(-1, values.shape[1]).astype(F32)
 
     cot_all = gather_rows(cot_rows)
     grad_out = cot_rows.astype(F32)
-    down_grad = reduce_last([contract_rows(a, cot_all) for a in active])
-    hidden_grad = [pull(contract_cols(cot_all, w))[0].astype(BF) for pull, w in zip(pull_gelu, down_full)]
-    up_grad = reduce_first([contract_rows(normed_three_all, h) for h in hidden_grad])
+    down_grad = spread(reduced(*[contract_rows(cot_all, a) for a in active]))
+    hidden_grad = [pull(matmul(cot_all, w))[0].astype(BF) for pull, w in zip(pull_gelu, down_full)]
+    up_grad = spread(reduced(*[contract_rows(normed_three_all, h) for h in hidden_grad]))
     third_grads = pull_third(
-        scatter_rows(contract_cols(hidden_grad[0], up_full[0]) + contract_cols(hidden_grad[1], up_full[1]))
+        scatter_rows([(hidden_grad[0], up_full[0], contract_cols), (hidden_grad[1], up_full[1], contract_cols)])
     )
     resid_two_grad = grad_out + third_grads[0]
     grad_two_low = resid_two_grad.astype(BF)
     grad_two_all = gather_rows(grad_two_low)
-    cross_out_grad = reduce_last([contract_rows(p, grad_two_all) for p in cross_parts])
-    cross_mix_grad = to_heads([contract_cols(grad_two_all, w).astype(BF) for w in cross_out_full], 1)[:, 0]
+    cross_out_grad = [contract_rows(grad_two_all, p) for p in cross_parts]
+    cross_mix_grad = to_heads([matmul(grad_two_all, w).astype(BF) for w in cross_out_full], 1)[:, 0]
     cq_back, ck_back, cv_back = attention_backward(cq, ck, cv, cross_sums, cross_mix_grad)
     cross_grads = pull_cross((cq_back, ck_back, cv_back))
     cross_grad_low = from_heads(cross_grads[0].astype(BF))
     pair_low = from_heads(cross_grads[1].astype(BF))
-    cross_q_grad = reduce_first([contract_rows(normed_two_all, g) for g in cross_grad_low])
-    cross_kv_grad = reduce_first([contract_rows(text_rows, g) for g in pair_low])
+    cross_q_grad = [contract_rows(normed_two_all, g) for g in cross_grad_low]
+    cross_kv_grad = [contract_rows(text_rows, g) for g in pair_low]
     text_part = contract_cols(pair_low[0], cross_kv_full[0]) + contract_cols(pair_low[1], cross_kv_full[1])
     text_part = lax.psum_scatter(text_part.astype(BF), "context", scatter_dimension=1, tiled=True)
     text_cols = text_part.shape[1] // ny
@@ -286,43 +340,60 @@
     text_theirs = other(lax.dynamic_slice_in_dim(text_part, (1 - y) * text_cols, text_cols, 1))
     text_grad = by_batch(text_mine, text_theirs).astype(F32)
     second_grads = pull_second(
-        scatter_rows(contract_cols(cross_grad_low[0], cross_q_full[0]) + contract_cols(cross_grad_low[1], cross_q_full[1]))
+        scatter_rows([(cross_grad_low[0], cross_q_full[0], contract_cols), (cross_grad_low[1], cross_q_full[1], contract_cols)])
     )
     resid_one_grad = resid_two_grad + second_grads[0]
     grad_one_low = resid_one_grad.astype(BF)
     grad_one_all = gather_rows(grad_one_low)
-    self_out_grad = reduce_last([contract_rows(p, grad_one_all) for p in mix_parts])
-    mix_grad = to_heads([contract_cols(grad_one_all, w).astype(BF) for w in self_out_full], 1)[:, 0]
+    self_out_grad = [contract_rows(grad_one_all, p) for p in mix_parts]
+    small_grad = [jnp.concatenate(g, 1) for g in zip(cross_q_grad, cross_kv_grad, cross_out_grad, self_out_grad)]
+    small_grad = spread(reduced(*small_grad))
+    mix_grad = to_heads([matmul(grad_one_all, w).astype(BF) for w in self_out_full], 1)[:, 0]
     q_back, k_back, v_back = attention_backward(query, key, value, self_sums, mix_grad)
     self_grads = pull_self(
         (q_back.astype(BF).astype(F32), k_back.astype(BF).astype(F32), v_back.astype(BF).astype(F32))
     )
     triple_low = from_heads(self_grads[0].astype(BF))
-    triple_grad = reduce_first([contract_rows(normed_one_all, g) for g in triple_low])
+    triple_grad = spread(reduced(*[contract_rows(normed_one_all, g) for g in triple_low]))
     first_grads = pull_first(
         (
             resid_one_grad,
-            scatter_rows(contract_cols(triple_low[0], triple_full[0]) + contract_cols(triple_low[1], triple_full[1])),
+            scatter_rows([(triple_low[0], triple_full[0], contract_cols), (triple_low[1], triple_full[1], contract_cols)]),
         )
     )
     summed_low = first_grads[0].astype(BF)
     summed_cols = lax.all_to_all(summed_low, "context", split_axis=1, concat_axis=0, tiled=True)
+    summed_cols = ranked(summed_cols.reshape(nk, local_len, eb), 0, True).reshape(length, eb)
     skip_part = contract_rows(tok_all, summed_cols).reshape(2, nz, ny, -1, eb)
     keep = lax.dynamic_index_in_dim(skip_part, y, 2, keepdims=False)
     give = lax.dynamic_index_in_dim(skip_part, 1 - y, 2, keepdims=False)
     skip_total = (keep + other(give.astype(BF)).astype(F32)).astype(BF)
-    skip_grad = lax.psum_scatter(jnp.transpose(skip_total, (1, 0, 2, 3)), "shard", scatter_dimension=0, tiled=True)[0]
-    skip_grad_out = jnp.transpose(spread(skip_grad), (1, 2, 0, 3)).reshape(2, -1, width).astype(F32)
-
-    skip_all = jnp.transpose(spread(skip_block), (1, 0, 2)).reshape(2 * width, width)
-    both_low = by_batch(summed_low, other(summed_low)).reshape(batch * local_len, width)
-    both_grad = contract_cols(both_low, skip_all).reshape(batch, local_len, 2, width)
+    skip_total = jnp.transpose(skip_total, (1, 0, 2, 3)).reshape(-1, eb)
+    skip_grad = lax.psum_scatter(skip_total, "shard", scatter_dimension=0, tiled=True)
+    skip_grad_out = jnp.transpose(spread(skip_grad), (1, 0, 2)).reshape(2, -1, width).astype(F32)
+
+    skip_all = gather_rows(skip_block[None])
+    both_low = by_batch(summed_low, other(summed_low)).reshape(batch * local_len, nk, eb)
+    both_grad = contract("tke,kde->td", ranked(both_low, 1, True), skip_all).reshape(batch, local_len, 2, width)
 
     def place(parts, size, half, total):
         out = jnp.zeros(parts[0].shape[:-1] + (total,), F32)
         at = out.ndim - 1
         out = lax.dynamic_update_slice_in_dim(out, parts[0], y * half + k * size, at)
         return lax.dynamic_update_slice_in_dim(out, parts[1], (1 - y) * half + k * size, at)
+
+    def everywhere(parts):
+        flat = jnp.concatenate([p.reshape(-1) for p in parts])
+        size = flat.shape[0]
+        flat = jnp.pad(flat, (0, -size % 1024)).reshape(-1, 128)
+        for axis_name in ("context", "tensor", "shard"):
+            for i in range(lax.axis_size(axis_name).bit_length() - 1):
+                flat = flat + flip(flat, axis_name, 1 << i)
+        flat, out, at = flat.reshape(-1), [], 0
+        for p in parts:
+            out.append(flat[at : at + p.size].reshape(p.shape))
+            at += p.size
+        return out
 
     def col_sums(values, count=1):
         return jnp.sum(values.astype(F32), 0).reshape(count, -1)
@@ -349,16 +420,12 @@
     shift_slots = lax.dynamic_update_slice_in_dim(
         jnp.zeros((sequences, width), F32), first_grads[1][None], z * ny + y, 0
     )
-    vectors = lax.psum(
-        (gains_grad, biases_grad, head_gain_grad, head_bias_grad, width_grad, column_grad, hidden_grad_sum, shift_slots),
-        ("shard", "context", "tensor"),
+    vectors = everywhere(
+        (gains_grad, biases_grad, head_gain_grad, head_bias_grad, width_grad, column_grad, hidden_grad_sum, shift_slots)
     )
     shift_grad_out = lax.dot_general(
         silu_rows.astype(F32), vectors[7], (((0,), (0,)), ((), ())), precision=lax.Precision.HIGHEST
     )
-
-    def spread_rows(values):
-        return lax.all_gather(values, "context", axis=0, tiled=True).astype(F32)
 
     return (
         result_out,
@@ -367,13 +434,13 @@
         text_grad,
         skip_grad_out,
         shift_grad_out,
-        spread_last(triple_grad, 3),
-        spread_rows(self_out_grad),
-        spread_last(cross_q_grad, 1)[:, 0],
-        spread_last(cross_kv_grad, 2),
-        spread_rows(cross_out_grad),
-        spread_last(up_grad, 1)[:, 0],
-        spread_rows(down_grad),
+        columns_out(triple_grad, 3),
+        rows_out(small_grad[:, :, 4 * cb :]),
+        columns_out(small_grad[:, :, :cb], 1)[:, 0],
+        columns_out(small_grad[:, :, cb : 3 * cb], 2),
+        rows_out(small_grad[:, :, 3 * cb : 4 * cb]),
+        columns_out(up_grad, 1)[:, 0],
+        rows_out(down_grad),
     ) + tuple(vectors[:7])
 
 

time: 1500 us -> 1080 us (0.72)
  waiting for transfers between devices: 737 us -> 345 us
  blocking collectives: 164 us -> 0 us
  other arithmetic: 102 us -> 165 us
  starting transfers between devices: 32.4 us -> 77.7 us
  matrix products: 226 us -> 246 us
    all_gather x15 -> x4, waiting for transfers between devices: 251 us -> 29.2 us  [gathered(): return lax.all_gather(values, 'shard', axis=0, tiled=True)]
    ppermute x0 -> x45, waiting for transfers between devices: none -> 189 us  [flip(): return lax.ppermute(values, axis_name, [(i, i ^ bit) for i in range(count)])]
    reduce_scatter x11 -> x4, waiting for transfers between devices: 161 us -> 0.01 us  [the longest x3 0.01 us: reduced(): lax.psum_scatter(total.astype(BF), 'shard', scatter_dimension=0, tiled=True)]
    all_gather x10 -> x0, blocking collectives: 118 us -> none  [the longest x2 36.6 us: gather_first(): return pair(lax.all_gather(values, 'shard', axis=0, tiled=True))]
    psum x1 -> x0, waiting for transfers between devices: 114 us -> none  [on_device(): lax.psum((gains_grad, biases_grad, head_gain_grad, head_bias_grad, width_...]
    unnamed x35 -> x12, waiting for transfers between devices: 55.6 us -> 0.17 us
    unnamed x2 -> x0, blocking collectives: 46 us -> none
    concatenate x0 -> x23, other arithmetic: none -> 44.4 us  [the longest x20 40.7 us: gather_rows(): values = jnp.concatenate([values, flip(values, 'context', bit)], 0)]
  transfers between devices with their start and end apart: 51 -> 73, of which waited for: 21 -> 29; matrix products, arithmetic and copies ran while one was open for 29% -> 52% of each run, Pallas kernels for 0% -> 0%
where the time goes in v2:
time: 1080 us; the launch traced here: 1060 us
  waiting for transfers between devices  345 us (32%)
  matrix products  246 us (23%)
  local copies, waits for them, and re-layouts  209 us (19%)
  other arithmetic  165 us (15%)
  starting transfers between devices  77.7 us (7%)
  between operations  17.9 us (2%)
    ppermute x45, waiting for transfers between devices, flip(): return lax.ppermute(values, axis_name, [(i, i ^ bit) for i in range(count)])  189 us
    ppermute x14, waiting for transfers between devices, other(): return lax.ppermute(values, 'tensor', swap)  125 us
    dot_general x13, matrix products, contract(): return jnp.einsum(form, left_side, right_side, preferred_element_type=F32)  63.8 us
    dot_general x16, matrix products, matmul(): return jnp.dot(left_side, right_side, preferred_element_type=F32)  61 us
    dot_general x15, matrix products, contract_rows(): lax.dot_general(left_side, right_side, (((0,), (0,)), ((), ())), preferre...  60.5 us
    dot_general x26, matrix products, contract_cols(): lax.dot_general(left_side, right_side, (((1,), (1,)), ((), ())), preferre...  59.1 us
    unnamed x432, local copies, waits for them, and re-layouts  56.2 us
    concatenate x20, other arithmetic, gather_rows(): values = jnp.concatenate([values, flip(values, 'context', bit)], 0)  40.7 us
  transfers between devices with their start and end apart: 73, of which 29 were waited for; matrix products, arithmetic and copies ran while one was open for 52% of the time, Pallas kernels for 0%

profile of v2, /device:TPU:0, one launch (start us, length us, event | category | flops | bytes accessed | tf_op | source)
XLA Modules:
  0.0 1061.3 jit_solution(13375010995258321884)
XLA Ops:
  23.3 4.9 all-to-all-start.1
  28.2 26.3 %collective-permute-done = bf16[256,2816]{1,0:T(8,128)(2,1)} collective-permute-done((bf16[256,2816]{1,0:T(8,128)(2,1)}, bf16[256,2816]{1,0:T(8,128)(2,1)}, u32[]{:S(2)}, u32[]{:S(2)}) %collective-permute-start) | collective-permute-done | bytes 1441824 | tf_op jit(solution)/shard_map/ppermute | solution.py:128
  61.6 21.5 %all-gather.5.cloned.1.call-done = bf16[1408,1056]{1,0:T(8,128)(2,1)} async-done(((bf16[352,1056]{1,0:T(8,128)(2,1)}), bf16[1408,1056]{1,0:T(8,128)(2,1)}) %all-gather.5.cloned.1.call-update) | async-done | bytes 2973712 | tf_op jit(solution)/shard_map/all_gather | solution.py:164
  91.9 19.6 %collective-permute-done.3 = f32[4,1408]{1,0:T(4,128)S(1)} collective-permute-done((f32[4,1408]{1,0:T(4,128)}, f32[4,1408]{1,0:T(4,128)S(1)}, u32[]{:S(2)}, u32[]{:S(2)}) %collective-permute-start.3) | collective-permute-done | bytes 22560 | tf_op jit(solution)/shard_map/ppermute | solution.py:118
  162.7 8.8 collective-permute-done.4
  183.3 22.2 %collective-permute-done.6 = bf16[1408,704]{0,1:T(8,128)(2,1)} collective-permute-done((bf16[1408,704]{0,1:T(8,128)(2,1)}, bf16[1408,704]{0,1:T(8,128)(2,1)}, u32[]{:S(2)}, u32[]{:S(2)}) %collective-permute-start.6) | collective-permute-done | bytes 1982496 | tf_op jit(solution)/shard_map/ppermute | solution.py:118
  214.7 8.2 multiply_reduce_fusion.1
  222.9 8.6 fusion
  231.5 7.8 fusion.94
  255.8 11.2 %collective-permute-done.10 = bf16[256,1408]{1,0:T(8,128)(2,1)S(1)} collective-permute-done((bf16[256,1408]{1,0:T(8,128)(2,1)S(1)}, bf16[256,1408]{1,0:T(8,128)(2,1)S(1)}, u32[]{:S(2)}, u32[]{:S(2)}) %collective-permute-start.10) | collective-permute-done | bytes 720928 | tf_op jit(solution)/shard_map/ppermute | solution.py:128
  275.8 8.8 reduce-scatter.15.cloned.1.call-start
  315.4 7.7 all-gather.11.cloned.1.call-done
  347.9 10.8 %collective-permute-done.15 = bf16[256,1408]{1,0:T(8,128)(2,1)} collective-permute-done((bf16[256,1408]{1,0:T(8,128)(2,1)}, bf16[256,1408]{1,0:T(8,128)(2,1)}, u32[]{:S(2)}, u32[]{:S(2)}) %collective-permute-start.15) | collective-permute-done | bytes 720928 | tf_op jit(solution)/shard_map/ppermute | solution.py:128
  370.0 61.2 %collective-permute-done.16 = bf16[256,1408]{1,0:T(8,128)(2,1)} collective-permute-done((bf16[256,1408]{1,0:T(8,128)(2,1)}, bf16[256,1408]{1,0:T(8,128)(2,1)}, u32[]{:S(2)}, u32[]{:S(2)}) %collective-permute-start.16) | collective-permute-done | bytes 720928 | tf_op jit(solution)/shard_map/ppermute | solution.py:128
  436.8 9.0 fusion.104
  445.9 8.4 copy.278
  459.4 5.5 multiply_convert_fusion.2
  465.0 7.2 convert_reduce_fusion
  472.2 4.8 convolution_convert_fusion.1
  478.5 5.7 multiply_convert_fusion.3
  484.3 6.7 convert_reduce_fusion.1
  511.9 14.5 %collective-permute-done.53 = bf16[1408,768]{1,0:T(8,128)(2,1)S(1)} collective-permute-done((bf16[1408,768]{1,0:T(8,128)(2,1)S(1)}, bf16[1408,768]{1,0:T(8,128)(2,1)S(1)}, u32[]{:S(2)}, u32[]{:S(2)}) %collective-permute-start.53) | collective-permute-done | bytes 2162720 | tf_op jit(solution)/shard_map/ppermute | solution.py:118
  526.4 5.6 add_convert_fusion.1
  532.3 4.7 fusion.22
  542.8 5.6 convolution_convert_fusion
  549.9 6.2 collective-permute-done.26
  556.7 13.5 %collective-permute-done.21 = bf16[256,1408]{1,0:T(8,128)(2,1)S(1)} collective-permute-done((bf16[256,1408]{1,0:T(8,128)(2,1)S(1)}, bf16[256,1408]{1,0:T(8,128)(2,1)S(1)}, u32[]{:S(2)}, u32[]{:S(2)}) %collective-permute-start.21) | collective-permute-done | bytes 720928 | tf_op jit(solution)/shard_map/ppermute | solution.py:128
  581.6 10.1 collective-permute-done.27
  598.7 6.3 add_convert_fusion
  605.0 7.3 collective-permute-done.22
  647.3 13.1 %collective-permute-done.30 = bf16[256,1408]{1,0:T(8,128)(2,1)S(1)} collective-permute-done((bf16[256,1408]{1,0:T(8,128)(2,1)S(1)}, bf16[256,1408]{1,0:T(8,128)(2,1)S(1)}, u32[]{:S(2)}, u32[]{:S(2)}) %collective-permute-start.30) | collective-permute-done | bytes 720928 | tf_op jit(solution)/shard_map/ppermute | solution.py:128
  674.9 8.0 collective-permute-done.31
  698.6 7.3 collective-permute-done.54
  713.5 8.7 fusion.90
  722.2 12.8 %multiply_reduce_fusion = (f32[4,1024]{1,0:T(4,128)S(1)}, f32[4,1024,1024]{1,2,0:T(8,128)}) fusion(f32[4,1024,1024]{1,2,0:T(8,128)} %get-tuple-element.371, f32[4,1024]{1,0:T(4,128)S(1)} %copy-done.121, bf16[1024,4,88]{0,2,1:T(8,128)(2,1)S(1)} %copy-done.69, bf16[1024,1,2,88]{0,3,2,1:T(8,128)(2,1)S(1)} %bitcast.502, bf16[1024,1,2,88]{0,3,2,1:T(8,128)(2,1)S(1)} %bitcast.500), kind=kOutput, calls=%fused_computation.10 | convolution fusion | flops 755331072 | bytes 35028992 | tf_op jit(solution)/shard_map/qhd,khd->hqk/dot_general | solution.py:18
  735.1 8.0 multiply_convert_fusion
  748.0 6.1 bitcast_multiply_fusion.2
  765.7 4.7 convolution_convert_fusion.2
  797.7 7.9 collective-permute-done.47
  807.1 5.0 fusion.37
  824.1 37.2 %collective-permute-done.50 = bf16[1408,880]{0,1:T(8,128)(2,1)} collective-permute-done((bf16[1408,880]{0,1:T(8,128)(2,1)}, bf16[1408,880]{0,1:T(8,128)(2,1)}, u32[]{:S(2)}, u32[]{:S(2)}) %collective-permute-start.50) | collective-permute-done | bytes 2478112 | tf_op jit(solution)/shard_map/ppermute | solution.py:118
  861.3 5.2 fusion.11
  914.0 5.4 fusion.125
  950.6 9.3 fusion.12
  959.9 8.0 reshape.832
  971.2 12.1 %fusion.222 = (f32[2,256,1,1408]{3,2,1,0:T(1,128)}, f32[2,256,1,1408]{3,2,1,0:T(1,128)}) fusion(f32[2,256,2,1408]{3,2,1,0:T(2,128)} %reshape.832), kind=kLoop, calls=%fused_computation.556 | loop fusion | bytes 11534336 | tf_op jit(solution)/shard_map/slice | solution.py:433
  999.0 5.4 collective-permute-done.40
  1012.5 5.1 copy.293
  (926 shorter events, 525.3 us)
Async XLA Ops:
  7.2 75.8 %all-gather.5.cloned.1.call-start = ((), (), s32[]{:S(2)}) async-start(), calls=%async_computation.10 | async-start | bytes 4055040 | tf_op jit(solution)/shard_map/all_gather | solution.py:164
  19.7 34.7 %collective-permute-start = (bf16[256,2816]{1,0:T(8,128)(2,1)}, bf16[256,2816]{1,0:T(8,128)(2,1)}, u32[]{:S(2)}, u32[]{:S(2)}) collective-permute-start(bf16[256,2816]{1,0:T(8,128)(2,1)} %pad_maximum_fusion.15), channel_id=1, source_target_pairs={{0,4},{2,6},{4,0},{6,2},{1,5},{3,7},{5,1},{7,3},{8,12},{10,14},{12... | collective-permute-start | bytes 4325384 | tf_op jit(solution)/shard_map/ppermute | solution.py:128
  23.3 38.0 %all-to-all-start.1 = ((s32[4,1,2]{2,1,0:T(1,128)}), s32[4,1,2]{2,1,0:T(1,128)S(1)}, u32[]{:S(2)}, u32[]{:S(2)}) async-start(s32[4,1,2]{2,1,0:T(1,128)} %broadcast_in_dim.228), calls=%async_computation.1 | async-start | bytes 4096 | tf_op jit(solution)/shard_map/all_to_all | solution.py:200
  57.8 60.1 %collective-permute-start.1 = (bf16[512,2816]{1,0:T(8,128)(2,1)}, bf16[512,2816]{1,0:T(8,128)(2,1)}, u32[]{:S(2)}, u32[]{:S(2)}) collective-permute-start(bf16[512,2816]{1,0:T(8,128)(2,1)} %pad_maximum_fusion.2), channel_id=1, source_target_pairs={{0,2},{2,0},{4,6},{6,4},{1,3},{3,1},{5,7},{7,5},{8,10},{10,8},{12,... | collective-permute-start | bytes 8650760 | tf_op jit(solution)/shard_map/ppermute | solution.py:128
  85.4 30.1 %collective-permute-start.2 = (bf16[4,2,176,352]{3,2,1,0:T(8,128)(2,1)}, bf16[4,2,176,352]{3,2,1,0:T(8,128)(2,1)}, u32[]{:S(2)}, u32[]{:S(2)}) collective-permute-start(bf16[4,2,176,352]{3,2,1,0:T(8,128)(2,1)} %bitcast.6), channel_id=1, source_target_pairs={{0,1},{1,0},{2,3},{3,2},{4,5},{5,4},{6,7},{7,6},{8,9},{9,8},{10,11... | collective-permute-start | bytes 2973704 | tf_op jit(solution)/shard_map/ppermute | solution.py:118
  89.2 22.3 %collective-permute-start.3 = (f32[4,1408]{1,0:T(4,128)}, f32[4,1408]{1,0:T(4,128)S(1)}, u32[]{:S(2)}, u32[]{:S(2)}) collective-permute-start(f32[4,1408]{1,0:T(4,128)} %bitcast.427), channel_id=1, source_target_pairs={{0,1},{1,0},{2,3},{3,2},{4,5},{5,4},{6,7},{7,6},{8,9},{9,8},{10,11... | collective-permute-start | bytes 67592 | tf_op jit(solution)/shard_map/ppermute | solution.py:118
  130.6 84.1 %all-gather.7.cloned.1.call-start = ((), (), s32[]{:S(2)}) async-start(), calls=%async_computation.11 | async-start | bytes 2703360 | tf_op jit(solution)/shard_map/all_gather | solution.py:164
  133.7 136.2 %all-gather.9.cloned.1.call-start = ((), (), s32[]{:S(2)}) async-start(), calls=%async_computation.12 | async-start | bytes 2703360 | tf_op jit(solution)/shard_map/all_gather | solution.py:164
  154.6 20.3 %collective-permute-start.7 = (s32[256,2]{0,1:T(2,128)S(1)}, s32[256,2]{0,1:T(2,128)S(1)}, u32[]{:S(2)}, u32[]{:S(2)}) collective-permute-start(s32[256,2]{0,1:T(2,128)S(1)} %fusion.166), channel_id=1, source_target_pairs={{0,4},{2,6},{4,0},{6,2},{1,5},{3,7},{5,1},{7,3},{8,12},{10,14},{12... | collective-permute-start | bytes 6152 | tf_op jit(solution)/shard_map/ppermute | solution.py:128
  156.7 166.5 %all-gather.11.cloned.1.call-start = ((), (), s32[]{:S(2)}) async-start(), calls=%async_computation.13 | async-start | bytes 2703360 | tf_op jit(solution)/shard_map/all_gather | solution.py:164
  161.1 44.5 %collective-permute-start.6 = (bf16[1408,704]{0,1:T(8,128)(2,1)}, bf16[1408,704]{0,1:T(8,128)(2,1)}, u32[]{:S(2)}, u32[]{:S(2)}) collective-permute-start(bf16[1408,704]{0,1:T(8,128)(2,1)} %copy.259), channel_id=1, source_target_pairs={{0,1},{1,0},{2,3},{3,2},{4,5},{5,4},{6,7},{7,6},{8,9},{9,8},{10,11... | collective-permute-start | bytes 5947400 | tf_op jit(solution)/shard_map/ppermute | solution.py:118
  254.3 45.3 %collective-permute-start.13 = (bf16[1408,704]{0,1:T(8,128)(2,1)}, bf16[1408,704]{0,1:T(8,128)(2,1)}, u32[]{:S(2)}, u32[]{:S(2)}) collective-permute-start(bf16[1408,704]{0,1:T(8,128)(2,1)} %copy.264), channel_id=1, source_target_pairs={{0,1},{1,0},{2,3},{3,2},{4,5},{5,4},{6,7},{7,6},{8,9},{9,8},{10,11... | collective-permute-start | bytes 5947400 | tf_op jit(solution)/shard_map/ppermute | solution.py:118
  275.8 414.8 %reduce-scatter.15.cloned.1.call-start = ((), (), s32[]{:S(2)}) async-start(), calls=%async_computation.15 | async-start | bytes 2703360 | tf_op jit(solution)/shard_map/reduce_scatter | solution.py:305
  341.8 92.0 %collective-permute-start.23 = (bf16[256,1408]{1,0:T(8,128)(2,1)}, bf16[256,1408]{1,0:T(8,128)(2,1)}, u32[]{:S(2)}, u32[]{:S(2)}) collective-permute-start(bf16[256,1408]{1,0:T(8,128)(2,1)} %get-tuple-element.232), channel_id=1, source_target_pairs={{0,4},{2,6},{4,0},{6,2},{1,5},{3,7},{5,1},{7,3},{8,12},{10,14},{12... | collective-permute-start | bytes 2162696 | tf_op jit(solution)/shard_map/ppermute | solution.py:128
  346.5 107.8 %collective-permute-start.36 = (bf16[1,2816,352]{1,2,0:T(8,128)(2,1)}, bf16[1,2816,352]{1,2,0:T(8,128)(2,1)}, u32[]{:S(2)}, u32[]{:S(2)}) collective-permute-start(bf16[1,2816,352]{1,2,0:T(8,128)(2,1)} %copy.275), channel_id=1, source_target_pairs={{0,4},{2,6},{4,0},{6,2},{1,5},{3,7},{5,1},{7,3},{8,12},{10,14},{12... | collective-permute-start | bytes 5947400 | tf_op jit(solution)/shard_map/ppermute | solution.py:128
  362.1 69.1 %collective-permute-start.16 = (bf16[256,1408]{1,0:T(8,128)(2,1)}, bf16[256,1408]{1,0:T(8,128)(2,1)}, u32[]{:S(2)}, u32[]{:S(2)}) collective-permute-start(bf16[256,1408]{1,0:T(8,128)(2,1)} %add_convert_fusion.5), channel_id=1, source_target_pairs={{0,4},{2,6},{4,0},{6,2},{1,5},{3,7},{5,1},{7,3},{8,12},{10,14},{12... | collective-permute-start | bytes 2162696 | tf_op jit(solution)/shard_map/ppermute | solution.py:128
  364.7 94.7 %collective-permute-start.18 = (bf16[1408,768]{1,0:T(8,128)(2,1)}, bf16[1408,768]{1,0:T(8,128)(2,1)}, u32[]{:S(2)}, u32[]{:S(2)}) collective-permute-start(bf16[1408,768]{1,0:T(8,128)(2,1)} %all-gather.9.cloned.1.call-done), channel_id=1, source_target_pairs={{0,1},{1,0},{2,3},{3,2},{4,5},{5,4},{6,7},{7,6},{8,9},{9,8},{10,11... | collective-permute-start | bytes 6488072 | tf_op jit(solution)/shard_map/ppermute | solution.py:118
  369.4 95.5 %collective-permute-start.19 = (bf16[1408,768]{1,0:T(8,128)(2,1)}, bf16[1408,768]{1,0:T(8,128)(2,1)}, u32[]{:S(2)}, u32[]{:S(2)}) collective-permute-start(bf16[1408,768]{1,0:T(8,128)(2,1)} %all-gather.11.cloned.1.call-done), channel_id=1, source_target_pairs={{0,1},{1,0},{2,3},{3,2},{4,5},{5,4},{6,7},{7,6},{8,9},{9,8},{10,11... | collective-permute-start | bytes 6488072 | tf_op jit(solution)/shard_map/ppermute | solution.py:118
  433.8 25.6 %collective-permute-start.17 = (bf16[512,1408]{1,0:T(8,128)(2,1)}, bf16[512,1408]{1,0:T(8,128)(2,1)}, u32[]{:S(2)}, u32[]{:S(2)}) collective-permute-start(bf16[512,1408]{1,0:T(8,128)(2,1)} %pad_maximum_fusion.19), channel_id=1, source_target_pairs={{0,2},{2,0},{4,6},{6,4},{1,3},{3,1},{5,7},{7,5},{8,10},{10,8},{12,... | collective-permute-start | bytes 4325384 | tf_op jit(solution)/shard_map/ppermute | solution.py:128
  436.4 28.5 %collective-permute-start.24 = (bf16[512,1408]{1,0:T(8,128)(2,1)}, bf16[512,1408]{1,0:T(8,128)(2,1)}, u32[]{:S(2)}, u32[]{:S(2)}) collective-permute-start(bf16[512,1408]{1,0:T(8,128)(2,1)} %pad_maximum_fusion.20), channel_id=1, source_target_pairs={{0,2},{2,0},{4,6},{6,4},{1,3},{3,1},{5,7},{7,5},{8,10},{10,8},{12,... | collective-permute-start | bytes 4325384 | tf_op jit(solution)/shard_map/ppermute | solution.py:128
  458.6 491.1 %collective-permute-start.37 = (bf16[2,2816,352]{1,2,0:T(8,128)(2,1)}, bf16[2,2816,352]{1,2,0:T(8,128)(2,1)}, u32[]{:S(2)}, u32[]{:S(2)}) collective-permute-start(bf16[2,2816,352]{1,2,0:T(8,128)(2,1)} %pad_maximum_fusion.1), channel_id=1, source_target_pairs={{0,2},{2,0},{4,6},{6,4},{1,3},{3,1},{5,7},{7,5},{8,10},{10,8},{12,... | collective-permute-start | bytes 11894792 | tf_op jit(solution)/shard_map/ppermute | solution.py:128
  477.0 49.4 %collective-permute-start.53 = (bf16[1408,768]{1,0:T(8,128)(2,1)S(1)}, bf16[1408,768]{1,0:T(8,128)(2,1)S(1)}, u32[]{:S(2)}, u32[]{:S(2)}) collective-permute-start(bf16[1408,768]{1,0:T(8,128)(2,1)S(1)} %convolution_convert_fusion.1), channel_id=1, source_target_pairs={{0,1},{1,0},{2,3},{3,2},{4,5},{5,4},{6,7},{7,6},{8,9},{9,8},{10,11... | collective-permute-start | bytes 6488072 | tf_op jit(solution)/shard_map/ppermute | solution.py:118
  498.2 34.1 %collective-permute-start.25 = (bf16[512,1408]{1,0:T(8,128)(2,1)}, bf16[512,1408]{1,0:T(8,128)(2,1)}, u32[]{:S(2)}, u32[]{:S(2)}) collective-permute-start(bf16[512,1408]{1,0:T(8,128)(2,1)} %fusion.39), channel_id=1, source_target_pairs={{0,2},{2,0},{4,6},{6,4},{1,3},{3,1},{5,7},{7,5},{8,10},{10,8},{12,... | collective-permute-start | bytes 4325384 | tf_op jit(solution)/shard_map/ppermute | solution.py:128
  503.9 34.6 %collective-permute-start.20 = (bf16[512,1408]{1,0:T(8,128)(2,1)}, bf16[512,1408]{1,0:T(8,128)(2,1)}, u32[]{:S(2)}, u32[]{:S(2)}) collective-permute-start(bf16[512,1408]{1,0:T(8,128)(2,1)} %fusion.38), channel_id=1, source_target_pairs={{0,2},{2,0},{4,6},{6,4},{1,3},{3,1},{5,7},{7,5},{8,10},{10,8},{12,... | collective-permute-start | bytes 4325384 | tf_op jit(solution)/shard_map/ppermute | solution.py:128
  532.0 165.8 %reduce-scatter.17.cloned.1.call-start = ((), (), s32[]{:S(2)}) async-start(), calls=%async_computation.16 | async-start | bytes 2703360 | tf_op jit(solution)/shard_map/reduce_scatter | solution.py:305
  542.2 28.0 %collective-permute-start.21 = (bf16[256,1408]{1,0:T(8,128)(2,1)S(1)}, bf16[256,1408]{1,0:T(8,128)(2,1)S(1)}, u32[]{:S(2)}, u32[]{:S(2)}) collective-permute-start(bf16[256,1408]{1,0:T(8,128)(2,1)S(1)} %slice.846), channel_id=1, source_target_pairs={{0,4},{2,6},{4,0},{6,2},{1,5},{3,7},{5,1},{7,3},{8,12},{10,14},{12... | collective-permute-start | bytes 2162696 | tf_op jit(solution)/shard_map/ppermute | solution.py:128
  548.4 50.2 %collective-permute-start.56 = (bf16[1408,768]{1,0:T(8,128)(2,1)}, bf16[1408,768]{1,0:T(8,128)(2,1)}, u32[]{:S(2)}, u32[]{:S(2)}) collective-permute-start(bf16[1408,768]{1,0:T(8,128)(2,1)} %convolution_convert_fusion), channel_id=1, source_target_pairs={{0,1},{1,0},{2,3},{3,2},{4,5},{5,4},{6,7},{7,6},{8,9},{9,8},{10,11... | collective-permute-start | bytes 6488072 | tf_op jit(solution)/shard_map/ppermute | solution.py:118
  580.1 32.2 %collective-permute-start.22 = (bf16[256,1408]{1,0:T(8,128)(2,1)}, bf16[256,1408]{1,0:T(8,128)(2,1)}, u32[]{:S(2)}, u32[]{:S(2)}) collective-permute-start(bf16[256,1408]{1,0:T(8,128)(2,1)} %get-tuple-element.290), channel_id=1, source_target_pairs={{0,1},{1,0},{2,3},{3,2},{4,5},{5,4},{6,7},{7,6},{8,9},{9,8},{10,11... | collective-permute-start | bytes 2162696 | tf_op jit(solution)/shard_map/ppermute | solution.py:118
  594.2 21.4 %collective-permute-start.28 = (bf16[512,1408]{1,0:T(8,128)(2,1)}, bf16[512,1408]{1,0:T(8,128)(2,1)}, u32[]{:S(2)}, u32[]{:S(2)}) collective-permute-start(bf16[512,1408]{1,0:T(8,128)(2,1)} %pad_maximum_fusion.21), channel_id=1, source_target_pairs={{0,2},{2,0},{4,6},{6,4},{1,3},{3,1},{5,7},{7,5},{8,10},{10,8},{12,... | collective-permute-start | bytes 4325384 | tf_op jit(solution)/shard_map/ppermute | solution.py:128
  605.0 270.8 %reduce-scatter.19.cloned.1.call-start = ((), (), s32[]{:S(2)}) async-start(), calls=%async_computation.17 | async-start | bytes 1351680
  668.0 299.9 %reduce-scatter.21.cloned.1.call-start = ((), (), s32[]{:S(2)}) async-start(), calls=%async_computation.18 | async-start | bytes 2252800
  685.4 21.7 %collective-permute-start.32 = (bf16[512,1408]{1,0:T(8,128)(2,1)}, bf16[512,1408]{1,0:T(8,128)(2,1)}, u32[]{:S(2)}, u32[]{:S(2)}) collective-permute-start(bf16[512,1408]{1,0:T(8,128)(2,1)} %pad_maximum_fusion.22), channel_id=1, source_target_pairs={{0,2},{2,0},{4,6},{6,4},{1,3},{3,1},{5,7},{7,5},{8,10},{10,8},{12,... | collective-permute-start | bytes 4325384 | tf_op jit(solution)/shard_map/ppermute | solution.py:128
  697.8 175.3 %collective-permute-start.57 = (bf16[1,352,768]{2,1,0:T(8,128)(2,1)}, bf16[1,352,768]{2,1,0:T(8,128)(2,1)}, u32[]{:S(2)}, u32[]{:S(2)}) collective-permute-start(bf16[1,352,768]{2,1,0:T(8,128)(2,1)} %bitcast.487), channel_id=1, source_target_pairs={{0,4},{2,6},{4,0},{6,2},{1,5},{3,7},{5,1},{7,3},{8,12},{10,14},{12... | collective-permute-start | bytes 1622024 | tf_op jit(solution)/shard_map/ppermute | solution.py:128
  707.1 185.0 %collective-permute-start.55 = (bf16[2,352,768]{2,1,0:T(8,128)(2,1)}, bf16[2,352,768]{2,1,0:T(8,128)(2,1)}, u32[]{:S(2)}, u32[]{:S(2)}) collective-permute-start(bf16[2,352,768]{2,1,0:T(8,128)(2,1)} %pad_maximum_fusion.26), channel_id=1, source_target_pairs={{0,2},{2,0},{4,6},{6,4},{1,3},{3,1},{5,7},{7,5},{8,10},{10,8},{12,... | collective-permute-start | bytes 3244040 | tf_op jit(solution)/shard_map/ppermute | solution.py:128
  770.3 35.3 %collective-permute-start.47 = (bf16[1408,528]{0,1:T(8,128)(2,1)}, bf16[1408,528]{0,1:T(8,128)(2,1)}, u32[]{:S(2)}, u32[]{:S(2)}) collective-permute-start(bf16[1408,528]{0,1:T(8,128)(2,1)} %convolution_convert_fusion.2), channel_id=1, source_target_pairs={{0,1},{1,0},{2,3},{3,2},{4,5},{5,4},{6,7},{7,6},{8,9},{9,8},{10,11... | collective-permute-start | bytes 4460552 | tf_op jit(solution)/shard_map/ppermute | solution.py:118
  794.7 21.3 %collective-permute-start.34 = (bf16[256,1408]{1,0:T(8,128)(2,1)}, bf16[256,1408]{1,0:T(8,128)(2,1)S(1)}, u32[]{:S(2)}, u32[]{:S(2)}) collective-permute-start(bf16[256,1408]{1,0:T(8,128)(2,1)} %slice.843), channel_id=1, source_target_pairs={{0,4},{2,6},{4,0},{6,2},{1,5},{3,7},{5,1},{7,3},{8,12},{10,14},{12... | collective-permute-start | bytes 2162696 | tf_op jit(solution)/shard_map/ppermute | solution.py:128
  805.6 55.7 %collective-permute-start.50 = (bf16[1408,880]{0,1:T(8,128)(2,1)}, bf16[1408,880]{0,1:T(8,128)(2,1)}, u32[]{:S(2)}, u32[]{:S(2)}) collective-permute-start(bf16[1408,880]{0,1:T(8,128)(2,1)} %pad_maximum_fusion.10), channel_id=1, source_target_pairs={{0,1},{1,0},{2,3},{3,2},{4,5},{5,4},{6,7},{7,6},{8,9},{9,8},{10,11... | collective-permute-start | bytes 7434248 | tf_op jit(solution)/shard_map/ppermute | solution.py:118
  815.9 154.9 %reduce-scatter.23.cloned.1.call-start = ((), (), s32[]{:S(2)}) async-start(), calls=%async_computation.19 | async-start | bytes 3153920 | tf_op jit(solution)/shard_map/reduce_scatter | solution.py:305
  875.3 22.1 %collective-permute-start.58 = (bf16[2,352,768]{2,1,0:T(8,128)(2,1)}, bf16[2,352,768]{2,1,0:T(8,128)(2,1)}, u32[]{:S(2)}, u32[]{:S(2)}) collective-permute-start(bf16[2,352,768]{2,1,0:T(8,128)(2,1)} %pad_maximum_fusion.27), channel_id=1, source_target_pairs={{0,2},{2,0},{4,6},{6,4},{1,3},{3,1},{5,7},{7,5},{8,10},{10,8},{12,... | collective-permute-start | bytes 3244040 | tf_op jit(solution)/shard_map/ppermute | solution.py:128
  885.7 20.1 %all-to-all-start.3 = ((bf16[256,4,352]{0,2,1:T(8,128)(2,1)}), bf16[256,4,352]{0,2,1:T(8,128)(2,1)}, u32[]{:S(2)}, u32[]{:S(2)}) async-start(bf16[256,4,352]{0,2,1:T(8,128)(2,1)} %bitcast.98), calls=%async_computation.3 | async-start | bytes 1441792 | tf_op jit(solution)/shard_map/all_to_all | solution.py:365
  889.9 105.4 %reduce-scatter.13.cloned.1.call-start = ((), (), s32[]{:S(2)}) async-start(), calls=%async_computation.14 | async-start | bytes 1351680 | tf_op jit(solution)/shard_map/reduce_scatter | solution.py:372
  904.1 29.3 %collective-permute-start.35 = (bf16[256,1408]{1,0:T(8,128)(2,1)S(1)}, bf16[256,1408]{1,0:T(8,128)(2,1)}, u32[]{:S(2)}, u32[]{:S(2)}) collective-permute-start(bf16[256,1408]{1,0:T(8,128)(2,1)S(1)} %get-tuple-element.238), channel_id=1, source_target_pairs={{0,1},{1,0},{2,3},{3,2},{4,5},{5,4},{6,7},{7,6},{8,9},{9,8},{10,11... | collective-permute-start | bytes 2162696 | tf_op jit(solution)/shard_map/ppermute | solution.py:118
  905.7 26.0 %collective-permute-start.45 = (f32[352,128]{1,0:T(8,128)S(1)}, f32[352,128]{1,0:T(8,128)S(1)}, u32[]{:S(2)}, u32[]{:S(2)}) collective-permute-start(f32[352,128]{1,0:T(8,128)S(1)} %add.859), channel_id=1, source_target_pairs={{0,8},{8,0},{16,24},{24,16},{1,9},{9,1},{17,25},{25,17},{2,10},{10... | collective-permute-start | bytes 540680 | tf_op jit(solution)/shard_map/ppermute | solution.py:128
  920.6 25.9 %collective-permute-start.39 = (bf16[2,4,176,352]{3,2,1,0:T(8,128)(2,1)}, bf16[2,4,176,352]{3,2,1,0:T(8,128)(2,1)}, u32[]{:S(2)}, u32[]{:S(2)}) collective-permute-start(bf16[2,4,176,352]{3,2,1,0:T(8,128)(2,1)} %fusion.102), channel_id=1, source_target_pairs={{0,1},{1,0},{2,3},{3,2},{4,5},{5,4},{6,7},{7,6},{8,9},{9,8},{10,11... | collective-permute-start | bytes 2973704 | tf_op jit(solution)/shard_map/ppermute | solution.py:118
  931.7 57.2 %collective-permute-start.46 = (f32[352,128]{1,0:T(8,128)S(1)}, f32[352,128]{1,0:T(8,128)S(1)}, u32[]{:S(2)}, u32[]{:S(2)}) collective-permute-start(f32[352,128]{1,0:T(8,128)S(1)} %add.860), channel_id=1, source_target_pairs={{0,16},{8,24},{16,0},{24,8},{1,17},{9,25},{17,1},{25,9},{2,18},{10... | collective-permute-start | bytes 540680 | tf_op jit(solution)/shard_map/ppermute | solution.py:128
  969.1 23.4 %collective-permute-start.48 = (bf16[1,352,528]{1,2,0:T(8,128)(2,1)S(1)}, bf16[1,352,528]{1,2,0:T(8,128)(2,1)S(1)}, u32[]{:S(2)}, u32[]{:S(2)}) collective-permute-start(bf16[1,352,528]{1,2,0:T(8,128)(2,1)S(1)} %bitcast.470), channel_id=1, source_target_pairs={{0,4},{2,6},{4,0},{6,2},{1,5},{3,7},{5,1},{7,3},{8,12},{10,14},{12... | collective-permute-start | bytes 1115144 | tf_op jit(solution)/shard_map/ppermute | solution.py:128
  970.8 26.1 %collective-permute-start.51 = (bf16[1,352,880]{2,1,0:T(8,128)(2,1)}, bf16[1,352,880]{2,1,0:T(8,128)(2,1)S(1)}, u32[]{:S(2)}, u32[]{:S(2)}) collective-permute-start(bf16[1,352,880]{2,1,0:T(8,128)(2,1)} %bitcast.476), channel_id=1, source_target_pairs={{0,4},{2,6},{4,0},{6,2},{1,5},{3,7},{5,1},{7,3},{8,12},{10,14},{12... | collective-permute-start | bytes 1858568 | tf_op jit(solution)/shard_map/ppermute | solution.py:128
  998.2 27.9 %collective-permute-start.52 = (bf16[2,352,880]{2,1,0:T(8,128)(2,1)}, bf16[2,352,880]{2,1,0:T(8,128)(2,1)}, u32[]{:S(2)}, u32[]{:S(2)}) collective-permute-start(bf16[2,352,880]{2,1,0:T(8,128)(2,1)} %pad_maximum_fusion.24), channel_id=1, source_target_pairs={{0,2},{2,0},{4,6},{6,4},{1,3},{3,1},{5,7},{7,5},{8,10},{10,8},{12,... | collective-permute-start | bytes 3717128 | tf_op jit(solution)/shard_map/ppermute | solution.py:128
  (233 other events, 3067.5 us)
Sparse Core Ops, SparseCore 0:
  15.2 67.8 all-gather.4
  133.8 48.5 all-gather.6
  184.5 45.5 all-gather.8
  275.9 47.1 all-gather.10
  532.1 43.4 reduce-scatter.14
  605.1 43.6 reduce-scatter.16
  668.1 23.2 reduce-scatter.18
  816.1 37.0 reduce-scatter.20
  871.0 53.3 reduce-scatter.22
  949.9 28.0 reduce-scatter.12

commit v3 on v2

--- a/solution.py
+++ b/solution.py
@@ -117,9 +117,6 @@
     def other(values):
         return lax.ppermute(values, "tensor", swap)
 
-    def pair(values):
-        return (values, other(values))
-
     bits = [1 << i for i in range(nk.bit_length() - 1)]
     relative = jnp.arange(nk) ^ k
 
@@ -127,10 +124,16 @@
         count = lax.axis_size(axis_name)
         return lax.ppermute(values, axis_name, [(i, i ^ bit) for i in range(count)])
 
-    def gather_rows(values):
-        for bit in reversed(bits):
+    def gather_far(values):
+        for bit in reversed(bits[1:]):
             values = jnp.concatenate([values, flip(values, "context", bit)], 0)
         return values
+
+    def gather_near(values):
+        return jnp.concatenate([values, flip(values, "context", bits[0])], 0)
+
+    def gather_rows(values):
+        return gather_near(gather_far(values))
 
     order = [sum(((p >> j) & 1) << (len(bits) - 1 - j) for j in range(len(bits))) for p in range(nk)]
 
@@ -161,12 +164,14 @@
         return jnp.stack([first, second])
 
     def gathered(values):
-        return lax.all_gather(values, "shard", axis=0, tiled=True)
+        return lax.all_gather(values, ("tensor", "shard"), axis=0, tiled=True)
+
+    def halves(values):
+        return (values[:width], values[width:])
 
     pin = lax.optimization_barrier
     first_part = jnp.concatenate(
         [
-            block(skip_weight, eb, 2).reshape(-1, eb),
             block(triple_weight, cb, 2).reshape(rows_z, 3 * cb),
             block(self_out_weight, cb, 0).T,
         ],
@@ -180,17 +185,18 @@
         ],
         1,
     )
+    skip_part = jnp.pad(block(skip_weight, eb, 2).reshape(-1, eb), ((0, 0), (0, -eb % 128)))
+    skip_z = lax.all_gather(skip_part, ("shard", "tensor"), axis=0, tiled=True)
+    skip_block = jnp.transpose(skip_z[:, :eb].reshape(nz * ny, 2, -1, eb), (1, 0, 2, 3)).reshape(2 * width, eb)
     first_z = gathered(first_part)
     second_z = gathered(second_part)
     up_z = gathered(block(up_weight, hb, 1))
     down_z = gathered(block(down_weight, hb, 0).T)
-    skip_z = first_z[:, :eb].reshape(nz, 2, -1, eb)
-    skip_block = jnp.transpose(by_batch(skip_z, other(skip_z)), (2, 1, 0, 3, 4)).reshape(2 * width, eb)
 
     def own_columns(values, size, half):
         last = values.ndim - 1
-        first = lax.dynamic_slice_in_dim(values, y * half + k * size, size, last)
-        second = lax.dynamic_slice_in_dim(values, (1 - y) * half + k * size, size, last)
+        first = lax.dynamic_slice_in_dim(values, k * size, size, last)
+        second = lax.dynamic_slice_in_dim(values, half + k * size, size, last)
         return (first, second)
 
     tok_rows, skip_rows, cot_rows = mine(tokens), mine(skip_in), mine(cotangent)
@@ -204,15 +210,17 @@
     shift_part = matmul(silu_rows, shift_weight).reshape(nz, ny, width)
     shift_mine = lax.dynamic_index_in_dim(shift_part, y, 1, keepdims=False)
     shift_give = lax.dynamic_index_in_dim(shift_part, 1 - y, 1, keepdims=False)
-    shift_part = shift_mine + other(shift_give)
+    shift_got = other(shift_give)
+    shift_part = shift_mine + shift_got
     shift_row = jnp.sum(lax.all_to_all(shift_part, "shard", 0, 0, tiled=True), 0) + width_biases[1]
 
-    tok_all = gather_rows(jnp.concatenate([tok_rows, skip_rows], 1))
-    summed_block = ranked(matmul(tok_all, skip_block).astype(BF).reshape(nk, local_len, eb)).reshape(length, eb)
+    tok_here = gather_far(jnp.concatenate([tok_rows, skip_rows], 1))
+    tok_halves = pin((tok_here, flip(tok_here, "context", bits[0])))
+    summed_block = jnp.concatenate([matmul(t, skip_block).astype(BF) for t in tok_halves], 0)
+    summed_block = ranked(summed_block.reshape(nk, local_len, eb)).reshape(length, eb)
     summed = lax.all_to_all(summed_block, "context", split_axis=0, concat_axis=1, tiled=True).astype(F32) + width_biases[0]
 
-    summed, first_z = pin((summed, first_z[:, eb:]))
-    first_pair = pair(first_z)
+    first_pair = halves(first_z)
     triple_full = [w[:, : 3 * cb] for w in first_pair]
     self_out_full = [w[:, 3 * cb :] for w in first_pair]
 
@@ -240,24 +248,26 @@
 
     (query, key, value), pull_self = jax.vjp(self_piece, triple, head_gains, head_biases)
     query, key, value = query.astype(BF), key.astype(BF), value.astype(BF)
-    query, key, value, second_z = pin((query, key, value, second_z))
-    second_pair = pair(second_z)
+    query, key, value, cot_late = pin((query, key, value, cot_rows))
+    cot_far = gather_far(cot_late)
+    mix, self_sums = attention_forward(query, key, value)
+    mix, cot_far = pin((mix, cot_far))
+    mix_parts = from_heads(mix[:, None])
+    resid_one = resid_zero + (
+        scatter_rows([(mix_parts[0], self_out_full[0], contract_cols), (mix_parts[1], self_out_full[1], contract_cols)]) + width_biases[2]
+    )
+
+
+    resid_one, second_z = pin((resid_one, second_z))
+
+    def second_piece(resid_in, gain_rows, bias_rows):
+        return layer_norm(resid_in, gain_rows[2], bias_rows[2])
+
+    normed_two, pull_second = jax.vjp(second_piece, resid_one, norm_gains, norm_biases)
+    second_pair = halves(second_z)
     cross_q_full = [w[:, :cb] for w in second_pair]
     cross_kv_full = [w[:, cb : 3 * cb] for w in second_pair]
     cross_out_full = [w[:, 3 * cb :] for w in second_pair]
-    mix, self_sums = attention_forward(query, key, value)
-    mix_parts = from_heads(mix[:, None])
-    resid_one = resid_zero + (
-        scatter_rows([(mix_parts[0], self_out_full[0], contract_cols), (mix_parts[1], self_out_full[1], contract_cols)]) + width_biases[2]
-    )
-
-    resid_one, up_z = pin((resid_one, up_z))
-    up_full = pair(up_z)
-
-    def second_piece(resid_in, gain_rows, bias_rows):
-        return layer_norm(resid_in, gain_rows[2], bias_rows[2])
-
-    normed_two, pull_second = jax.vjp(second_piece, resid_one, norm_gains, norm_biases)
     normed_two_all = gather_rows(normed_two.astype(BF))
     cq_bias = own_columns(column_biases[3], cb, half_cols)
     kv_bias = own_columns(column_biases[4:6], cb, half_cols)
@@ -271,19 +281,22 @@
 
     (cq, ck, cv), pull_cross = jax.vjp(cross_piece, cross_raw, pair_raw, head_gains, head_biases)
     cq, ck, cv = cq.astype(BF), ck.astype(BF), cv.astype(BF)
-    cq, ck, cv, down_z = pin((cq, ck, cv, down_z))
-    down_full = pair(down_z)
     cross_mix, cross_sums = attention_forward(cq, ck, cv)
     cross_parts = from_heads(cross_mix[:, None])
     resid_two = resid_one + (
         scatter_rows([(cross_parts[0], cross_out_full[0], contract_cols), (cross_parts[1], cross_out_full[1], contract_cols)]) + width_biases[3]
     )
 
+    resid_two, up_z = pin((resid_two, up_z))
+
     def third_piece(resid_in, gain_rows, bias_rows):
         return layer_norm(resid_in, gain_rows[3], bias_rows[3])
 
     normed_three, pull_third = jax.vjp(third_piece, resid_two, norm_gains, norm_biases)
     normed_three_all = gather_rows(normed_three.astype(BF))
+    up_full, down_full = halves(up_z), halves(down_z)
+    normed_three_all, skip_late = pin((normed_three_all, skip_block))
+    skip_far = gather_far(skip_late[None])
     hidden_bias = own_columns(hidden_biases, hb, half_hidden)
 
     def gelu_piece(hidden_in):
@@ -294,31 +307,60 @@
         act, pull = jax.vjp(gelu_piece, matmul(normed_three_all, w) + b)
         active.append(act.astype(BF))
         pull_gelu.append(pull)
-    result = resid_two + (
-        scatter_rows([(active[0], down_full[0], contract_cols), (active[1], down_full[1], contract_cols)]) + width_biases[4]
-    )
-    result_low = result.astype(BF)
-    result_out = by_batch(result_low, other(result_low)).astype(F32)
-
-    def reduced(own, theirs):
-        total = own + other(theirs.astype(BF)).astype(F32)
+    def reduced(parts):
+        total = jnp.concatenate([p.astype(BF) for p in parts], 0)
+        return lax.psum_scatter(total, ("tensor", "shard"), scatter_dimension=0, tiled=True)
+
+    def own_first(parts):
+        return (jnp.where(y == 0, parts[0], parts[1]), jnp.where(y == 0, parts[1], parts[0]))
+
+    def over_shard(own, received):
+        total = own + received.astype(F32)
         return lax.psum_scatter(total.astype(BF), "shard", scatter_dimension=0, tiled=True)
 
     def spread(values):
-        return ranked(gather_rows(values[None]))
+        values = values[None]
+        for bit in reversed(bits):
+            got, high = flip(values, "context", bit), (k & bit) != 0
+            values = jnp.concatenate([jnp.where(high, got, values), jnp.where(high, values, got)], 0)
+        return values
+
+    def by_rank(values, count):
+        depth = len(bits)
+        rows = values.shape[1]
+        values = values.reshape((2,) * depth + (rows, count, -1))
+        back = tuple(reversed(range(depth)))
+        return jnp.transpose(values, (depth, depth + 1) + back + (depth + 2,)).reshape(rows, count, -1)
 
     def columns_out(values, count):
-        got = values.reshape(nk, values.shape[1], count, -1)
-        return jnp.transpose(got, (1, 2, 0, 3)).reshape(values.shape[1], count, -1).astype(F32)
+        return by_rank(spread(values), count).astype(F32)
+
+    def placed_out(values, count):
+        got = gather_rows(values[None])
+        size = values.shape[1] // count
+        source = ((jnp.asarray(order) ^ k)[:, None] * size + jnp.arange(size)).astype(jnp.int32)
+        select = (source[:, :, None] == jnp.arange(nk * size)).astype(BF)
+        return jnp.stack(
+            [contract("prn,pnm->rm", got[:, :, i * size : (i + 1) * size], select) for i in range(count)], 1
+        )
 
     def rows_out(values):
-        return jnp.transpose(values, (0, 2, 1)).reshape(-1, values.shape[1]).astype(F32)
-
-    cot_all = gather_rows(cot_rows)
+        depth = len(bits)
+        count, rows = values.shape[1:]
+        values = values.reshape((2,) * depth + (count, rows))
+        values = jnp.transpose(values, tuple(reversed(range(depth))) + (depth, depth + 1))
+        return values.reshape(-1, rows).astype(F32)
+
+    def wide_out(values):
+        return jnp.concatenate([values[order[p]] for p in range(nk)], 1).astype(F32)
+
+    cot_all = gather_near(cot_far)
     grad_out = cot_rows.astype(F32)
-    down_grad = spread(reduced(*[contract_rows(cot_all, a) for a in active]))
+    down_grad = reduced([contract_rows(cot_all, a) for a in active]).T
     hidden_grad = [pull(matmul(cot_all, w))[0].astype(BF) for pull, w in zip(pull_gelu, down_full)]
-    up_grad = spread(reduced(*[contract_rows(normed_three_all, h) for h in hidden_grad]))
+    hidden_grad[0], hidden_grad[1], skip_far = pin((hidden_grad[0], hidden_grad[1], skip_far))
+    skip_all = gather_near(skip_far)
+    up_grad = reduced([contract_rows(normed_three_all, h) for h in hidden_grad])
     third_grads = pull_third(
         scatter_rows([(hidden_grad[0], up_full[0], contract_cols), (hidden_grad[1], up_full[1], contract_cols)])
     )
@@ -347,43 +389,61 @@
     grad_one_all = gather_rows(grad_one_low)
     self_out_grad = [contract_rows(grad_one_all, p) for p in mix_parts]
     small_grad = [jnp.concatenate(g, 1) for g in zip(cross_q_grad, cross_kv_grad, cross_out_grad, self_out_grad)]
-    small_grad = spread(reduced(*small_grad))
+    small_grad = own_first(small_grad)
     mix_grad = to_heads([matmul(grad_one_all, w).astype(BF) for w in self_out_full], 1)[:, 0]
+    mix_grad, small_low, down_grad, active[0], active[1] = pin(
+        (mix_grad, small_grad[1].astype(BF), down_grad, active[0], active[1])
+    )
+    down_grad = spread(down_grad)
+    small_low = other(small_low)
+    result = resid_two + (
+        scatter_rows([(active[0], down_full[0], contract_cols), (active[1], down_full[1], contract_cols)]) + width_biases[4]
+    )
+    result_low = result.astype(BF)
+    result_out = by_batch(result_low, other(result_low)).astype(F32)
     q_back, k_back, v_back = attention_backward(query, key, value, self_sums, mix_grad)
+    q_back, k_back, v_back = q_back.astype(BF), k_back.astype(BF), v_back.astype(BF)
     self_grads = pull_self(
-        (q_back.astype(BF).astype(F32), k_back.astype(BF).astype(F32), v_back.astype(BF).astype(F32))
-    )
-    triple_low = from_heads(self_grads[0].astype(BF))
-    triple_grad = spread(reduced(*[contract_rows(normed_one_all, g) for g in triple_low]))
-    first_grads = pull_first(
-        (
-            resid_one_grad,
-            scatter_rows([(triple_low[0], triple_full[0], contract_cols), (triple_low[1], triple_full[1], contract_cols)]),
-        )
-    )
+        (q_back.astype(F32), k_back.astype(F32), v_back.astype(F32))
+    )
+    triple_raw, small_low = pin((self_grads[0].astype(BF), small_low))
+    small_grad = over_shard(small_grad[0], small_low)
+    triple_low = from_heads(triple_raw)
+    triple_grad = [contract_rows(normed_one_all, g) for g in own_first(triple_low)]
+    triple_got = other(triple_grad[1].astype(BF))
+    normed_grad = scatter_rows([(triple_low[0], triple_full[0], contract_cols), (triple_low[1], triple_full[1], contract_cols)])
+    normed_grad, triple_got, up_grad = pin((normed_grad, triple_got, up_grad))
+    up_grad = spread(up_grad)
+    triple_grad = over_shard(triple_grad[0], triple_got)
+    first_grads = pull_first((resid_one_grad, normed_grad))
     summed_low = first_grads[0].astype(BF)
     summed_cols = lax.all_to_all(summed_low, "context", split_axis=1, concat_axis=0, tiled=True)
     summed_cols = ranked(summed_cols.reshape(nk, local_len, eb), 0, True).reshape(length, eb)
-    skip_part = contract_rows(tok_all, summed_cols).reshape(2, nz, ny, -1, eb)
+    skip_part = contract_rows(tok_halves[0], summed_cols[: length // 2]) + contract_rows(tok_halves[1], summed_cols[length // 2 :])
+    skip_part = pin(skip_part.astype(BF)).reshape(2, nz, ny, -1, eb)
     keep = lax.dynamic_index_in_dim(skip_part, y, 2, keepdims=False)
     give = lax.dynamic_index_in_dim(skip_part, 1 - y, 2, keepdims=False)
-    skip_total = (keep + other(give.astype(BF)).astype(F32)).astype(BF)
+    skip_total = (keep.astype(F32) + other(give).astype(F32)).astype(BF)
     skip_total = jnp.transpose(skip_total, (1, 0, 2, 3)).reshape(-1, eb)
     skip_grad = lax.psum_scatter(skip_total, "shard", scatter_dimension=0, tiled=True)
-    skip_grad_out = jnp.transpose(spread(skip_grad), (1, 0, 2)).reshape(2, -1, width).astype(F32)
-
-    skip_all = gather_rows(skip_block[None])
+    skip_grad_out = placed_out(skip_grad, 1).reshape(2, -1, width)
+
     both_low = by_batch(summed_low, other(summed_low)).reshape(batch * local_len, nk, eb)
-    both_grad = contract("tke,kde->td", ranked(both_low, 1, True), skip_all).reshape(batch, local_len, 2, width)
+    both_low = ranked(both_low, 1, True)
+    tok_grad, skip_rows_grad = [
+        contract("tke,kde->td", both_low, w).reshape(batch, local_len, width)
+        for w in (skip_all[:, :width], skip_all[:, width:])
+    ]
 
     def place(parts, size, half, total):
         out = jnp.zeros(parts[0].shape[:-1] + (total,), F32)
         at = out.ndim - 1
-        out = lax.dynamic_update_slice_in_dim(out, parts[0], y * half + k * size, at)
-        return lax.dynamic_update_slice_in_dim(out, parts[1], (1 - y) * half + k * size, at)
+        out = lax.dynamic_update_slice_in_dim(out, parts[0], k * size, at)
+        return lax.dynamic_update_slice_in_dim(out, parts[1], half + k * size, at)
 
     def everywhere(parts):
         flat = jnp.concatenate([p.reshape(-1) for p in parts])
+        flat = pin((flat, skip_part))[0]
         size = flat.shape[0]
         flat = jnp.pad(flat, (0, -size % 1024)).reshape(-1, 128)
         for axis_name in ("context", "tensor", "shard"):
@@ -429,17 +489,17 @@
 
     return (
         result_out,
-        both_grad[:, :, 0],
-        both_grad[:, :, 1],
+        tok_grad,
+        skip_rows_grad,
         text_grad,
         skip_grad_out,
         shift_grad_out,
-        columns_out(triple_grad, 3),
-        rows_out(small_grad[:, :, 4 * cb :]),
-        columns_out(small_grad[:, :, :cb], 1)[:, 0],
-        columns_out(small_grad[:, :, cb : 3 * cb], 2),
-        rows_out(small_grad[:, :, 3 * cb : 4 * cb]),
-        columns_out(up_grad, 1)[:, 0],
+        placed_out(triple_grad, 3),
+        rows_out(spread(small_grad[:, 4 * cb :].T)),
+        placed_out(small_grad[:, :cb], 1)[:, 0],
+        placed_out(small_grad[:, cb : 3 * cb], 2),
+        rows_out(spread(small_grad[:, 3 * cb : 4 * cb].T)),
+        wide_out(up_grad),
         rows_out(down_grad),
     ) + tuple(vectors[:7])
 

time: 1080 us -> 907 us (0.84)
  local copies, waits for them, and re-layouts: 209 us -> 138 us
  waiting for transfers between devices: 345 us -> 275 us
  starting transfers between devices: 77.7 us -> 59.7 us
    ppermute x14 -> x7, waiting for transfers between devices: 125 us -> 16.3 us  [other(): return lax.ppermute(values, 'tensor', swap)]
    ppermute x45 -> x51, waiting for transfers between devices: 189 us -> 207 us  [flip(): return lax.ppermute(values, axis_name, [(i, i ^ bit) for i in range(count)])]
    slice x3 -> x4, local copies, waits for them, and re-layouts: 18.6 us -> 2.47 us  [the longest x1 1.3 us: on_device(): small_grad[:, 3 * cb:4 * cb]]
    gather x8 -> x3, local copies, waits for them, and re-layouts: 19.3 us -> 5.41 us  [ranked(): jnp.take(values, where, axis=axis, indices_are_sorted=False, unique_indic...]
    reduce_sum x2, other arithmetic: 9.54 us -> 22.6 us  [attention_forward(): weight_sum = jnp.sum(exponent, -1, keepdims=True)]
    concatenate x23 -> x29, other arithmetic: 44.5 us -> 32 us  [the longest x13 17.9 us: gather_far(): values = jnp.concatenate([values, flip(values, 'context', bit)], 0)]
    ppermute x14 -> x7, starting transfers between devices: 18.1 us -> 6.07 us  [other(): return lax.ppermute(values, 'tensor', swap)]
    reshape x4 -> x1, local copies, waits for them, and re-layouts: 11.7 us -> 0.05 us  [on_device(): summed_block.reshape(nk, local_len, eb)]
  transfers between devices with their start and end apart: 73 -> 73, of which waited for: 29 -> 32; matrix products, arithmetic and copies ran while one was open for 52% -> 54% of each run, Pallas kernels for 0% -> 0%
where the time goes in v3:
time: 907 us; the launch traced here: 895 us
  waiting for transfers between devices  275 us (30%)
  matrix products  250 us (28%)
  other arithmetic  155 us (17%)
  local copies, waits for them, and re-layouts  138 us (15%)
  starting transfers between devices  59.7 us (7%)
  between operations  18.4 us (2%)
    ppermute x51, waiting for transfers between devices, flip(): return lax.ppermute(values, axis_name, [(i, i ^ bit) for i in range(count)])  207 us
    dot_general x21, matrix products, contract(): return jnp.einsum(form, left_side, right_side, preferred_element_type=F32)  74 us
    dot_general x17, matrix products, matmul(): return jnp.dot(left_side, right_side, preferred_element_type=F32)  64.4 us
    dot_general x16, matrix products, contract_rows(): lax.dot_general(left_side, right_side, (((0,), (0,)), ((), ())), preferre...  56 us
    dot_general x26, matrix products, contract_cols(): lax.dot_general(left_side, right_side, (((1,), (1,)), ((), ())), preferre...  54 us
    unnamed x512, local copies, waits for them, and re-layouts  48.8 us
    all_gather x4, waiting for transfers between devices, gathered(): return lax.all_gather(values, ('tensor', 'shard'), axis=0, tiled=True)  37.2 us
    ppermute x51, starting transfers between devices, flip(): return lax.ppermute(values, axis_name, [(i, i ^ bit) for i in range(count)])  37.2 us
  transfers between devices with their start and end apart: 73, of which 32 were waited for; matrix products, arithmetic and copies ran while one was open for 54% of the time, Pallas kernels for 0%

profile of v3, /device:TPU:0, one launch (start us, length us, event | category | flops | bytes accessed | tf_op | source)
XLA Modules:
  0.0 895.5 jit_solution(12190534217510308966)
XLA Ops:
  14.1 31.6 %collective-permute-done = bf16[256,2816]{1,0:T(8,128)(2,1)S(1)} collective-permute-done((bf16[256,2816]{1,0:T(8,128)(2,1)S(1)}, bf16[256,2816]{1,0:T(8,128)(2,1)S(1)}, u32[]{:S(2)}, u32[]{:S(2)}) %collective-permute-start) | collective-permute-done | bytes 1441824 | tf_op jit(solution)/shard_map/ppermute | solution.py:125
  51.8 5.1 all-to-all-start.1
  57.7 4.9 all-to-all-done.1
  90.1 8.6 all-to-all-done
  116.4 7.7 collective-permute-done.3
  133.6 5.4 all-gather.8.cloned.1.call-done
  139.0 4.3 convolution_add_fusion.15
  154.5 8.2 multiply_reduce_fusion.1
  162.8 21.6 %fusion = f32[4,1024]{1,0:T(4,128)S(1)} fusion(f32[4,1024,1024]{1,2,0:T(8,128)} %get-tuple-element.336, f32[4,1024]{1,0:T(4,128)S(1)} %get-tuple-element.335), kind=kLoop, calls=%fused_computation.9 | loop fusion | flops 12578816 | bytes 16809984 | tf_op jit(solution)/shard_map/reduce_sum | solution.py:66
  184.4 7.9 fusion.129
  200.5 17.6 %collective-permute-done.9 = bf16[256,1408]{1,0:T(8,128)(2,1)S(1)} collective-permute-done((bf16[256,1408]{1,0:T(8,128)(2,1)S(1)}, bf16[256,1408]{1,0:T(8,128)(2,1)S(1)}, u32[]{:S(2)}, u32[]{:S(2)}) %collective-permute-start.9) | collective-permute-done | bytes 720928 | tf_op jit(solution)/shard_map/ppermute | solution.py:125
  225.7 4.7 constant_dynamic-slice_fusion.7
  230.4 11.1 %collective-permute-done.10 = bf16[256,1408]{1,0:T(8,128)(2,1)} collective-permute-done((bf16[256,1408]{1,0:T(8,128)(2,1)S(1)}, bf16[256,1408]{1,0:T(8,128)(2,1)}, u32[]{:S(2)}, u32[]{:S(2)}) %collective-permute-start.10) | collective-permute-done | bytes 720928 | tf_op jit(solution)/shard_map/ppermute | solution.py:125
  276.2 17.5 %collective-permute-done.13 = bf16[256,1408]{1,0:T(8,128)(2,1)S(1)} collective-permute-done((bf16[256,1408]{1,0:T(8,128)(2,1)S(1)}, bf16[256,1408]{1,0:T(8,128)(2,1)S(1)}, u32[]{:S(2)}, u32[]{:S(2)}) %collective-permute-start.13) | collective-permute-done | bytes 720928 | tf_op jit(solution)/shard_map/ppermute | solution.py:125
  293.9 4.7 all-gather.12.cloned.1.call-done
  300.9 15.1 %collective-permute-done.15 = bf16[256,1408]{1,0:T(8,128)(2,1)S(1)} collective-permute-done((bf16[256,1408]{1,0:T(8,128)(2,1)S(1)}, bf16[256,1408]{1,0:T(8,128)(2,1)S(1)}, u32[]{:S(2)}, u32[]{:S(2)}) %collective-permute-start.15) | collective-permute-done | bytes 720928 | tf_op jit(solution)/shard_map/ppermute | solution.py:125
  326.6 4.1 copy.104
  332.2 8.3 multiply_convert_fusion.2
  340.6 6.4 multiply_convert_fusion.3
  347.0 27.1 %all-gather.14.cloned.1.call-done = bf16[2816,768]{1,0:T(8,128)(2,1)} async-done(((bf16[352,768]{1,0:T(8,128)(2,1)}), bf16[2816,768]{1,0:T(8,128)(2,1)}) %all-gather.14.cloned.1.call-update) | async-done | bytes 4325392 | tf_op jit(solution)/shard_map/all_gather | solution.py:167
  374.0 7.6 fusion.27
  381.7 6.5 fusion.20
  388.2 4.5 pad_maximum_fusion.4
  401.9 16.7 %collective-permute-done.19 = bf16[256,1408]{1,0:T(8,128)(2,1)S(1)} collective-permute-done((bf16[256,1408]{1,0:T(8,128)(2,1)S(1)}, bf16[256,1408]{1,0:T(8,128)(2,1)S(1)}, u32[]{:S(2)}, u32[]{:S(2)}) %collective-permute-start.19) | collective-permute-done | bytes 720928 | tf_op jit(solution)/shard_map/ppermute | solution.py:125
  423.7 15.9 %collective-permute-done.20 = bf16[256,1408]{1,0:T(8,128)(2,1)S(1)} collective-permute-done((bf16[256,1408]{1,0:T(8,128)(2,1)S(1)}, bf16[256,1408]{1,0:T(8,128)(2,1)S(1)}, u32[]{:S(2)}, u32[]{:S(2)}) %collective-permute-start.20) | collective-permute-done | bytes 720928 | tf_op jit(solution)/shard_map/ppermute | solution.py:125
  457.2 4.9 convolution_convert_fusion.2
  462.1 4.5 convolution_convert_fusion.3
  475.8 5.4 convolution_convert_fusion.1
  517.6 12.7 %collective-permute-done.23 = bf16[256,1408]{1,0:T(8,128)(2,1)S(1)} collective-permute-done((bf16[256,1408]{1,0:T(8,128)(2,1)S(1)}, bf16[256,1408]{1,0:T(8,128)(2,1)S(1)}, u32[]{:S(2)}, u32[]{:S(2)}) %collective-permute-start.23) | collective-permute-done | bytes 720928 | tf_op jit(solution)/shard_map/ppermute | solution.py:125
  541.0 10.6 %collective-permute-done.24 = bf16[256,1408]{1,0:T(8,128)(2,1)} collective-permute-done((bf16[256,1408]{1,0:T(8,128)(2,1)}, bf16[256,1408]{1,0:T(8,128)(2,1)}, u32[]{:S(2)}, u32[]{:S(2)}) %collective-permute-start.24) | collective-permute-done | bytes 720928 | tf_op jit(solution)/shard_map/ppermute | solution.py:125
  561.6 6.5 collective-permute-done.35
  584.4 5.2 select_convert_fusion
  597.4 13.9 %multiply_reduce_fusion = (f32[4,1024]{1,0:T(4,128)S(1)}, f32[4,1024,1024]{1,2,0:T(8,128)}) fusion(f32[4,1024,1024]{1,2,0:T(8,128)} %get-tuple-element.336, f32[4,1024]{1,0:T(4,128)S(1)} %log_add_fusion, bf16[1024,4,88]{0,2,1:T(8,128)(2,1)S(1)} %copy-done.54, bf16[1024,4,88]{0,2,1:T(8,128)(2,1)S(1)} %copy-done.99), kind=kOutput, calls=%fused_computation.5 | convolution fusion | flops 754970624 | bytes 35028992 | tf_op jit(solution)/shard_map/qhd,khd->hqk/dot_general | solution.py:18
  612.9 8.1 multiply_convert_fusion
  626.0 6.2 bitcast_multiply_fusion.2
  661.1 5.4 copy.116
  666.5 6.9 reshape.955
  684.8 4.2 fusion.31
  689.1 6.4 add_convert_fusion
  696.7 4.9 copy.128
  702.8 4.5 convolution_convert_fusion.4
  718.4 15.4 %collective-permute-done.31 = bf16[256,1408]{1,0:T(8,128)(2,1)S(1)} collective-permute-done((bf16[256,1408]{1,0:T(8,128)(2,1)S(1)}, bf16[256,1408]{1,0:T(8,128)(2,1)S(1)}, u32[]{:S(2)}, u32[]{:S(2)}) %collective-permute-start.31) | collective-permute-done | bytes 720928 | tf_op jit(solution)/shard_map/ppermute | solution.py:125
  735.1 7.5 collective-permute-done.32
  754.4 5.3 fusion.28
  791.8 4.6 reshape.1007
  803.4 8.6 collective-permute-done.41
  812.9 6.8 fusion.8
  821.4 6.4 fusion.10
  (1031 shorter events, 439.4 us)
Async XLA Ops:
  7.2 64.5 %all-gather.6.cloned.1.call-start = ((), (), s32[]{:S(2)}) async-start(), calls=%async_computation.10 | async-start | bytes 2433024 | tf_op jit(solution)/shard_map/all_gather | solution.py:189
  9.3 129.7 %all-gather.8.cloned.1.call-start = ((), (), s32[]{:S(2)}) async-start(), calls=%async_computation.11 | async-start | bytes 4866048 | tf_op jit(solution)/shard_map/all_gather | solution.py:167
  11.1 34.6 %collective-permute-start = (bf16[256,2816]{1,0:T(8,128)(2,1)S(1)}, bf16[256,2816]{1,0:T(8,128)(2,1)S(1)}, u32[]{:S(2)}, u32[]{:S(2)}) collective-permute-start(bf16[256,2816]{1,0:T(8,128)(2,1)S(1)} %pad_maximum_fusion.16), channel_id=1, source_target_pairs={{0,4},{2,6},{4,0},{6,2},{1,5},{3,7},{5,1},{7,3},{8,12},{10,14},{12... | collective-permute-start | bytes 4325384 | tf_op jit(solution)/shard_map/ppermute | solution.py:125
  47.5 26.2 %collective-permute-start.1 = (bf16[512,2816]{1,0:T(8,128)(2,1)}, bf16[512,2816]{1,0:T(8,128)(2,1)}, u32[]{:S(2)}, u32[]{:S(2)}) collective-permute-start(bf16[512,2816]{1,0:T(8,128)(2,1)} %pad_maximum_fusion.6), channel_id=1, source_target_pairs={{0,2},{2,0},{4,6},{6,4},{1,3},{3,1},{5,7},{7,5},{8,10},{10,8},{12,... | collective-permute-start | bytes 8650760 | tf_op jit(solution)/shard_map/ppermute | solution.py:125
  68.4 15.9 %all-to-all-start.2 = ((f32[4,1,1408]{2,1,0:T(1,128)}), f32[4,1,1408]{2,1,0:T(1,128)S(1)}, u32[]{:S(2)}, u32[]{:S(2)}) async-start(f32[4,1,1408]{2,1,0:T(1,128)} %all_to_all.32), calls=%async_computation.2 | async-start | bytes 45056 | tf_op jit(solution)/shard_map/all_to_all | solution.py:215
  84.4 14.4 %all-to-all-start = ((bf16[4,256,352]{1,2,0:T(8,128)(2,1)}), bf16[4,256,352]{1,2,0:T(8,128)(2,1)S(1)}, u32[]{:S(2)}, u32[]{:S(2)}) async-start(bf16[4,256,352]{1,2,0:T(8,128)(2,1)} %broadcast_select_fusion.8), calls=%async_computation | async-start | bytes 1441792 | tf_op jit(solution)/shard_map/all_to_all | solution.py:221
  87.9 131.9 %all-gather.10.cloned.1.call-start = ((), (), s32[]{:S(2)}) async-start(), calls=%async_computation.12 | async-start | bytes 4866048 | tf_op jit(solution)/shard_map/all_gather | solution.py:167
  106.3 17.8 %collective-permute-start.3 = (bf16[256,1408]{1,0:T(8,128)(2,1)S(1)}, bf16[256,1408]{1,0:T(8,128)(2,1)}, u32[]{:S(2)}, u32[]{:S(2)}) collective-permute-start(bf16[256,1408]{1,0:T(8,128)(2,1)S(1)} %add_convert_fusion.6), channel_id=1, source_target_pairs={{0,4},{2,6},{4,0},{6,2},{1,5},{3,7},{5,1},{7,3},{8,12},{10,14},{12... | collective-permute-start | bytes 2162696 | tf_op jit(solution)/shard_map/ppermute | solution.py:125
  107.0 22.7 %collective-permute-start.5 = (s32[256,2]{0,1:T(2,128)S(1)}, s32[256,2]{0,1:T(2,128)S(1)}, u32[]{:S(2)}, u32[]{:S(2)}) collective-permute-start(s32[256,2]{0,1:T(2,128)S(1)} %fusion.217), channel_id=1, source_target_pairs={{0,4},{2,6},{4,0},{6,2},{1,5},{3,7},{5,1},{7,3},{8,12},{10,14},{12... | collective-permute-start | bytes 6152 | tf_op jit(solution)/shard_map/ppermute | solution.py:125
  116.4 182.2 %all-gather.12.cloned.1.call-start = ((), (), s32[]{:S(2)}) async-start(), calls=%async_computation.13 | async-start | bytes 4866048 | tf_op jit(solution)/shard_map/all_gather | solution.py:167
  126.5 12.5 %collective-permute-start.4 = (bf16[512,1408]{1,0:T(8,128)(2,1)}, bf16[512,1408]{1,0:T(8,128)(2,1)}, u32[]{:S(2)}, u32[]{:S(2)}) collective-permute-start(bf16[512,1408]{1,0:T(8,128)(2,1)} %pad_maximum_fusion.17), channel_id=1, source_target_pairs={{0,2},{2,0},{4,6},{6,4},{1,3},{3,1},{5,7},{7,5},{8,10},{10,8},{12,... | collective-permute-start | bytes 4325384 | tf_op jit(solution)/shard_map/ppermute | solution.py:125
  153.0 39.4 %collective-permute-start.7 = (bf16[256,1408]{1,0:T(8,128)(2,1)S(1)}, bf16[256,1408]{1,0:T(8,128)(2,1)S(1)}, u32[]{:S(2)}, u32[]{:S(2)}) collective-permute-start(bf16[256,1408]{1,0:T(8,128)(2,1)S(1)} %get-tuple-element.54), channel_id=1, source_target_pairs={{0,4},{2,6},{4,0},{6,2},{1,5},{3,7},{5,1},{7,3},{8,12},{10,14},{12... | collective-permute-start | bytes 2162696 | tf_op jit(solution)/shard_map/ppermute | solution.py:125
  199.8 18.2 %collective-permute-start.9 = (bf16[256,1408]{1,0:T(8,128)(2,1)S(1)}, bf16[256,1408]{1,0:T(8,128)(2,1)S(1)}, u32[]{:S(2)}, u32[]{:S(2)}) collective-permute-start(bf16[256,1408]{1,0:T(8,128)(2,1)S(1)} %slice.969), channel_id=1, source_target_pairs={{0,4},{2,6},{4,0},{6,2},{1,5},{3,7},{5,1},{7,3},{8,12},{10,14},{12... | collective-permute-start | bytes 2162696 | tf_op jit(solution)/shard_map/ppermute | solution.py:125
  224.0 17.5 %collective-permute-start.10 = (bf16[256,1408]{1,0:T(8,128)(2,1)S(1)}, bf16[256,1408]{1,0:T(8,128)(2,1)}, u32[]{:S(2)}, u32[]{:S(2)}) collective-permute-start(bf16[256,1408]{1,0:T(8,128)(2,1)S(1)} %add_convert_fusion.5), channel_id=1, source_target_pairs={{0,4},{2,6},{4,0},{6,2},{1,5},{3,7},{5,1},{7,3},{8,12},{10,14},{12... | collective-permute-start | bytes 2162696 | tf_op jit(solution)/shard_map/ppermute | solution.py:125
  225.5 148.5 %all-gather.14.cloned.1.call-start = ((), (), s32[]{:S(2)}) async-start(), calls=%async_computation.14 | async-start | bytes 4866048 | tf_op jit(solution)/shard_map/all_gather | solution.py:167
  270.8 289.3 %reduce-scatter.19.cloned.1.call-start = ((), (), s32[]{:S(2)}) async-start(), calls=%async_computation.18 | async-start | bytes 1351680
  275.5 18.1 %collective-permute-start.13 = (bf16[256,1408]{1,0:T(8,128)(2,1)S(1)}, bf16[256,1408]{1,0:T(8,128)(2,1)S(1)}, u32[]{:S(2)}, u32[]{:S(2)}) collective-permute-start(bf16[256,1408]{1,0:T(8,128)(2,1)S(1)} %slice.968), channel_id=1, source_target_pairs={{0,4},{2,6},{4,0},{6,2},{1,5},{3,7},{5,1},{7,3},{8,12},{10,14},{12... | collective-permute-start | bytes 2162696 | tf_op jit(solution)/shard_map/ppermute | solution.py:125
  299.4 16.7 %collective-permute-start.15 = (bf16[256,1408]{1,0:T(8,128)(2,1)S(1)}, bf16[256,1408]{1,0:T(8,128)(2,1)S(1)}, u32[]{:S(2)}, u32[]{:S(2)}) collective-permute-start(bf16[256,1408]{1,0:T(8,128)(2,1)S(1)} %add_convert_fusion.4), channel_id=1, source_target_pairs={{0,4},{2,6},{4,0},{6,2},{1,5},{3,7},{5,1},{7,3},{8,12},{10,14},{12... | collective-permute-start | bytes 2162696 | tf_op jit(solution)/shard_map/ppermute | solution.py:125
  300.9 19.9 %collective-permute-start.14 = (bf16[512,1408]{1,0:T(8,128)(2,1)}, bf16[512,1408]{1,0:T(8,128)(2,1)}, u32[]{:S(2)}, u32[]{:S(2)}) collective-permute-start(bf16[512,1408]{1,0:T(8,128)(2,1)} %pad_maximum_fusion.18), channel_id=1, source_target_pairs={{0,2},{2,0},{4,6},{6,4},{1,3},{3,1},{5,7},{7,5},{8,10},{10,8},{12,... | collective-permute-start | bytes 4325384 | tf_op jit(solution)/shard_map/ppermute | solution.py:125
  330.7 57.4 %collective-permute-start.17 = (bf16[1,2816,352]{1,2,0:T(8,128)(2,1)}, bf16[1,2816,352]{1,2,0:T(8,128)(2,1)}, u32[]{:S(2)}, u32[]{:S(2)}) collective-permute-start(bf16[1,2816,352]{1,2,0:T(8,128)(2,1)} %bitcast.477), channel_id=1, source_target_pairs={{0,4},{2,6},{4,0},{6,2},{1,5},{3,7},{5,1},{7,3},{8,12},{10,14},{12... | collective-permute-start | bytes 5947400 | tf_op jit(solution)/shard_map/ppermute | solution.py:125
  400.4 18.2 %collective-permute-start.19 = (bf16[256,1408]{1,0:T(8,128)(2,1)S(1)}, bf16[256,1408]{1,0:T(8,128)(2,1)S(1)}, u32[]{:S(2)}, u32[]{:S(2)}) collective-permute-start(bf16[256,1408]{1,0:T(8,128)(2,1)S(1)} %slice.967), channel_id=1, source_target_pairs={{0,4},{2,6},{4,0},{6,2},{1,5},{3,7},{5,1},{7,3},{8,12},{10,14},{12... | collective-permute-start | bytes 2162696 | tf_op jit(solution)/shard_map/ppermute | solution.py:125
  422.3 17.3 %collective-permute-start.20 = (bf16[256,1408]{1,0:T(8,128)(2,1)S(1)}, bf16[256,1408]{1,0:T(8,128)(2,1)S(1)}, u32[]{:S(2)}, u32[]{:S(2)}) collective-permute-start(bf16[256,1408]{1,0:T(8,128)(2,1)S(1)} %get-tuple-element.186), channel_id=1, source_target_pairs={{0,4},{2,6},{4,0},{6,2},{1,5},{3,7},{5,1},{7,3},{8,12},{10,14},{12... | collective-permute-start | bytes 2162696 | tf_op jit(solution)/shard_map/ppermute | solution.py:125
  457.2 132.4 %reduce-scatter.13.cloned.1.call-start = ((), (), s32[]{:S(2)}) async-start(), calls=%async_computation.15 | async-start | bytes 4866048 | tf_op jit(solution)/shard_map/reduce_scatter | solution.py:312
  469.0 266.1 %reduce-scatter.15.cloned.1.call-start = ((), (), s32[]{:S(2)}) async-start(), calls=%async_computation.16 | async-start | bytes 4866048 | tf_op jit(solution)/shard_map/reduce_scatter | solution.py:312
  475.7 28.3 %collective-permute-start.34 = (bf16[2,2816,352]{1,2,0:T(8,128)(2,1)}, bf16[2,2816,352]{1,2,0:T(8,128)(2,1)}, u32[]{:S(2)}, u32[]{:S(2)}) collective-permute-start(bf16[2,2816,352]{1,2,0:T(8,128)(2,1)} %pad_maximum_fusion.4), channel_id=1, source_target_pairs={{0,2},{2,0},{4,6},{6,4},{1,3},{3,1},{5,7},{7,5},{8,10},{10,8},{12,... | collective-permute-start | bytes 11894792 | tf_op jit(solution)/shard_map/ppermute | solution.py:125
  501.2 339.4 %reduce-scatter.23.cloned.1.call-start = ((), (), s32[]{:S(2)}) async-start(), calls=%async_computation.20 | async-start | bytes 3153920
  511.9 18.4 %collective-permute-start.23 = (bf16[256,1408]{1,0:T(8,128)(2,1)S(1)}, bf16[256,1408]{1,0:T(8,128)(2,1)S(1)}, u32[]{:S(2)}, u32[]{:S(2)}) collective-permute-start(bf16[256,1408]{1,0:T(8,128)(2,1)S(1)} %slice.966), channel_id=1, source_target_pairs={{0,4},{2,6},{4,0},{6,2},{1,5},{3,7},{5,1},{7,3},{8,12},{10,14},{12... | collective-permute-start | bytes 2162696 | tf_op jit(solution)/shard_map/ppermute | solution.py:125
  533.8 17.9 %collective-permute-start.24 = (bf16[256,1408]{1,0:T(8,128)(2,1)}, bf16[256,1408]{1,0:T(8,128)(2,1)}, u32[]{:S(2)}, u32[]{:S(2)}) collective-permute-start(bf16[256,1408]{1,0:T(8,128)(2,1)} %get-tuple-element.188), channel_id=1, source_target_pairs={{0,4},{2,6},{4,0},{6,2},{1,5},{3,7},{5,1},{7,3},{8,12},{10,14},{12... | collective-permute-start | bytes 2162696 | tf_op jit(solution)/shard_map/ppermute | solution.py:125
  553.1 16.2 %collective-permute-start.25 = (bf16[512,1408]{1,0:T(8,128)(2,1)S(1)}, bf16[512,1408]{1,0:T(8,128)(2,1)}, u32[]{:S(2)}, u32[]{:S(2)}) collective-permute-start(bf16[512,1408]{1,0:T(8,128)(2,1)S(1)} %pad_maximum_fusion.23), channel_id=1, source_target_pairs={{0,2},{2,0},{4,6},{6,4},{1,3},{3,1},{5,7},{7,5},{8,10},{10,8},{12,... | collective-permute-start | bytes 4325384 | tf_op jit(solution)/shard_map/ppermute | solution.py:125
  589.6 56.6 %collective-permute-start.56 = (bf16[1,768,352]{1,2,0:T(8,128)(2,1)}, bf16[1,768,352]{1,2,0:T(8,128)(2,1)}, u32[]{:S(2)}, u32[]{:S(2)}) collective-permute-start(bf16[1,768,352]{1,2,0:T(8,128)(2,1)} %bitcast.551), channel_id=1, source_target_pairs={{0,4},{2,6},{4,0},{6,2},{1,5},{3,7},{5,1},{7,3},{8,12},{10,14},{12... | collective-permute-start | bytes 1622024 | tf_op jit(solution)/shard_map/ppermute | solution.py:125
  591.1 89.5 %collective-permute-start.29 = (bf16[1408,880]{0,1:T(8,128)(2,1)}, bf16[1408,880]{0,1:T(8,128)(2,1)}, u32[]{:S(2)}, u32[]{:S(2)}) collective-permute-start(bf16[1408,880]{0,1:T(8,128)(2,1)} %select_convert_fusion), channel_id=1, source_target_pairs={{0,1},{1,0},{2,3},{3,2},{4,5},{5,4},{6,7},{7,6},{8,9},{9,8},{10,11... | collective-permute-start | bytes 7434248 | tf_op jit(solution)/shard_map/ppermute | solution.py:118
  597.3 57.8 %collective-permute-start.26 = (bf16[512,1408]{1,0:T(8,128)(2,1)}, bf16[512,1408]{1,0:T(8,128)(2,1)}, u32[]{:S(2)}, u32[]{:S(2)}) collective-permute-start(bf16[512,1408]{1,0:T(8,128)(2,1)} %fusion.30), channel_id=1, source_target_pairs={{0,2},{2,0},{4,6},{6,4},{1,3},{3,1},{5,7},{7,5},{8,10},{10,8},{12,... | collective-permute-start | bytes 4325384 | tf_op jit(solution)/shard_map/ppermute | solution.py:125
  658.2 18.7 %collective-permute-start.27 = (bf16[256,1408]{1,0:T(8,128)(2,1)S(1)}, bf16[256,1408]{1,0:T(8,128)(2,1)}, u32[]{:S(2)}, u32[]{:S(2)}) collective-permute-start(bf16[256,1408]{1,0:T(8,128)(2,1)S(1)} %slice.965), channel_id=1, source_target_pairs={{0,4},{2,6},{4,0},{6,2},{1,5},{3,7},{5,1},{7,3},{8,12},{10,14},{12... | collective-permute-start | bytes 2162696 | tf_op jit(solution)/shard_map/ppermute | solution.py:125
  678.8 36.6 %collective-permute-start.28 = (bf16[256,1408]{1,0:T(8,128)(2,1)S(1)}, bf16[256,1408]{1,0:T(8,128)(2,1)}, u32[]{:S(2)}, u32[]{:S(2)}) collective-permute-start(bf16[256,1408]{1,0:T(8,128)(2,1)S(1)} %fusion.80), channel_id=1, source_target_pairs={{0,1},{1,0},{2,3},{3,2},{4,5},{5,4},{6,7},{7,6},{8,9},{9,8},{10,11... | collective-permute-start | bytes 2162696 | tf_op jit(solution)/shard_map/ppermute | solution.py:118
  689.0 22.3 %collective-permute-start.30 = (bf16[512,1408]{1,0:T(8,128)(2,1)}, bf16[512,1408]{1,0:T(8,128)(2,1)}, u32[]{:S(2)}, u32[]{:S(2)}) collective-permute-start(bf16[512,1408]{1,0:T(8,128)(2,1)} %fusion.31), channel_id=1, source_target_pairs={{0,2},{2,0},{4,6},{6,4},{1,3},{3,1},{5,7},{7,5},{8,10},{10,8},{12,... | collective-permute-start | bytes 4325384 | tf_op jit(solution)/shard_map/ppermute | solution.py:125
  707.3 35.3 %collective-permute-start.32 = (bf16[1408,528]{0,1:T(8,128)(2,1)}, bf16[1408,528]{0,1:T(8,128)(2,1)}, u32[]{:S(2)}, u32[]{:S(2)}) collective-permute-start(bf16[1408,528]{0,1:T(8,128)(2,1)} %convolution_convert_fusion.4), channel_id=1, source_target_pairs={{0,1},{1,0},{2,3},{3,2},{4,5},{5,4},{6,7},{7,6},{8,9},{9,8},{10,11... | collective-permute-start | bytes 4460552 | tf_op jit(solution)/shard_map/ppermute | solution.py:118
  715.2 18.6 %collective-permute-start.31 = (bf16[256,1408]{1,0:T(8,128)(2,1)S(1)}, bf16[256,1408]{1,0:T(8,128)(2,1)S(1)}, u32[]{:S(2)}, u32[]{:S(2)}) collective-permute-start(bf16[256,1408]{1,0:T(8,128)(2,1)S(1)} %slice.964), channel_id=1, source_target_pairs={{0,4},{2,6},{4,0},{6,2},{1,5},{3,7},{5,1},{7,3},{8,12},{10,14},{12... | collective-permute-start | bytes 2162696 | tf_op jit(solution)/shard_map/ppermute | solution.py:125
  750.1 35.0 %collective-permute-start.33 = (bf16[256,1408]{1,0:T(8,128)(2,1)S(1)}, bf16[256,1408]{1,0:T(8,128)(2,1)}, u32[]{:S(2)}, u32[]{:S(2)}) collective-permute-start(bf16[256,1408]{1,0:T(8,128)(2,1)S(1)} %get-tuple-element.190), channel_id=1, source_target_pairs={{0,1},{1,0},{2,3},{3,2},{4,5},{5,4},{6,7},{7,6},{8,9},{9,8},{10,11... | collective-permute-start | bytes 2162696 | tf_op jit(solution)/shard_map/ppermute | solution.py:118
  750.4 15.3 %all-to-all-start.3 = ((bf16[256,4,352]{0,2,1:T(8,128)(2,1)}), bf16[256,4,352]{0,2,1:T(8,128)(2,1)S(1)}, u32[]{:S(2)}, u32[]{:S(2)}) async-start(bf16[256,4,352]{0,2,1:T(8,128)(2,1)} %bitcast.102), calls=%async_computation.5 | async-start | bytes 1441792 | tf_op jit(solution)/shard_map/all_to_all | solution.py:420
  753.9 101.8 %reduce-scatter.21.cloned.1.call-start = ((), (), s32[]{:S(2)}) async-start(), calls=%async_computation.19 | async-start | bytes 2252800
  763.4 14.8 %collective-permute-start.54 = (bf16[1,352,768]{2,1,0:T(8,128)(2,1)S(1)}, bf16[1,352,768]{2,1,0:T(8,128)(2,1)}, u32[]{:S(2)}, u32[]{:S(2)}) collective-permute-start(bf16[1,352,768]{2,1,0:T(8,128)(2,1)S(1)} %bitcast.550), channel_id=1, source_target_pairs={{0,4},{2,6},{4,0},{6,2},{1,5},{3,7},{5,1},{7,3},{8,12},{10,14},{12... | collective-permute-start | bytes 1622024 | tf_op jit(solution)/shard_map/ppermute | solution.py:125
  765.4 104.5 %reduce-scatter.17.cloned.1.call-start = ((), (), s32[]{:S(2)}) async-start(), calls=%async_computation.17 | async-start | bytes 1351680 | tf_op jit(solution)/shard_map/reduce_scatter | solution.py:428
  780.6 58.5 %collective-permute-start.55 = (bf16[2,352,768]{2,1,0:T(8,128)(2,1)}, bf16[2,352,768]{2,1,0:T(8,128)(2,1)}, u32[]{:S(2)}, u32[]{:S(2)}) collective-permute-start(bf16[2,352,768]{2,1,0:T(8,128)(2,1)} %pad_maximum_fusion.26), channel_id=1, source_target_pairs={{0,2},{2,0},{4,6},{6,4},{1,3},{3,1},{5,7},{7,5},{8,10},{10,8},{12,... | collective-permute-start | bytes 3244040 | tf_op jit(solution)/shard_map/ppermute | solution.py:125
  781.7 54.8 %collective-permute-start.36 = (bf16[2,4,176,352]{3,2,1,0:T(8,128)(2,1)}, bf16[2,4,176,352]{3,2,1,0:T(8,128)(2,1)}, u32[]{:S(2)}, u32[]{:S(2)}) collective-permute-start(bf16[2,4,176,352]{3,2,1,0:T(8,128)(2,1)} %dynamic-slice_bitcast_fusion), channel_id=1, source_target_pairs={{0,1},{1,0},{2,3},{3,2},{4,5},{5,4},{6,7},{7,6},{8,9},{9,8},{10,11... | collective-permute-start | bytes 2973704 | tf_op jit(solution)/shard_map/ppermute | solution.py:118
  790.2 21.8 %collective-permute-start.41 = (f32[352,128]{1,0:T(8,128)S(1)}, f32[352,128]{1,0:T(8,128)S(1)}, u32[]{:S(2)}, u32[]{:S(2)}) collective-permute-start(f32[352,128]{1,0:T(8,128)S(1)} %fusion.352), channel_id=1, source_target_pairs={{0,1},{1,0},{2,3},{3,2},{4,5},{5,4},{6,7},{7,6},{8,9},{9,8},{10,11... | collective-permute-start | bytes 540680 | tf_op jit(solution)/shard_map/ppermute | solution.py:125
  851.3 12.2 %collective-permute-start.49 = (bf16[2,352,176]{1,2,0:T(8,128)(2,1)}, bf16[2,352,176]{1,2,0:T(8,128)(2,1)}, u32[]{:S(2)}, u32[]{:S(2)}) collective-permute-start(bf16[2,352,176]{1,2,0:T(8,128)(2,1)} %pad_maximum_fusion.39), channel_id=1, source_target_pairs={{0,2},{2,0},{4,6},{6,4},{1,3},{3,1},{5,7},{7,5},{8,10},{10,8},{12,... | collective-permute-start | bytes 743432 | tf_op jit(solution)/shard_map/ppermute | solution.py:125
  857.0 11.9 %collective-permute-start.44 = (bf16[1,352,528]{1,2,0:T(8,128)(2,1)S(1)}, bf16[1,352,528]{1,2,0:T(8,128)(2,1)S(1)}, u32[]{:S(2)}, u32[]{:S(2)}) collective-permute-start(bf16[1,352,528]{1,2,0:T(8,128)(2,1)S(1)} %bitcast.488), channel_id=1, source_target_pairs={{0,4},{2,6},{4,0},{6,2},{1,5},{3,7},{5,1},{7,3},{8,12},{10,14},{12... | collective-permute-start | bytes 1115144 | tf_op jit(solution)/shard_map/ppermute | solution.py:125
  859.7 11.8 %collective-permute-start.51 = (bf16[2,352,352]{1,2,0:T(8,128)(2,1)}, bf16[2,352,352]{1,2,0:T(8,128)(2,1)}, u32[]{:S(2)}, u32[]{:S(2)}) collective-permute-start(bf16[2,352,352]{1,2,0:T(8,128)(2,1)} %pad_maximum_fusion.35), channel_id=1, source_target_pairs={{0,2},{2,0},{4,6},{6,4},{1,3},{3,1},{5,7},{7,5},{8,10},{10,8},{12,... | collective-permute-start | bytes 1486856 | tf_op jit(solution)/shard_map/ppermute | solution.py:125
  (272 other events, 2969.2 us)
Sparse Core Ops, SparseCore 0:
  10.8 52.5 all-gather.5
  66.0 72.8 all-gather.7
  141.6 72.8 all-gather.9
  225.6 72.9 all-gather.11
  301.1 72.9 all-gather.13
  457.3 23.4 reduce-scatter.18
  485.0 90.2 reduce-scatter.12
  579.4 103.0 reduce-scatter.14
  707.7 49.2 reduce-scatter.22
  765.5 37.5 reduce-scatter.20
  839.2 27.9 reduce-scatter.16

commit v4 on v3

--- a/solution.py
+++ b/solution.py
@@ -117,6 +117,7 @@
     def other(values):
         return lax.ppermute(values, "tensor", swap)
 
+    pin = lax.optimization_barrier
     bits = [1 << i for i in range(nk.bit_length() - 1)]
     relative = jnp.arange(nk) ^ k
 
@@ -141,7 +142,7 @@
         where = (jnp.asarray(order) ^ k) if back else jnp.asarray(order)[relative]
         return jnp.take(values, where, axis=axis, indices_are_sorted=False, unique_indices=True)
 
-    def scatter_rows(pieces):
+    def partial_rows(pieces):
         half = pieces[0][0].shape[0] // 2
 
         def part(first):
@@ -151,12 +152,26 @@
                 total = now if total is None else total + now
             return total
 
-        sent = flip(part(False).astype(BF), "context", bits[0])
-        total = part(True) + sent.astype(F32)
+        return part(False).astype(BF), part(True)
+
+    def sum_rows(sent, total, fill=()):
+        total = total + flip(sent, "context", bits[0]).astype(F32)
         for bit in bits[1:]:
             half = total.shape[0] // 2
-            total = total[:half] + flip(total[half:].astype(BF), "context", bit).astype(F32)
-        return total
+            got = flip(total[half:].astype(BF), "context", bit)
+            got, fill = pin((got, fill))
+            total = total[:half] + got.astype(F32)
+        return total, fill
+
+    def scatter_rows(pieces):
+        return sum_rows(*partial_rows(pieces))[0]
+
+    def gather_filled(values, fill):
+        for bit in reversed(bits[1:]):
+            got = flip(values, "context", bit)
+            got, fill = pin((got, fill))
+            values = jnp.concatenate([values, got], 0)
+        return gather_near(values), fill
 
     def by_batch(own, theirs):
         first = jnp.where(y == 0, own, theirs)
@@ -169,7 +184,6 @@
     def halves(values):
         return (values[:width], values[width:])
 
-    pin = lax.optimization_barrier
     first_part = jnp.concatenate(
         [
             block(triple_weight, cb, 2).reshape(rows_z, 3 * cb),
@@ -215,7 +229,8 @@
     shift_row = jnp.sum(lax.all_to_all(shift_part, "shard", 0, 0, tiled=True), 0) + width_biases[1]
 
     tok_here = gather_far(jnp.concatenate([tok_rows, skip_rows], 1))
-    tok_halves = pin((tok_here, flip(tok_here, "context", bits[0])))
+    tok_halves = (tok_here, flip(tok_here, "context", bits[0]))
+    tok_halves, text_rows = pin((tok_halves, text_rows))
     summed_block = jnp.concatenate([matmul(t, skip_block).astype(BF) for t in tok_halves], 0)
     summed_block = ranked(summed_block.reshape(nk, local_len, eb)).reshape(length, eb)
     summed = lax.all_to_all(summed_block, "context", split_axis=0, concat_axis=1, tiled=True).astype(F32) + width_biases[0]
@@ -307,8 +322,10 @@
         act, pull = jax.vjp(gelu_piece, matmul(normed_three_all, w) + b)
         active.append(act.astype(BF))
         pull_gelu.append(pull)
-    def reduced(parts):
-        total = jnp.concatenate([p.astype(BF) for p in parts], 0)
+    def stacked(parts):
+        return jnp.concatenate([p.astype(BF) for p in parts], 0)
+
+    def reduced(total):
         return lax.psum_scatter(total, ("tensor", "shard"), scatter_dimension=0, tiled=True)
 
     def own_first(parts):
@@ -335,14 +352,10 @@
     def columns_out(values, count):
         return by_rank(spread(values), count).astype(F32)
 
-    def placed_out(values, count):
-        got = gather_rows(values[None])
-        size = values.shape[1] // count
+    def placed_out(got, size, first, count, form="prn,pnm->rm"):
         source = ((jnp.asarray(order) ^ k)[:, None] * size + jnp.arange(size)).astype(jnp.int32)
         select = (source[:, :, None] == jnp.arange(nk * size)).astype(BF)
-        return jnp.stack(
-            [contract("prn,pnm->rm", got[:, :, i * size : (i + 1) * size], select) for i in range(count)], 1
-        )
+        return [contract(form, got[:, :, i * size : (i + 1) * size], select) for i in range(first, first + count)]
 
     def rows_out(values):
         depth = len(bits)
@@ -356,104 +369,125 @@
 
     cot_all = gather_near(cot_far)
     grad_out = cot_rows.astype(F32)
-    down_grad = reduced([contract_rows(cot_all, a) for a in active]).T
+    down_sum = stacked([contract_rows(cot_all, a) for a in active])
+    result_parts = partial_rows([(active[0], down_full[0], contract_cols), (active[1], down_full[1], contract_cols)])
     hidden_grad = [pull(matmul(cot_all, w))[0].astype(BF) for pull, w in zip(pull_gelu, down_full)]
     hidden_grad[0], hidden_grad[1], skip_far = pin((hidden_grad[0], hidden_grad[1], skip_far))
     skip_all = gather_near(skip_far)
-    up_grad = reduced([contract_rows(normed_three_all, h) for h in hidden_grad])
-    third_grads = pull_third(
-        scatter_rows([(hidden_grad[0], up_full[0], contract_cols), (hidden_grad[1], up_full[1], contract_cols)])
-    )
+    up_sum = stacked([contract_rows(normed_three_all, h) for h in hidden_grad])
+    third_back = partial_rows([(hidden_grad[0], up_full[0], contract_cols), (hidden_grad[1], up_full[1], contract_cols)])
+    third_back, result_parts = sum_rows(*third_back, result_parts)
+    third_grads = pull_third(third_back)
     resid_two_grad = grad_out + third_grads[0]
     grad_two_low = resid_two_grad.astype(BF)
     grad_two_all = gather_rows(grad_two_low)
-    cross_out_grad = [contract_rows(grad_two_all, p) for p in cross_parts]
+    down_grad = reduced(down_sum).T
+    cross_out_grad = [contract_rows(grad_two_all, p).astype(BF) for p in cross_parts]
     cross_mix_grad = to_heads([matmul(grad_two_all, w).astype(BF) for w in cross_out_full], 1)[:, 0]
     cq_back, ck_back, cv_back = attention_backward(cq, ck, cv, cross_sums, cross_mix_grad)
     cross_grads = pull_cross((cq_back, ck_back, cv_back))
     cross_grad_low = from_heads(cross_grads[0].astype(BF))
     pair_low = from_heads(cross_grads[1].astype(BF))
-    cross_q_grad = [contract_rows(normed_two_all, g) for g in cross_grad_low]
-    cross_kv_grad = [contract_rows(text_rows, g) for g in pair_low]
+    cross_q_grad = [contract_rows(normed_two_all, g).astype(BF) for g in cross_grad_low]
+    cross_kv_grad = [contract_rows(text_rows, g).astype(BF) for g in pair_low]
     text_part = contract_cols(pair_low[0], cross_kv_full[0]) + contract_cols(pair_low[1], cross_kv_full[1])
-    text_part = lax.psum_scatter(text_part.astype(BF), "context", scatter_dimension=1, tiled=True)
+    second_back = partial_rows(
+        [(cross_grad_low[0], cross_q_full[0], contract_cols), (cross_grad_low[1], cross_q_full[1], contract_cols)]
+    )
+    second_back = sum_rows(*second_back)[0]
+    text_part, up_grad = pin((text_part.astype(BF), reduced(up_sum)))
+    text_part = lax.psum_scatter(text_part, "context", scatter_dimension=1, tiled=True)
     text_cols = text_part.shape[1] // ny
-    text_mine = lax.dynamic_slice_in_dim(text_part, y * text_cols, text_cols, 1)
-    text_theirs = other(lax.dynamic_slice_in_dim(text_part, (1 - y) * text_cols, text_cols, 1))
-    text_grad = by_batch(text_mine, text_theirs).astype(F32)
-    second_grads = pull_second(
-        scatter_rows([(cross_grad_low[0], cross_q_full[0], contract_cols), (cross_grad_low[1], cross_q_full[1], contract_cols)])
-    )
+    second_grads = pull_second(second_back)
     resid_one_grad = resid_two_grad + second_grads[0]
     grad_one_low = resid_one_grad.astype(BF)
-    grad_one_all = gather_rows(grad_one_low)
-    self_out_grad = [contract_rows(grad_one_all, p) for p in mix_parts]
+    grad_one_all, (cross_q_grad, cross_kv_grad, cross_out_grad) = gather_filled(
+        grad_one_low, (cross_q_grad, cross_kv_grad, cross_out_grad)
+    )
+    self_out_grad = [contract_rows(grad_one_all, p).astype(BF) for p in mix_parts]
     small_grad = [jnp.concatenate(g, 1) for g in zip(cross_q_grad, cross_kv_grad, cross_out_grad, self_out_grad)]
     small_grad = own_first(small_grad)
     mix_grad = to_heads([matmul(grad_one_all, w).astype(BF) for w in self_out_full], 1)[:, 0]
-    mix_grad, small_low, down_grad, active[0], active[1] = pin(
-        (mix_grad, small_grad[1].astype(BF), down_grad, active[0], active[1])
-    )
+    mix_grad, small_low, down_grad, result_parts = pin((mix_grad, small_grad[1], down_grad, result_parts))
+    small_low = other(small_low)
     down_grad = spread(down_grad)
-    small_low = other(small_low)
-    result = resid_two + (
-        scatter_rows([(active[0], down_full[0], contract_cols), (active[1], down_full[1], contract_cols)]) + width_biases[4]
-    )
+    result = resid_two + (sum_rows(*result_parts)[0] + width_biases[4])
     result_low = result.astype(BF)
-    result_out = by_batch(result_low, other(result_low)).astype(F32)
     q_back, k_back, v_back = attention_backward(query, key, value, self_sums, mix_grad)
     q_back, k_back, v_back = q_back.astype(BF), k_back.astype(BF), v_back.astype(BF)
     self_grads = pull_self(
         (q_back.astype(F32), k_back.astype(F32), v_back.astype(F32))
     )
-    triple_raw, small_low = pin((self_grads[0].astype(BF), small_low))
-    small_grad = over_shard(small_grad[0], small_low)
+    triple_raw, small_low, up_grad = pin((self_grads[0].astype(BF), small_low, up_grad))
+    small_grad = over_shard(small_grad[0].astype(F32), small_low)
     triple_low = from_heads(triple_raw)
     triple_grad = [contract_rows(normed_one_all, g) for g in own_first(triple_low)]
     triple_got = other(triple_grad[1].astype(BF))
     normed_grad = scatter_rows([(triple_low[0], triple_full[0], contract_cols), (triple_low[1], triple_full[1], contract_cols)])
-    normed_grad, triple_got, up_grad = pin((normed_grad, triple_got, up_grad))
-    up_grad = spread(up_grad)
-    triple_grad = over_shard(triple_grad[0], triple_got)
+    normed_grad, triple_got = pin((normed_grad, triple_got))
     first_grads = pull_first((resid_one_grad, normed_grad))
     summed_low = first_grads[0].astype(BF)
+    triple_grad = over_shard(triple_grad[0], triple_got)
     summed_cols = lax.all_to_all(summed_low, "context", split_axis=1, concat_axis=0, tiled=True)
     summed_cols = ranked(summed_cols.reshape(nk, local_len, eb), 0, True).reshape(length, eb)
     skip_part = contract_rows(tok_halves[0], summed_cols[: length // 2]) + contract_rows(tok_halves[1], summed_cols[length // 2 :])
-    skip_part = pin(skip_part.astype(BF)).reshape(2, nz, ny, -1, eb)
+    skip_part, text_part, down_grad, result_low, up_grad, summed_late = pin(
+        (skip_part.astype(BF), text_part, down_grad, result_low, up_grad, summed_low)
+    )
+    up_grad = spread(up_grad)
+    text_mine = lax.dynamic_slice_in_dim(text_part, y * text_cols, text_cols, 1)
+    skip_part = skip_part.reshape(2, nz, ny, -1, eb)
     keep = lax.dynamic_index_in_dim(skip_part, y, 2, keepdims=False)
     give = lax.dynamic_index_in_dim(skip_part, 1 - y, 2, keepdims=False)
     skip_total = (keep.astype(F32) + other(give).astype(F32)).astype(BF)
+    skip_total, small_grad, triple_grad, result_low = pin((skip_total, small_grad, triple_grad, result_low))
+    small_all = gather_rows(small_grad[None])
+    result_out = by_batch(result_low, other(result_low)).astype(F32)
+    text_theirs = other(lax.dynamic_slice_in_dim(text_part, (1 - y) * text_cols, text_cols, 1))
+    text_grad = by_batch(text_mine, text_theirs).astype(F32)
     skip_total = jnp.transpose(skip_total, (1, 0, 2, 3)).reshape(-1, eb)
+
+    both_low = by_batch(summed_late, other(summed_late)).reshape(batch * local_len, nk, eb)
     skip_grad = lax.psum_scatter(skip_total, "shard", scatter_dimension=0, tiled=True)
-    skip_grad_out = placed_out(skip_grad, 1).reshape(2, -1, width)
-
-    both_low = by_batch(summed_low, other(summed_low)).reshape(batch * local_len, nk, eb)
+    triple_all = gather_rows(triple_grad[None])
     both_low = ranked(both_low, 1, True)
     tok_grad, skip_rows_grad = [
         contract("tke,kde->td", both_low, w).reshape(batch, local_len, width)
         for w in (skip_all[:, :width], skip_all[:, width:])
     ]
 
+    triple_out = jnp.stack(placed_out(triple_all, cb, 0, 3), 1)
+    small_out = (
+        placed_out(small_all, cb, 4, 1, "prn,pnm->mr")[0],
+        placed_out(small_all, cb, 0, 1)[0],
+        jnp.stack(placed_out(small_all, cb, 1, 2), 1),
+        placed_out(small_all, cb, 3, 1, "prn,pnm->mr")[0],
+    )
+
     def place(parts, size, half, total):
         out = jnp.zeros(parts[0].shape[:-1] + (total,), F32)
         at = out.ndim - 1
         out = lax.dynamic_update_slice_in_dim(out, parts[0], k * size, at)
         return lax.dynamic_update_slice_in_dim(out, parts[1], half + k * size, at)
 
-    def everywhere(parts):
+    def everywhere(parts, fills):
         flat = jnp.concatenate([p.reshape(-1) for p in parts])
-        flat = pin((flat, skip_part))[0]
+        flat = pin((flat, skip_total))[0]
         size = flat.shape[0]
         flat = jnp.pad(flat, (0, -size % 1024)).reshape(-1, 128)
-        for axis_name in ("context", "tensor", "shard"):
-            for i in range(lax.axis_size(axis_name).bit_length() - 1):
-                flat = flat + flip(flat, axis_name, 1 << i)
+        stages = [(a, 1 << i) for a in ("context", "tensor", "shard") for i in range(lax.axis_size(a).bit_length() - 1)]
+        fills = list(fills)
+        for at, (axis_name, bit) in enumerate(stages):
+            got = flip(flat, axis_name, bit)
+            slot = at - len(stages) + len(fills)
+            if slot >= 0:
+                got, fills[slot] = pin((got, fills[slot]))
+            flat = flat + got
         flat, out, at = flat.reshape(-1), [], 0
         for p in parts:
             out.append(flat[at : at + p.size].reshape(p.shape))
             at += p.size
-        return out
+        return out, fills
 
     def col_sums(values, count=1):
         return jnp.sum(values.astype(F32), 0).reshape(count, -1)
@@ -480,9 +514,12 @@
     shift_slots = lax.dynamic_update_slice_in_dim(
         jnp.zeros((sequences, width), F32), first_grads[1][None], z * ny + y, 0
     )
-    vectors = everywhere(
-        (gains_grad, biases_grad, head_gain_grad, head_bias_grad, width_grad, column_grad, hidden_grad_sum, shift_slots)
-    )
+    vectors, fills = everywhere(
+        (gains_grad, biases_grad, head_gain_grad, head_bias_grad, width_grad, column_grad, hidden_grad_sum, shift_slots),
+        (tok_grad, skip_rows_grad, (triple_out, small_out)),
+    )
+    tok_grad, skip_rows_grad, (triple_out, small_out) = fills
+    skip_grad_out = placed_out(gather_rows(skip_grad[None]), eb, 0, 1)[0].reshape(2, -1, width)
     shift_grad_out = lax.dot_general(
         silu_rows.astype(F32), vectors[7], (((0,), (0,)), ((), ())), precision=lax.Precision.HIGHEST
     )
@@ -494,11 +531,8 @@
         text_grad,
         skip_grad_out,
         shift_grad_out,
-        placed_out(triple_grad, 3),
-        rows_out(spread(small_grad[:, 4 * cb :].T)),
-        placed_out(small_grad[:, :cb], 1)[:, 0],
-        placed_out(small_grad[:, cb : 3 * cb], 2),
-        rows_out(spread(small_grad[:, 3 * cb : 4 * cb].T)),
+        triple_out,
+        *small_out,
         wide_out(up_grad),
         rows_out(down_grad),
     ) + tuple(vectors[:7])

time: 907 us -> 875 us (0.965)
  waiting for transfers between devices: 275 us -> 252 us
  matrix products: 250 us -> 235 us
    ppermute x51 -> x45, waiting for transfers between devices: 207 us -> 193 us  [flip(): return lax.ppermute(values, axis_name, [(i, i ^ bit) for i in range(count)])]
    reduce_sum x2, other arithmetic: 22.6 us -> 9.71 us  [attention_forward(): weight_sum = jnp.sum(exponent, -1, keepdims=True)]
    dot_general x26, matrix products: 54 us -> 43.8 us  [contract_cols(): lax.dot_general(left_side, right_side, (((1,), (1,)), ((), ())), preferre...]
    dot_general x21 -> x23, matrix products: 74 us -> 79.4 us  [contract(): return jnp.einsum(form, left_side, right_side, preferred_element_type=F32)]
    ppermute x51 -> x45, starting transfers between devices: 37.2 us -> 34 us  [flip(): return lax.ppermute(values, axis_name, [(i, i ^ bit) for i in range(count)])]
    unnamed x512 -> x513, local copies, waits for them, and re-layouts: 48.8 us -> 48.5 us
  transfers between devices with their start and end apart: 73 -> 67, of which waited for: 32 -> 29; matrix products, arithmetic and copies ran while one was open for 54% -> 56% of each run, Pallas kernels for 0% -> 0%
where the time goes in v4:
time: 875 us; the launch traced here: 865 us
  waiting for transfers between devices  252 us (29%)
  matrix products  235 us (27%)
  other arithmetic  155 us (18%)
  local copies, waits for them, and re-layouts  147 us (17%)
  starting transfers between devices  58.1 us (7%)
  between operations  18.4 us (2%)
    ppermute x45, waiting for transfers between devices, flip(): return lax.ppermute(values, axis_name, [(i, i ^ bit) for i in range(count)])  193 us
    dot_general x23, matrix products, contract(): return jnp.einsum(form, left_side, right_side, preferred_element_type=F32)  79.4 us
    dot_general x17, matrix products, matmul(): return jnp.dot(left_side, right_side, preferred_element_type=F32)  61.7 us
    dot_general x16, matrix products, contract_rows(): lax.dot_general(left_side, right_side, (((0,), (0,)), ((), ())), preferre...  48.6 us
    unnamed x513, local copies, waits for them, and re-layouts  48.5 us
    dot_general x26, matrix products, contract_cols(): lax.dot_general(left_side, right_side, (((1,), (1,)), ((), ())), preferre...  43.8 us
    all_gather x4, waiting for transfers between devices, gathered(): return lax.all_gather(values, ('tensor', 'shard'), axis=0, tiled=True)  35.7 us
    ppermute x45, starting transfers between devices, flip(): return lax.ppermute(values, axis_name, [(i, i ^ bit) for i in range(count)])  34 us
  transfers between devices with their start and end apart: 67, of which 29 were waited for; matrix products, arithmetic and copies ran while one was open for 56% of the time, Pallas kernels for 0%

profile of v4, /device:TPU:0, one launch (start us, length us, event | category | flops | bytes accessed | tf_op | source)
XLA Modules:
  0.0 865.2 jit_solution(18277177301361291784)
XLA Ops:
  14.8 31.6 %collective-permute-done = bf16[256,2816]{1,0:T(8,128)(2,1)S(1)} collective-permute-done((bf16[256,2816]{1,0:T(8,128)(2,1)S(1)}, bf16[256,2816]{1,0:T(8,128)(2,1)S(1)}, u32[]{:S(2)}, u32[]{:S(2)}) %collective-permute-start) | collective-permute-done | bytes 1441824 | tf_op jit(solution)/shard_map/ppermute | solution.py:126
  48.7 5.2 all-to-all-start.1
  58.3 4.7 constant_dynamic-slice_fusion.15
  69.2 5.1 all-to-all-start.2
  92.7 8.4 all-to-all-done
  118.8 7.7 collective-permute-done.3
  139.2 4.3 convolution_add_fusion.15
  154.7 8.2 multiply_reduce_fusion.1
  163.0 8.8 %fusion = f32[4,1024]{1,0:T(4,128)S(1)} fusion(f32[4,1024,1024]{1,2,0:T(8,128)} %get-tuple-element.389, f32[4,1024]{1,0:T(4,128)S(1)} %get-tuple-element.388), kind=kLoop, calls=%fused_computation.9 | loop fusion | flops 12578816 | bytes 16809984 | tf_op jit(solution)/shard_map/reduce_sum | solution.py:66
  171.8 8.4 fusion.131
  188.3 17.6 %collective-permute-done.10 = bf16[256,1408]{1,0:T(8,128)(2,1)S(1)} collective-permute-done((bf16[256,1408]{1,0:T(8,128)(2,1)S(1)}, bf16[256,1408]{1,0:T(8,128)(2,1)S(1)}, u32[]{:S(2)}, u32[]{:S(2)}) %collective-permute-start.10) | collective-permute-done | bytes 720928 | tf_op jit(solution)/shard_map/ppermute | solution.py:126
  207.7 7.1 all-gather.12.cloned.1.call-done
  221.1 14.2 %collective-permute-done.11 = bf16[256,1408]{1,0:T(8,128)(2,1)} collective-permute-done((bf16[256,1408]{1,0:T(8,128)(2,1)S(1)}, bf16[256,1408]{1,0:T(8,128)(2,1)}, u32[]{:S(2)}, u32[]{:S(2)}) %collective-permute-start.11) | collective-permute-done | bytes 720928 | tf_op jit(solution)/shard_map/ppermute | solution.py:126
  269.6 14.6 %collective-permute-done.14 = bf16[256,1408]{1,0:T(8,128)(2,1)S(1)} collective-permute-done((bf16[256,1408]{1,0:T(8,128)(2,1)S(1)}, bf16[256,1408]{1,0:T(8,128)(2,1)S(1)}, u32[]{:S(2)}, u32[]{:S(2)}) %collective-permute-start.14) | collective-permute-done | bytes 720928 | tf_op jit(solution)/shard_map/ppermute | solution.py:126
  287.2 5.8 all-gather.14.cloned.1.call-done
  299.4 12.2 %collective-permute-done.15 = bf16[256,1408]{1,0:T(8,128)(2,1)} collective-permute-done((bf16[256,1408]{1,0:T(8,128)(2,1)}, bf16[256,1408]{1,0:T(8,128)(2,1)}, u32[]{:S(2)}, u32[]{:S(2)}) %collective-permute-start.15) | collective-permute-done | bytes 720928 | tf_op jit(solution)/shard_map/ppermute | solution.py:126
  322.3 4.1 copy.102
  327.8 7.6 multiply_convert_fusion.2
  338.0 4.7 multiply_convert_fusion.3
  348.9 19.6 %all-gather.10.cloned.1.call-done = bf16[2816,768]{1,0:T(8,128)(2,1)} async-done(((bf16[352,768]{1,0:T(8,128)(2,1)}), bf16[2816,768]{1,0:T(8,128)(2,1)}) %all-gather.10.cloned.1.call-update) | async-done | bytes 4325392 | tf_op jit(solution)/shard_map/all_gather | solution.py:182
  368.5 7.6 fusion.27
  380.3 4.4 pad_maximum_fusion.2
  402.0 13.1 %collective-permute-done.19 = bf16[256,1408]{1,0:T(8,128)(2,1)S(1)} collective-permute-done((bf16[256,1408]{1,0:T(8,128)(2,1)S(1)}, bf16[256,1408]{1,0:T(8,128)(2,1)S(1)}, u32[]{:S(2)}, u32[]{:S(2)}) %collective-permute-start.19) | collective-permute-done | bytes 720928 | tf_op jit(solution)/shard_map/ppermute | solution.py:126
  419.8 4.9 convolution_convert_fusion.1
  424.8 10.2 %collective-permute-done.20 = bf16[256,1408]{1,0:T(8,128)(2,1)S(1)} collective-permute-done((bf16[256,1408]{1,0:T(8,128)(2,1)S(1)}, bf16[256,1408]{1,0:T(8,128)(2,1)S(1)}, u32[]{:S(2)}, u32[]{:S(2)}) %collective-permute-start.20) | collective-permute-done | bytes 720928 | tf_op jit(solution)/shard_map/ppermute | solution.py:126
  441.3 4.4 constant_dynamic-update-slice_fusion.3
  479.1 10.7 %collective-permute-done.23 = bf16[256,1408]{1,0:T(8,128)(2,1)S(1)} collective-permute-done((bf16[256,1408]{1,0:T(8,128)(2,1)S(1)}, bf16[256,1408]{1,0:T(8,128)(2,1)S(1)}, u32[]{:S(2)}, u32[]{:S(2)}) %collective-permute-start.23) | collective-permute-done | bytes 720928 | tf_op jit(solution)/shard_map/ppermute | solution.py:126
  501.2 9.8 %collective-permute-done.24 = bf16[256,1408]{1,0:T(8,128)(2,1)S(1)} collective-permute-done((bf16[256,1408]{1,0:T(8,128)(2,1)S(1)}, bf16[256,1408]{1,0:T(8,128)(2,1)S(1)}, u32[]{:S(2)}, u32[]{:S(2)}) %collective-permute-start.24) | collective-permute-done | bytes 720928 | tf_op jit(solution)/shard_map/ppermute | solution.py:126
  537.2 6.5 broadcast_select_fusion
  543.7 10.1 %fusion.127 = bf16[1024,1,4,88]{0,3,2,1:T(8,128)(2,1)} fusion(bf16[1024,4,88]{0,2,1:T(8,128)(2,1)} %maximum_bitcast_fusion.1, f32[4,1024,1024]{1,2,0:T(8,128)} %get-tuple-element.389, f32[4,1024]{1,0:T(4,128)S(1)} %copy-done.153), kind=kOutput, calls=%fused_computation.292 | convolution fusion | flops 751140864 | bytes 18235392 | tf_op jit(solution)/shard_map/hqk,qhd->khd/dot_general | solution.py:18
  553.9 11.3 %multiply_reduce_fusion = (f32[4,1024]{1,0:T(4,128)S(1)}, f32[4,1024,1024]{1,2,0:T(8,128)}) fusion(f32[4,1024,1024]{1,2,0:T(8,128)} %get-tuple-element.389, f32[4,1024]{1,0:T(4,128)S(1)} %copy-done.153, bf16[1024,4,88]{0,2,1:T(8,128)(2,1)S(1)} %copy-done.49, bf16[1024,4,88]{0,2,1:T(8,128)(2,1)S(1)} %copy-done.82), kind=kOutput, calls=%fused_computation.5 | convolution fusion | flops 754970624 | bytes 35028992 | tf_op jit(solution)/shard_map/qhd,khd->hqk/dot_general | solution.py:18
  568.6 12.7 %multiply_convert_fusion = bf16[4,1024,1024]{1,2,0:T(8,128)(2,1)S(1)} fusion(f32[4,1024,1024]{1,2,0:T(8,128)} %get-tuple-element.403, f32[4,1024,1024]{1,2,0:T(8,128)} %get-tuple-element.389, f32[4,1024]{1,0:T(4,128)S(1)} %get-tuple-element.402, f32[4,1024]{1,0:T(4,128)S(1)} %copy-done.153), kind=kLoop, calls=%fused_computation.4 | loop fusion | flops 20971520 | bytes 41975808 | tf_op jit(solution)/shard_map/convert_element_type | solution.py:78
  608.9 10.2 %collective-permute-done.33 = bf16[256,1408]{1,0:T(8,128)(2,1)} collective-permute-done((bf16[256,1408]{1,0:T(8,128)(2,1)}, bf16[256,1408]{1,0:T(8,128)(2,1)}, u32[]{:S(2)}, u32[]{:S(2)}) %collective-permute-start.33) | collective-permute-done | bytes 720928 | tf_op jit(solution)/shard_map/ppermute | solution.py:126
  619.1 5.6 collective-permute-done.26
  628.7 4.2 fusion.31
  633.0 8.6 add_convert_fusion
  641.5 4.3 copy.127
  647.1 4.6 convolution_convert_fusion.4
  664.7 13.3 %collective-permute-done.28 = bf16[256,1408]{1,0:T(8,128)(2,1)S(1)} collective-permute-done((bf16[256,1408]{1,0:T(8,128)(2,1)}, bf16[256,1408]{1,0:T(8,128)(2,1)S(1)}, u32[]{:S(2)}, u32[]{:S(2)}) %collective-permute-start.28) | collective-permute-done | bytes 720928 | tf_op jit(solution)/shard_map/ppermute | solution.py:126
  679.5 7.5 collective-permute-done.29
  697.5 5.3 fusion.28
  724.3 5.4 copy.117
  729.7 6.6 reshape.989
  749.0 7.0 fusion.8
  756.0 6.6 fusion.10
  788.0 14.0 %collective-permute-done.38 = f32[352,128]{1,0:T(8,128)S(1)} collective-permute-done((f32[352,128]{1,0:T(8,128)}, f32[352,128]{1,0:T(8,128)S(1)}, u32[]{:S(2)}, u32[]{:S(2)}) %collective-permute-start.38) | collective-permute-done | bytes 180256 | tf_op jit(solution)/shard_map/ppermute | solution.py:126
  809.6 5.2 collective-permute-done.41
  853.4 4.8 fusion.5
  (1014 shorter events, 428.3 us)
Async XLA Ops:
  7.2 67.0 %all-gather.6.cloned.1.call-start = ((), (), s32[]{:S(2)}) async-start(), calls=%async_computation.10 | async-start | bytes 2433024 | tf_op jit(solution)/shard_map/all_gather | solution.py:203
  11.8 34.6 %collective-permute-start = (bf16[256,2816]{1,0:T(8,128)(2,1)S(1)}, bf16[256,2816]{1,0:T(8,128)(2,1)S(1)}, u32[]{:S(2)}, u32[]{:S(2)}) collective-permute-start(bf16[256,2816]{1,0:T(8,128)(2,1)S(1)} %pad_maximum_fusion.17), channel_id=1, source_target_pairs={{0,4},{2,6},{4,0},{6,2},{1,5},{3,7},{5,1},{7,3},{8,12},{10,14},{12... | collective-permute-start | bytes 4325384 | tf_op jit(solution)/shard_map/ppermute | solution.py:126
  48.1 28.0 %collective-permute-start.1 = (bf16[512,2816]{1,0:T(8,128)(2,1)}, bf16[512,2816]{1,0:T(8,128)(2,1)}, u32[]{:S(2)}, u32[]{:S(2)}) collective-permute-start(bf16[512,2816]{1,0:T(8,128)(2,1)} %pad_maximum_fusion.4), channel_id=1, source_target_pairs={{0,2},{2,0},{4,6},{6,4},{1,3},{3,1},{5,7},{7,5},{8,10},{10,8},{12,... | collective-permute-start | bytes 8650760 | tf_op jit(solution)/shard_map/ppermute | solution.py:126
  53.9 85.3 %all-gather.8.cloned.1.call-start = ((), (), s32[]{:S(2)}) async-start(), calls=%async_computation.11 | async-start | bytes 4866048 | tf_op jit(solution)/shard_map/all_gather | solution.py:182
  69.2 17.6 %all-to-all-start.2 = ((f32[4,1,1408]{2,1,0:T(1,128)}), f32[4,1,1408]{2,1,0:T(1,128)S(1)}, u32[]{:S(2)}, u32[]{:S(2)}) async-start(f32[4,1,1408]{2,1,0:T(1,128)} %all_to_all.32), calls=%async_computation.2 | async-start | bytes 45056 | tf_op jit(solution)/shard_map/all_to_all | solution.py:229
  86.7 14.4 %all-to-all-start = ((bf16[4,256,352]{1,2,0:T(8,128)(2,1)}), bf16[4,256,352]{1,2,0:T(8,128)(2,1)S(1)}, u32[]{:S(2)}, u32[]{:S(2)}) async-start(bf16[4,256,352]{1,2,0:T(8,128)(2,1)} %broadcast_select_fusion.9), calls=%async_computation | async-start | bytes 1441792 | tf_op jit(solution)/shard_map/all_to_all | solution.py:236
  90.2 124.5 %all-gather.12.cloned.1.call-start = ((), (), s32[]{:S(2)}) async-start(), calls=%async_computation.13 | async-start | bytes 4866048 | tf_op jit(solution)/shard_map/all_gather | solution.py:182
  108.7 17.8 %collective-permute-start.3 = (bf16[256,1408]{1,0:T(8,128)(2,1)S(1)}, bf16[256,1408]{1,0:T(8,128)(2,1)}, u32[]{:S(2)}, u32[]{:S(2)}) collective-permute-start(bf16[256,1408]{1,0:T(8,128)(2,1)S(1)} %add_convert_fusion.6), channel_id=1, source_target_pairs={{0,4},{2,6},{4,0},{6,2},{1,5},{3,7},{5,1},{7,3},{8,12},{10,14},{12... | collective-permute-start | bytes 2162696 | tf_op jit(solution)/shard_map/ppermute | solution.py:126
  109.2 22.7 %collective-permute-start.5 = (s32[256,2]{0,1:T(2,128)S(1)}, s32[256,2]{0,1:T(2,128)S(1)}, u32[]{:S(2)}, u32[]{:S(2)}) collective-permute-start(s32[256,2]{0,1:T(2,128)S(1)} %fusion.218), channel_id=1, source_target_pairs={{0,4},{2,6},{4,0},{6,2},{1,5},{3,7},{5,1},{7,3},{8,12},{10,14},{12... | collective-permute-start | bytes 6152 | tf_op jit(solution)/shard_map/ppermute | solution.py:126
  118.7 174.3 %all-gather.14.cloned.1.call-start = ((), (), s32[]{:S(2)}) async-start(), calls=%async_computation.14 | async-start | bytes 4866048 | tf_op jit(solution)/shard_map/all_gather | solution.py:182
  153.2 27.0 %collective-permute-start.7 = (bf16[256,1408]{1,0:T(8,128)(2,1)S(1)}, bf16[256,1408]{1,0:T(8,128)(2,1)S(1)}, u32[]{:S(2)}, u32[]{:S(2)}) collective-permute-start(bf16[256,1408]{1,0:T(8,128)(2,1)S(1)} %get-tuple-element.87), channel_id=1, source_target_pairs={{0,4},{2,6},{4,0},{6,2},{1,5},{3,7},{5,1},{7,3},{8,12},{10,14},{12... | collective-permute-start | bytes 2162696 | tf_op jit(solution)/shard_map/ppermute | solution.py:126
  187.7 18.2 %collective-permute-start.10 = (bf16[256,1408]{1,0:T(8,128)(2,1)S(1)}, bf16[256,1408]{1,0:T(8,128)(2,1)S(1)}, u32[]{:S(2)}, u32[]{:S(2)}) collective-permute-start(bf16[256,1408]{1,0:T(8,128)(2,1)S(1)} %slice.972), channel_id=1, source_target_pairs={{0,4},{2,6},{4,0},{6,2},{1,5},{3,7},{5,1},{7,3},{8,12},{10,14},{12... | collective-permute-start | bytes 2162696 | tf_op jit(solution)/shard_map/ppermute | solution.py:126
  218.5 16.8 %collective-permute-start.11 = (bf16[256,1408]{1,0:T(8,128)(2,1)S(1)}, bf16[256,1408]{1,0:T(8,128)(2,1)}, u32[]{:S(2)}, u32[]{:S(2)}) collective-permute-start(bf16[256,1408]{1,0:T(8,128)(2,1)S(1)} %add_convert_fusion.5), channel_id=1, source_target_pairs={{0,4},{2,6},{4,0},{6,2},{1,5},{3,7},{5,1},{7,3},{8,12},{10,14},{12... | collective-permute-start | bytes 2162696 | tf_op jit(solution)/shard_map/ppermute | solution.py:126
  220.9 147.6 %all-gather.10.cloned.1.call-start = ((), (), s32[]{:S(2)}) async-start(), calls=%async_computation.12 | async-start | bytes 4866048 | tf_op jit(solution)/shard_map/all_gather | solution.py:182
  265.7 18.5 %collective-permute-start.14 = (bf16[256,1408]{1,0:T(8,128)(2,1)S(1)}, bf16[256,1408]{1,0:T(8,128)(2,1)S(1)}, u32[]{:S(2)}, u32[]{:S(2)}) collective-permute-start(bf16[256,1408]{1,0:T(8,128)(2,1)S(1)} %slice.971), channel_id=1, source_target_pairs={{0,4},{2,6},{4,0},{6,2},{1,5},{3,7},{5,1},{7,3},{8,12},{10,14},{12... | collective-permute-start | bytes 2162696 | tf_op jit(solution)/shard_map/ppermute | solution.py:126
  269.1 274.6 %reduce-scatter.13.cloned.1.call-start = ((), (), s32[]{:S(2)}) async-start(), calls=%async_computation.15 | async-start | bytes 4866048 | tf_op jit(solution)/shard_map/reduce_scatter | solution.py:329
  294.7 16.9 %collective-permute-start.15 = (bf16[256,1408]{1,0:T(8,128)(2,1)}, bf16[256,1408]{1,0:T(8,128)(2,1)}, u32[]{:S(2)}, u32[]{:S(2)}) collective-permute-start(bf16[256,1408]{1,0:T(8,128)(2,1)} %add_convert_fusion.4), channel_id=1, source_target_pairs={{0,4},{2,6},{4,0},{6,2},{1,5},{3,7},{5,1},{7,3},{8,12},{10,14},{12... | collective-permute-start | bytes 2162696 | tf_op jit(solution)/shard_map/ppermute | solution.py:126
  299.4 17.9 %collective-permute-start.8 = (bf16[512,1408]{1,0:T(8,128)(2,1)}, bf16[512,1408]{1,0:T(8,128)(2,1)S(1)}, u32[]{:S(2)}, u32[]{:S(2)}) collective-permute-start(bf16[512,1408]{1,0:T(8,128)(2,1)} %pad_maximum_fusion.19), channel_id=1, source_target_pairs={{0,2},{2,0},{4,6},{6,4},{1,3},{3,1},{5,7},{7,5},{8,10},{10,8},{12,... | collective-permute-start | bytes 4325384 | tf_op jit(solution)/shard_map/ppermute | solution.py:126
  326.4 53.9 %collective-permute-start.17 = (bf16[1,2816,352]{1,2,0:T(8,128)(2,1)}, bf16[1,2816,352]{1,2,0:T(8,128)(2,1)}, u32[]{:S(2)}, u32[]{:S(2)}) collective-permute-start(bf16[1,2816,352]{1,2,0:T(8,128)(2,1)} %bitcast.460), channel_id=1, source_target_pairs={{0,4},{2,6},{4,0},{6,2},{1,5},{3,7},{5,1},{7,3},{8,12},{10,14},{12... | collective-permute-start | bytes 5947400 | tf_op jit(solution)/shard_map/ppermute | solution.py:126
  348.7 216.5 %reduce-scatter.15.cloned.1.call-start = ((), (), s32[]{:S(2)}) async-start(), calls=%async_computation.16 | async-start | bytes 4866048 | tf_op jit(solution)/shard_map/reduce_scatter | solution.py:329
  396.5 18.6 %collective-permute-start.19 = (bf16[256,1408]{1,0:T(8,128)(2,1)S(1)}, bf16[256,1408]{1,0:T(8,128)(2,1)S(1)}, u32[]{:S(2)}, u32[]{:S(2)}) collective-permute-start(bf16[256,1408]{1,0:T(8,128)(2,1)S(1)} %slice.970), channel_id=1, source_target_pairs={{0,4},{2,6},{4,0},{6,2},{1,5},{3,7},{5,1},{7,3},{8,12},{10,14},{12... | collective-permute-start | bytes 2162696 | tf_op jit(solution)/shard_map/ppermute | solution.py:126
  417.1 17.9 %collective-permute-start.20 = (bf16[256,1408]{1,0:T(8,128)(2,1)S(1)}, bf16[256,1408]{1,0:T(8,128)(2,1)S(1)}, u32[]{:S(2)}, u32[]{:S(2)}) collective-permute-start(bf16[256,1408]{1,0:T(8,128)(2,1)S(1)} %get-tuple-element.252), channel_id=1, source_target_pairs={{0,4},{2,6},{4,0},{6,2},{1,5},{3,7},{5,1},{7,3},{8,12},{10,14},{12... | collective-permute-start | bytes 2162696 | tf_op jit(solution)/shard_map/ppermute | solution.py:126
  419.2 93.1 %collective-permute-start.40 = (bf16[2,2816,352]{1,2,0:T(8,128)(2,1)}, bf16[2,2816,352]{1,2,0:T(8,128)(2,1)}, u32[]{:S(2)}, u32[]{:S(2)}) collective-permute-start(bf16[2,2816,352]{1,2,0:T(8,128)(2,1)} %pad_maximum_fusion.2), channel_id=1, source_target_pairs={{0,2},{2,0},{4,6},{6,4},{1,3},{3,1},{5,7},{7,5},{8,10},{10,8},{12,... | collective-permute-start | bytes 11894792 | tf_op jit(solution)/shard_map/ppermute | solution.py:126
  441.2 165.9 %reduce-scatter.19.cloned.1.call-start = ((), (), s32[]{:S(2)}) async-start(), calls=%async_computation.18 | async-start | bytes 1351680
  471.3 18.5 %collective-permute-start.23 = (bf16[256,1408]{1,0:T(8,128)(2,1)S(1)}, bf16[256,1408]{1,0:T(8,128)(2,1)S(1)}, u32[]{:S(2)}, u32[]{:S(2)}) collective-permute-start(bf16[256,1408]{1,0:T(8,128)(2,1)S(1)} %slice.969), channel_id=1, source_target_pairs={{0,4},{2,6},{4,0},{6,2},{1,5},{3,7},{5,1},{7,3},{8,12},{10,14},{12... | collective-permute-start | bytes 2162696 | tf_op jit(solution)/shard_map/ppermute | solution.py:126
  493.0 17.9 %collective-permute-start.24 = (bf16[256,1408]{1,0:T(8,128)(2,1)S(1)}, bf16[256,1408]{1,0:T(8,128)(2,1)S(1)}, u32[]{:S(2)}, u32[]{:S(2)}) collective-permute-start(bf16[256,1408]{1,0:T(8,128)(2,1)S(1)} %get-tuple-element.254), channel_id=1, source_target_pairs={{0,4},{2,6},{4,0},{6,2},{1,5},{3,7},{5,1},{7,3},{8,12},{10,14},{12... | collective-permute-start | bytes 2162696 | tf_op jit(solution)/shard_map/ppermute | solution.py:126
  566.6 200.9 %reduce-scatter.21.cloned.1.call-start = ((), (), s32[]{:S(2)}) async-start(), calls=%async_computation.19 | async-start | bytes 3153920
  566.7 27.2 %collective-permute-start.30 = (bf16[1,768,352]{1,2,0:T(8,128)(2,1)S(1)}, bf16[1,768,352]{1,2,0:T(8,128)(2,1)S(1)}, u32[]{:S(2)}, u32[]{:S(2)}) collective-permute-start(bf16[1,768,352]{1,2,0:T(8,128)(2,1)S(1)} %bitcast.523), channel_id=1, source_target_pairs={{0,4},{2,6},{4,0},{6,2},{1,5},{3,7},{5,1},{7,3},{8,12},{10,14},{12... | collective-permute-start | bytes 1622024 | tf_op jit(solution)/shard_map/ppermute | solution.py:126
  568.2 27.2 %collective-permute-start.32 = (bf16[512,1408]{1,0:T(8,128)(2,1)}, bf16[512,1408]{1,0:T(8,128)(2,1)}, u32[]{:S(2)}, u32[]{:S(2)}) collective-permute-start(bf16[512,1408]{1,0:T(8,128)(2,1)} %fusion.30), channel_id=1, source_target_pairs={{0,2},{2,0},{4,6},{6,4},{1,3},{3,1},{5,7},{7,5},{8,10},{10,8},{12,... | collective-permute-start | bytes 4325384 | tf_op jit(solution)/shard_map/ppermute | solution.py:126
  568.2 56.5 %collective-permute-start.26 = (bf16[1408,880]{0,1:T(8,128)(2,1)}, bf16[1408,880]{0,1:T(8,128)(2,1)}, u32[]{:S(2)}, u32[]{:S(2)}) collective-permute-start(bf16[1408,880]{0,1:T(8,128)(2,1)} %broadcast_select_fusion), channel_id=1, source_target_pairs={{0,1},{1,0},{2,3},{3,2},{4,5},{5,4},{6,7},{7,6},{8,9},{9,8},{10,11... | collective-permute-start | bytes 7434248 | tf_op jit(solution)/shard_map/ppermute | solution.py:118
  600.3 18.8 %collective-permute-start.33 = (bf16[256,1408]{1,0:T(8,128)(2,1)}, bf16[256,1408]{1,0:T(8,128)(2,1)}, u32[]{:S(2)}, u32[]{:S(2)}) collective-permute-start(bf16[256,1408]{1,0:T(8,128)(2,1)} %slice.967), channel_id=1, source_target_pairs={{0,4},{2,6},{4,0},{6,2},{1,5},{3,7},{5,1},{7,3},{8,12},{10,14},{12... | collective-permute-start | bytes 2162696 | tf_op jit(solution)/shard_map/ppermute | solution.py:126
  632.9 22.0 %collective-permute-start.27 = (bf16[512,1408]{1,0:T(8,128)(2,1)}, bf16[512,1408]{1,0:T(8,128)(2,1)}, u32[]{:S(2)}, u32[]{:S(2)}) collective-permute-start(bf16[512,1408]{1,0:T(8,128)(2,1)} %fusion.31), channel_id=1, source_target_pairs={{0,2},{2,0},{4,6},{6,4},{1,3},{3,1},{5,7},{7,5},{8,10},{10,8},{12,... | collective-permute-start | bytes 4325384 | tf_op jit(solution)/shard_map/ppermute | solution.py:126
  651.7 35.3 %collective-permute-start.29 = (bf16[1408,528]{0,1:T(8,128)(2,1)}, bf16[1408,528]{0,1:T(8,128)(2,1)}, u32[]{:S(2)}, u32[]{:S(2)}) collective-permute-start(bf16[1408,528]{0,1:T(8,128)(2,1)} %convolution_convert_fusion.4), channel_id=1, source_target_pairs={{0,1},{1,0},{2,3},{3,2},{4,5},{5,4},{6,7},{7,6},{8,9},{9,8},{10,11... | collective-permute-start | bytes 4460552 | tf_op jit(solution)/shard_map/ppermute | solution.py:118
  659.4 18.5 %collective-permute-start.28 = (bf16[256,1408]{1,0:T(8,128)(2,1)}, bf16[256,1408]{1,0:T(8,128)(2,1)S(1)}, u32[]{:S(2)}, u32[]{:S(2)}) collective-permute-start(bf16[256,1408]{1,0:T(8,128)(2,1)} %slice.968), channel_id=1, source_target_pairs={{0,4},{2,6},{4,0},{6,2},{1,5},{3,7},{5,1},{7,3},{8,12},{10,14},{12... | collective-permute-start | bytes 2162696 | tf_op jit(solution)/shard_map/ppermute | solution.py:126
  697.0 72.0 %reduce-scatter.23.cloned.1.call-start = ((), (), s32[]{:S(2)}) async-start(), calls=%async_computation.20 | async-start | bytes 2252800
  706.5 129.0 %reduce-scatter.17.cloned.1.call-start = ((), (), s32[]{:S(2)}) async-start(), calls=%async_computation.17 | async-start | bytes 1351680 | tf_op jit(solution)/shard_map/reduce_scatter | solution.py:451
  717.5 18.8 %collective-permute-start.42 = (bf16[333,176]{1,0:T(8,128)(2,1)S(1)}, bf16[333,176]{1,0:T(8,128)(2,1)S(1)}, u32[]{:S(2)}, u32[]{:S(2)}) collective-permute-start(bf16[333,176]{1,0:T(8,128)(2,1)S(1)} %constant_dynamic-slice_fusion), channel_id=1, source_target_pairs={{0,1},{1,0},{2,3},{3,2},{4,5},{5,4},{6,7},{7,6},{8,9},{9,8},{10,11... | collective-permute-start | bytes 351656 | tf_op jit(solution)/shard_map/ppermute | solution.py:118
  718.2 19.4 %collective-permute-start.50 = (bf16[1,352,768]{2,1,0:T(8,128)(2,1)}, bf16[1,352,768]{2,1,0:T(8,128)(2,1)}, u32[]{:S(2)}, u32[]{:S(2)}) collective-permute-start(bf16[1,352,768]{2,1,0:T(8,128)(2,1)} %bitcast.522), channel_id=1, source_target_pairs={{0,4},{2,6},{4,0},{6,2},{1,5},{3,7},{5,1},{7,3},{8,12},{10,14},{12... | collective-permute-start | bytes 1622024 | tf_op jit(solution)/shard_map/ppermute | solution.py:126
  719.6 20.8 %collective-permute-start.39 = (bf16[256,1408]{1,0:T(8,128)(2,1)S(1)}, bf16[256,1408]{1,0:T(8,128)(2,1)}, u32[]{:S(2)}, u32[]{:S(2)}) collective-permute-start(bf16[256,1408]{1,0:T(8,128)(2,1)S(1)} %get-tuple-element.126), channel_id=1, source_target_pairs={{0,1},{1,0},{2,3},{3,2},{4,5},{5,4},{6,7},{7,6},{8,9},{9,8},{10,11... | collective-permute-start | bytes 2162696 | tf_op jit(solution)/shard_map/ppermute | solution.py:118
  723.3 39.3 %collective-permute-start.34 = (bf16[2,4,176,352]{3,2,1,0:T(8,128)(2,1)}, bf16[2,4,176,352]{3,2,1,0:T(8,128)(2,1)}, u32[]{:S(2)}, u32[]{:S(2)}) collective-permute-start(bf16[2,4,176,352]{3,2,1,0:T(8,128)(2,1)} %dynamic-slice_bitcast_fusion), channel_id=1, source_target_pairs={{0,1},{1,0},{2,3},{3,2},{4,5},{5,4},{6,7},{7,6},{8,9},{9,8},{10,11... | collective-permute-start | bytes 2973704 | tf_op jit(solution)/shard_map/ppermute | solution.py:118
  739.9 25.3 %collective-permute-start.51 = (bf16[2,352,768]{2,1,0:T(8,128)(2,1)}, bf16[2,352,768]{2,1,0:T(8,128)(2,1)}, u32[]{:S(2)}, u32[]{:S(2)}) collective-permute-start(bf16[2,352,768]{2,1,0:T(8,128)(2,1)} %pad_maximum_fusion.28), channel_id=1, source_target_pairs={{0,2},{2,0},{4,6},{6,4},{1,3},{3,1},{5,7},{7,5},{8,10},{10,8},{12,... | collective-permute-start | bytes 3244040 | tf_op jit(solution)/shard_map/ppermute | solution.py:126
  777.4 26.4 %collective-permute-start.46 = (bf16[1,352,528]{1,2,0:T(8,128)(2,1)S(1)}, bf16[1,352,528]{1,2,0:T(8,128)(2,1)}, u32[]{:S(2)}, u32[]{:S(2)}) collective-permute-start(bf16[1,352,528]{1,2,0:T(8,128)(2,1)S(1)} %bitcast.472), channel_id=1, source_target_pairs={{0,4},{2,6},{4,0},{6,2},{1,5},{3,7},{5,1},{7,3},{8,12},{10,14},{12... | collective-permute-start | bytes 1115144 | tf_op jit(solution)/shard_map/ppermute | solution.py:126
  779.1 26.8 %collective-permute-start.48 = (bf16[1,352,880]{2,1,0:T(8,128)(2,1)}, bf16[1,352,880]{2,1,0:T(8,128)(2,1)}, u32[]{:S(2)}, u32[]{:S(2)}) collective-permute-start(bf16[1,352,880]{2,1,0:T(8,128)(2,1)} %copy.112), channel_id=1, source_target_pairs={{0,4},{2,6},{4,0},{6,2},{1,5},{3,7},{5,1},{7,3},{8,12},{10,14},{12... | collective-permute-start | bytes 1858568 | tf_op jit(solution)/shard_map/ppermute | solution.py:126
  780.6 36.8 %collective-permute-start.35 = (bf16[256,1408]{1,0:T(8,128)(2,1)}, bf16[256,1408]{1,0:T(8,128)(2,1)}, u32[]{:S(2)}, u32[]{:S(2)}) collective-permute-start(bf16[256,1408]{1,0:T(8,128)(2,1)} %fusion.80), channel_id=1, source_target_pairs={{0,1},{1,0},{2,3},{3,2},{4,5},{5,4},{6,7},{7,6},{8,9},{9,8},{10,11... | collective-permute-start | bytes 2162696 | tf_op jit(solution)/shard_map/ppermute | solution.py:118
  784.3 17.7 %collective-permute-start.38 = (f32[352,128]{1,0:T(8,128)}, f32[352,128]{1,0:T(8,128)S(1)}, u32[]{:S(2)}, u32[]{:S(2)}) collective-permute-start(f32[352,128]{1,0:T(8,128)} %fusion.343), channel_id=1, source_target_pairs={{0,1},{1,0},{2,3},{3,2},{4,5},{5,4},{6,7},{7,6},{8,9},{9,8},{10,11... | collective-permute-start | bytes 540680 | tf_op jit(solution)/shard_map/ppermute | solution.py:126
  805.8 14.8 %collective-permute-start.47 = (bf16[2,352,528]{1,2,0:T(8,128)(2,1)}, bf16[2,352,528]{1,2,0:T(8,128)(2,1)}, u32[]{:S(2)}, u32[]{:S(2)}) collective-permute-start(bf16[2,352,528]{1,2,0:T(8,128)(2,1)} %pad_maximum_fusion.29), channel_id=1, source_target_pairs={{0,2},{2,0},{4,6},{6,4},{1,3},{3,1},{5,7},{7,5},{8,10},{10,8},{12,... | collective-permute-start | bytes 2230280 | tf_op jit(solution)/shard_map/ppermute | solution.py:126
  809.1 17.4 %collective-permute-start.49 = (bf16[2,352,880]{2,1,0:T(8,128)(2,1)}, bf16[2,352,880]{2,1,0:T(8,128)(2,1)}, u32[]{:S(2)}, u32[]{:S(2)}) collective-permute-start(bf16[2,352,880]{2,1,0:T(8,128)(2,1)} %copy.114), channel_id=1, source_target_pairs={{0,2},{2,0},{4,6},{6,4},{1,3},{3,1},{5,7},{7,5},{8,10},{10,8},{12,... | collective-permute-start | bytes 3717128 | tf_op jit(solution)/shard_map/ppermute | solution.py:126
  815.5 23.6 %collective-permute-start.45 = (f32[352,128]{1,0:T(8,128)}, f32[352,128]{1,0:T(8,128)}, u32[]{:S(2)}, u32[]{:S(2)}) collective-permute-start(f32[352,128]{1,0:T(8,128)} %add.923), channel_id=1, source_target_pairs={{0,16},{8,24},{16,0},{24,8},{1,17},{9,25},{17,1},{25,9},{2,18},{10... | collective-permute-start | bytes 540680 | tf_op jit(solution)/shard_map/ppermute | solution.py:126
  (270 other events, 3090.4 us)
Sparse Core Ops, SparseCore 0:
  10.8 52.5 all-gather.5
  66.0 73.0 all-gather.7
  141.8 72.9 all-gather.11
  221.0 72.0 all-gather.13
  295.6 72.8 all-gather.9
  372.5 88.7 reduce-scatter.12
  465.5 89.8 reduce-scatter.14
  566.7 23.5 reduce-scatter.18
  646.0 48.4 reduce-scatter.20
  706.6 37.8 reduce-scatter.22
  788.1 30.5 reduce-scatter.16

commit v5 on v4

--- a/solution.py
+++ b/solution.py
@@ -134,7 +134,10 @@
         return jnp.concatenate([values, flip(values, "context", bits[0])], 0)
 
     def gather_rows(values):
-        return gather_near(gather_far(values))
+        blocks = [values]
+        for bit in reversed(bits):
+            blocks = blocks + [flip(b, "context", bit) for b in blocks]
+        return jnp.concatenate(blocks, 0)
 
     order = [sum(((p >> j) & 1) << (len(bits) - 1 - j) for j in range(len(bits))) for p in range(nk)]
 
@@ -167,11 +170,14 @@
         return sum_rows(*partial_rows(pieces))[0]
 
     def gather_filled(values, fill):
+        blocks = [values]
         for bit in reversed(bits[1:]):
-            got = flip(values, "context", bit)
-            got, fill = pin((got, fill))
-            values = jnp.concatenate([values, got], 0)
-        return gather_near(values), fill
+            got, fill = pin(([flip(b, "context", bit) for b in blocks], fill))
+            blocks = blocks + got
+        return jnp.concatenate(blocks + [flip(b, "context", bits[0]) for b in blocks], 0), fill
+
+    def own_first(parts):
+        return (jnp.where(y == 0, parts[0], parts[1]), jnp.where(y == 0, parts[1], parts[0]))
 
     def by_batch(own, theirs):
         first = jnp.where(y == 0, own, theirs)
@@ -203,7 +209,7 @@
     skip_z = lax.all_gather(skip_part, ("shard", "tensor"), axis=0, tiled=True)
     skip_block = jnp.transpose(skip_z[:, :eb].reshape(nz * ny, 2, -1, eb), (1, 0, 2, 3)).reshape(2 * width, eb)
     first_z = gathered(first_part)
-    second_z = gathered(second_part)
+    second_z = lax.all_gather(second_part, "shard", axis=0, tiled=True)
     up_z = gathered(block(up_weight, hb, 1))
     down_z = gathered(block(down_weight, hb, 0).T)
 
@@ -273,19 +279,19 @@
     )
 
 
-    resid_one, second_z = pin((resid_one, second_z))
+    resid_one, second_z, second_other = pin((resid_one, second_z, other(second_z)))
 
     def second_piece(resid_in, gain_rows, bias_rows):
         return layer_norm(resid_in, gain_rows[2], bias_rows[2])
 
     normed_two, pull_second = jax.vjp(second_piece, resid_one, norm_gains, norm_biases)
-    second_pair = halves(second_z)
+    second_pair = (second_z, second_other)
     cross_q_full = [w[:, :cb] for w in second_pair]
     cross_kv_full = [w[:, cb : 3 * cb] for w in second_pair]
     cross_out_full = [w[:, 3 * cb :] for w in second_pair]
     normed_two_all = gather_rows(normed_two.astype(BF))
-    cq_bias = own_columns(column_biases[3], cb, half_cols)
-    kv_bias = own_columns(column_biases[4:6], cb, half_cols)
+    cq_bias = own_first(own_columns(column_biases[3], cb, half_cols))
+    kv_bias = own_first(own_columns(column_biases[4:6], cb, half_cols))
     cross_raw = to_heads([matmul(normed_two_all, w) + b.reshape(1, -1) for w, b in zip(cross_q_full, cq_bias)], 1)
     pair_raw = to_heads([matmul(text_rows, w) + b.reshape(1, -1) for w, b in zip(cross_kv_full, kv_bias)], 2)
 
@@ -327,9 +333,6 @@
 
     def reduced(total):
         return lax.psum_scatter(total, ("tensor", "shard"), scatter_dimension=0, tiled=True)
-
-    def own_first(parts):
-        return (jnp.where(y == 0, parts[0], parts[1]), jnp.where(y == 0, parts[1], parts[0]))
 
     def over_shard(own, received):
         total = own + received.astype(F32)
@@ -404,26 +407,26 @@
     grad_one_all, (cross_q_grad, cross_kv_grad, cross_out_grad) = gather_filled(
         grad_one_low, (cross_q_grad, cross_kv_grad, cross_out_grad)
     )
-    self_out_grad = [contract_rows(grad_one_all, p).astype(BF) for p in mix_parts]
+    self_out_grad = [contract_rows(grad_one_all, p).astype(BF) for p in own_first(mix_parts)]
     small_grad = [jnp.concatenate(g, 1) for g in zip(cross_q_grad, cross_kv_grad, cross_out_grad, self_out_grad)]
-    small_grad = own_first(small_grad)
     mix_grad = to_heads([matmul(grad_one_all, w).astype(BF) for w in self_out_full], 1)[:, 0]
     mix_grad, small_low, down_grad, result_parts = pin((mix_grad, small_grad[1], down_grad, result_parts))
     small_low = other(small_low)
     down_grad = spread(down_grad)
-    result = resid_two + (sum_rows(*result_parts)[0] + width_biases[4])
-    result_low = result.astype(BF)
+    result_part = result_parts[1] + flip(result_parts[0], "context", bits[0]).astype(F32)
     q_back, k_back, v_back = attention_backward(query, key, value, self_sums, mix_grad)
     q_back, k_back, v_back = q_back.astype(BF), k_back.astype(BF), v_back.astype(BF)
     self_grads = pull_self(
         (q_back.astype(F32), k_back.astype(F32), v_back.astype(F32))
     )
     triple_raw, small_low, up_grad = pin((self_grads[0].astype(BF), small_low, up_grad))
-    small_grad = over_shard(small_grad[0].astype(F32), small_low)
+    small_total = (small_grad[0].astype(F32) + small_low.astype(F32)).astype(BF)
+    small_grad = lax.psum_scatter(small_total, "shard", scatter_dimension=0, tiled=True)
     triple_low = from_heads(triple_raw)
     triple_grad = [contract_rows(normed_one_all, g) for g in own_first(triple_low)]
     triple_got = other(triple_grad[1].astype(BF))
-    normed_grad = scatter_rows([(triple_low[0], triple_full[0], contract_cols), (triple_low[1], triple_full[1], contract_cols)])
+    normed_grad = partial_rows([(triple_low[0], triple_full[0], contract_cols), (triple_low[1], triple_full[1], contract_cols)])
+    normed_grad = sum_rows(*normed_grad, small_total[:8, :128])[0]
     normed_grad, triple_got = pin((normed_grad, triple_got))
     first_grads = pull_first((resid_one_grad, normed_grad))
     summed_low = first_grads[0].astype(BF)
@@ -431,38 +434,33 @@
     summed_cols = lax.all_to_all(summed_low, "context", split_axis=1, concat_axis=0, tiled=True)
     summed_cols = ranked(summed_cols.reshape(nk, local_len, eb), 0, True).reshape(length, eb)
     skip_part = contract_rows(tok_halves[0], summed_cols[: length // 2]) + contract_rows(tok_halves[1], summed_cols[length // 2 :])
-    skip_part, text_part, down_grad, result_low, up_grad, summed_late = pin(
-        (skip_part.astype(BF), text_part, down_grad, result_low, up_grad, summed_low)
-    )
+    skip_part, text_part, down_grad, result_part, up_grad = pin(
+        (skip_part.astype(BF), text_part, down_grad, result_part, up_grad)
+    )
+    for bit in bits[1:]:
+        half = result_part.shape[0] // 2
+        result_part = result_part[:half] + flip(result_part[half:].astype(BF), "context", bit).astype(F32)
+    result_low = (resid_two + (result_part + width_biases[4])).astype(BF)
     up_grad = spread(up_grad)
-    text_mine = lax.dynamic_slice_in_dim(text_part, y * text_cols, text_cols, 1)
     skip_part = skip_part.reshape(2, nz, ny, -1, eb)
     keep = lax.dynamic_index_in_dim(skip_part, y, 2, keepdims=False)
     give = lax.dynamic_index_in_dim(skip_part, 1 - y, 2, keepdims=False)
     skip_total = (keep.astype(F32) + other(give).astype(F32)).astype(BF)
-    skip_total, small_grad, triple_grad, result_low = pin((skip_total, small_grad, triple_grad, result_low))
-    small_all = gather_rows(small_grad[None])
-    result_out = by_batch(result_low, other(result_low)).astype(F32)
+    skip_total, small_grad, triple_grad, result_low, summed_late, text_part = pin(
+        (skip_total, small_grad, triple_grad, result_low, summed_low, text_part)
+    )
+    text_mine = lax.dynamic_slice_in_dim(text_part, y * text_cols, text_cols, 1)
     text_theirs = other(lax.dynamic_slice_in_dim(text_part, (1 - y) * text_cols, text_cols, 1))
     text_grad = by_batch(text_mine, text_theirs).astype(F32)
     skip_total = jnp.transpose(skip_total, (1, 0, 2, 3)).reshape(-1, eb)
 
     both_low = by_batch(summed_late, other(summed_late)).reshape(batch * local_len, nk, eb)
     skip_grad = lax.psum_scatter(skip_total, "shard", scatter_dimension=0, tiled=True)
-    triple_all = gather_rows(triple_grad[None])
-    both_low = ranked(both_low, 1, True)
+    both_low, skip_grad = pin((ranked(both_low, 1, True), skip_grad))
     tok_grad, skip_rows_grad = [
         contract("tke,kde->td", both_low, w).reshape(batch, local_len, width)
         for w in (skip_all[:, :width], skip_all[:, width:])
     ]
-
-    triple_out = jnp.stack(placed_out(triple_all, cb, 0, 3), 1)
-    small_out = (
-        placed_out(small_all, cb, 4, 1, "prn,pnm->mr")[0],
-        placed_out(small_all, cb, 0, 1)[0],
-        jnp.stack(placed_out(small_all, cb, 1, 2), 1),
-        placed_out(small_all, cb, 3, 1, "prn,pnm->mr")[0],
-    )
 
     def place(parts, size, half, total):
         out = jnp.zeros(parts[0].shape[:-1] + (total,), F32)
@@ -470,24 +468,20 @@
         out = lax.dynamic_update_slice_in_dim(out, parts[0], k * size, at)
         return lax.dynamic_update_slice_in_dim(out, parts[1], half + k * size, at)
 
-    def everywhere(parts, fills):
+    def flattened(parts):
         flat = jnp.concatenate([p.reshape(-1) for p in parts])
-        flat = pin((flat, skip_total))[0]
-        size = flat.shape[0]
-        flat = jnp.pad(flat, (0, -size % 1024)).reshape(-1, 128)
-        stages = [(a, 1 << i) for a in ("context", "tensor", "shard") for i in range(lax.axis_size(a).bit_length() - 1)]
-        fills = list(fills)
-        for at, (axis_name, bit) in enumerate(stages):
-            got = flip(flat, axis_name, bit)
-            slot = at - len(stages) + len(fills)
-            if slot >= 0:
-                got, fills[slot] = pin((got, fills[slot]))
-            flat = flat + got
+        return jnp.pad(flat, (0, -flat.shape[0] % 1024)).reshape(-1, 128)
+
+    def restored(flat, parts):
         flat, out, at = flat.reshape(-1), [], 0
         for p in parts:
             out.append(flat[at : at + p.size].reshape(p.shape))
             at += p.size
-        return out, fills
+        return out
+
+    def summed_over(flat, axis_name, bit, fill):
+        got, fill = pin((flip(flat, axis_name, bit), fill))
+        return flat + got, fill
 
     def col_sums(values, count=1):
         return jnp.sum(values.astype(F32), 0).reshape(count, -1)
@@ -506,20 +500,41 @@
         ]
     )
     column_parts = [
-        jnp.concatenate([col_sums(t, 3), col_sums(c, 1), col_sums(p, 2)], 0)
-        for t, c, p in zip(triple_low, cross_grad_low, pair_low)
+        jnp.concatenate([t, c], 0)
+        for t, c in zip(
+            [col_sums(t, 3) for t in triple_low],
+            own_first([jnp.concatenate([col_sums(c, 1), col_sums(p, 2)], 0) for c, p in zip(cross_grad_low, pair_low)]),
+        )
     ]
     column_grad = place(column_parts, cb, half_cols, width)
     hidden_grad_sum = place([col_sums(h)[0] for h in hidden_grad], hb, half_hidden, hidden_biases.shape[0])
     shift_slots = lax.dynamic_update_slice_in_dim(
         jnp.zeros((sequences, width), F32), first_grads[1][None], z * ny + y, 0
     )
-    vectors, fills = everywhere(
-        (gains_grad, biases_grad, head_gain_grad, head_bias_grad, width_grad, column_grad, hidden_grad_sum, shift_slots),
-        (tok_grad, skip_rows_grad, (triple_out, small_out)),
-    )
-    tok_grad, skip_rows_grad, (triple_out, small_out) = fills
-    skip_grad_out = placed_out(gather_rows(skip_grad[None]), eb, 0, 1)[0].reshape(2, -1, width)
+    parts = (gains_grad, biases_grad, head_gain_grad, head_bias_grad, width_grad, column_grad, hidden_grad_sum, shift_slots)
+    flat, skip_total = pin((flattened(parts), skip_total))
+    for bit in bits:
+        flat, (small_grad, triple_grad) = summed_over(flat, "context", bit, (small_grad, triple_grad))
+    small_all, triple_all = gather_rows(small_grad[None]), gather_rows(triple_grad[None])
+    triple_out = jnp.stack(placed_out(triple_all, cb, 0, 3), 1)
+    small_out = (
+        placed_out(small_all, cb, 4, 1, "prn,pnm->mr")[0],
+        placed_out(small_all, cb, 0, 1)[0],
+        jnp.stack(placed_out(small_all, cb, 1, 2), 1),
+        placed_out(small_all, cb, 3, 1, "prn,pnm->mr")[0],
+    )
+
+    for i in range(ny.bit_length() - 1):
+        flat, (tok_grad, result_low) = summed_over(flat, "tensor", 1 << i, (tok_grad, result_low))
+    result_out = by_batch(result_low, other(result_low)).astype(F32)
+    skip_gathered = gather_rows(skip_grad[None])
+    for i in range(nz.bit_length() - 1):
+        if i == 0:
+            flat, (skip_rows_grad, skip_gathered) = summed_over(flat, "shard", 1, (skip_rows_grad, skip_gathered))
+        else:
+            flat, (triple_out, small_out) = summed_over(flat, "shard", 1 << i, (triple_out, small_out))
+    vectors = restored(flat, parts)
+    skip_grad_out = placed_out(skip_gathered, eb, 0, 1)[0].reshape(2, -1, width)
     shift_grad_out = lax.dot_general(
         silu_rows.astype(F32), vectors[7], (((0,), (0,)), ((), ())), precision=lax.Precision.HIGHEST
     )

time: 875 us -> 840 us (0.960)
  waiting for transfers between devices: 252 us -> 227 us
  other arithmetic: 155 us -> 141 us
  local copies, waits for them, and re-layouts: 147 us -> 156 us
    all_gather x4 -> x3, waiting for transfers between devices: 35.7 us -> 3.03 us  [gathered(): return lax.all_gather(values, ('tensor', 'shard'), axis=0, tiled=True)]
    ppermute x7 -> x8, waiting for transfers between devices: 13.6 us -> 45.4 us  [other(): return lax.ppermute(values, 'tensor', swap)]
    ppermute x45 -> x54, waiting for transfers between devices: 193 us -> 171 us  [flip(): return lax.ppermute(values, axis_name, [(i, i ^ bit) for i in range(count)])]
    dot_general x23, matrix products: 79.4 us -> 68.9 us  [contract(): return jnp.einsum(form, left_side, right_side, preferred_element_type=F32)]
    unnamed x513 -> x457, local copies, waits for them, and re-layouts: 48.5 us -> 49.9 us
    ppermute x45 -> x54, starting transfers between devices: 34 us -> 33.1 us  [flip(): return lax.ppermute(values, axis_name, [(i, i ^ bit) for i in range(count)])]
  transfers between devices with their start and end apart: 67 -> 77, of which waited for: 29 -> 26; matrix products, arithmetic and copies ran while one was open for 56% -> 59% of each run, Pallas kernels for 0% -> 0%
where the time goes in v5:
time: 840 us; the launch traced here: 830 us
  waiting for transfers between devices  227 us (27%)
  matrix products  227 us (27%)
  local copies, waits for them, and re-layouts  156 us (19%)
  other arithmetic  141 us (17%)
  starting transfers between devices  61.4 us (7%)
  between operations  18.1 us (2%)
    ppermute x54, waiting for transfers between devices, flip(): return lax.ppermute(values, axis_name, [(i, i ^ bit) for i in range(count)])  171 us
    dot_general x23, matrix products, contract(): return jnp.einsum(form, left_side, right_side, preferred_element_type=F32)  68.9 us
    dot_general x17, matrix products, matmul(): return jnp.dot(left_side, right_side, preferred_element_type=F32)  60.3 us
    dot_general x26, matrix products, contract_cols(): lax.dot_general(left_side, right_side, (((1,), (1,)), ((), ())), preferre...  50.1 us
    unnamed x457, local copies, waits for them, and re-layouts  49.9 us
    dot_general x16, matrix products, contract_rows(): lax.dot_general(left_side, right_side, (((0,), (0,)), ((), ())), preferre...  46.3 us
    ppermute x8, waiting for transfers between devices, other(): return lax.ppermute(values, 'tensor', swap)  45.4 us
    ppermute x54, starting transfers between devices, flip(): return lax.ppermute(values, axis_name, [(i, i ^ bit) for i in range(count)])  33.1 us
  transfers between devices with their start and end apart: 77, of which 26 were waited for; matrix products, arithmetic and copies ran while one was open for 59% of the time, Pallas kernels for 0%

profile of v5, /device:TPU:0, one launch (start us, length us, event | category | flops | bytes accessed | tf_op | source)
XLA Modules:
  0.0 830.5 jit_solution(2400769287620959302)
XLA Ops:
  20.0 28.6 %collective-permute-done = bf16[256,2816]{1,0:T(8,128)(2,1)} collective-permute-done((bf16[256,2816]{1,0:T(8,128)(2,1)}, bf16[256,2816]{1,0:T(8,128)(2,1)}, u32[]{:S(2)}, u32[]{:S(2)}) %collective-permute-start) | collective-permute-done | bytes 1441824 | tf_op jit(solution)/shard_map/ppermute | solution.py:126
  56.6 4.9 all-to-all-start.1
  62.8 4.7 constant_dynamic-slice_fusion.15
  73.8 5.1 all-to-all-start.2
  120.7 12.3 %collective-permute-done.3 = bf16[256,1408]{1,0:T(8,128)(2,1)} collective-permute-done((bf16[256,1408]{1,0:T(8,128)(2,1)}, bf16[256,1408]{1,0:T(8,128)(2,1)}, u32[]{:S(2)}, u32[]{:S(2)}) %collective-permute-start.3) | collective-permute-done | bytes 720928 | tf_op jit(solution)/shard_map/ppermute | solution.py:126
  139.4 4.3 convolution_add_fusion.15
  143.7 4.3 convolution_add_fusion.16
  154.9 8.2 multiply_reduce_fusion.1
  163.1 8.8 %fusion = f32[4,1024]{1,0:T(4,128)S(1)} fusion(f32[4,1024,1024]{1,2,0:T(8,128)} %get-tuple-element.455, f32[4,1024]{1,0:T(4,128)S(1)} %get-tuple-element.454), kind=kLoop, calls=%fused_computation.9 | loop fusion | flops 12578816 | bytes 16809984 | tf_op jit(solution)/shard_map/reduce_sum | solution.py:66
  171.9 7.8 fusion.128
  186.8 4.1 copy.152
  201.9 15.2 %collective-permute-done.12 = bf16[256,1408]{1,0:T(8,128)(2,1)S(1)} collective-permute-done((bf16[256,1408]{1,0:T(8,128)(2,1)}, bf16[256,1408]{1,0:T(8,128)(2,1)S(1)}, u32[]{:S(2)}, u32[]{:S(2)}) %collective-permute-start.12) | collective-permute-done | bytes 720928 | tf_op jit(solution)/shard_map/ppermute | solution.py:126
  219.5 27.1 %collective-permute-done.13 = bf16[1408,704]{0,1:T(8,128)(2,1)} collective-permute-done((bf16[1408,704]{0,1:T(8,128)(2,1)}, bf16[1408,704]{0,1:T(8,128)(2,1)}, u32[]{:S(2)}, u32[]{:S(2)}) %collective-permute-start.13) | collective-permute-done | bytes 1982496 | tf_op jit(solution)/shard_map/ppermute | solution.py:118
  254.6 8.9 %collective-permute-done.14 = bf16[256,1408]{1,0:T(8,128)(2,1)} collective-permute-done((bf16[256,1408]{1,0:T(8,128)(2,1)}, bf16[256,1408]{1,0:T(8,128)(2,1)}, u32[]{:S(2)}, u32[]{:S(2)}) %collective-permute-start.14) | collective-permute-done | bytes 720928 | tf_op jit(solution)/shard_map/ppermute | solution.py:126
  296.0 14.3 %collective-permute-done.18 = bf16[256,1408]{1,0:T(8,128)(2,1)S(1)} collective-permute-done((bf16[256,1408]{1,0:T(8,128)(2,1)S(1)}, bf16[256,1408]{1,0:T(8,128)(2,1)S(1)}, u32[]{:S(2)}, u32[]{:S(2)}) %collective-permute-start.18) | collective-permute-done | bytes 720928 | tf_op jit(solution)/shard_map/ppermute | solution.py:126
  318.6 13.6 %collective-permute-done.19 = bf16[256,1408]{1,0:T(8,128)(2,1)S(1)} collective-permute-done((bf16[256,1408]{1,0:T(8,128)(2,1)S(1)}, bf16[256,1408]{1,0:T(8,128)(2,1)S(1)}, u32[]{:S(2)}, u32[]{:S(2)}) %collective-permute-start.19) | collective-permute-done | bytes 720928 | tf_op jit(solution)/shard_map/ppermute | solution.py:126
  335.6 5.9 pad_maximum_fusion.7
  341.5 4.3 copy.155
  346.7 7.3 multiply_convert_fusion.2
  356.5 4.7 multiply_convert_fusion.3
  367.7 7.6 fusion.29
  375.4 4.1 fusion.22
  379.5 12.3 %collective-permute-done.22 = bf16[1,2816,352]{1,2,0:T(8,128)(2,1)} collective-permute-done((bf16[1,2816,352]{1,2,0:T(8,128)(2,1)}, bf16[1,2816,352]{1,2,0:T(8,128)(2,1)}, u32[]{:S(2)}, u32[]{:S(2)}) %collective-permute-start.22) | collective-permute-done | bytes 1982496 | tf_op jit(solution)/shard_map/ppermute | solution.py:126
  415.0 11.3 %collective-permute-done.24 = bf16[256,1408]{1,0:T(8,128)(2,1)S(1)} collective-permute-done((bf16[256,1408]{1,0:T(8,128)(2,1)S(1)}, bf16[256,1408]{1,0:T(8,128)(2,1)S(1)}, u32[]{:S(2)}, u32[]{:S(2)}) %collective-permute-start.24) | collective-permute-done | bytes 720928 | tf_op jit(solution)/shard_map/ppermute | solution.py:126
  430.3 4.9 convolution_convert_fusion
  435.7 10.4 %collective-permute-done.25 = bf16[256,1408]{1,0:T(8,128)(2,1)S(1)} collective-permute-done((bf16[256,1408]{1,0:T(8,128)(2,1)S(1)}, bf16[256,1408]{1,0:T(8,128)(2,1)S(1)}, u32[]{:S(2)}, u32[]{:S(2)}) %collective-permute-start.25) | collective-permute-done | bytes 720928 | tf_op jit(solution)/shard_map/ppermute | solution.py:126
  448.5 4.5 constant_dynamic-update-slice_fusion.3
  493.3 12.1 %collective-permute-done.29 = bf16[256,1408]{1,0:T(8,128)(2,1)S(1)} collective-permute-done((bf16[256,1408]{1,0:T(8,128)(2,1)S(1)}, bf16[256,1408]{1,0:T(8,128)(2,1)S(1)}, u32[]{:S(2)}, u32[]{:S(2)}) %collective-permute-start.29) | collective-permute-done | bytes 720928 | tf_op jit(solution)/shard_map/ppermute | solution.py:126
  514.0 11.6 %collective-permute-done.30 = bf16[256,1408]{1,0:T(8,128)(2,1)S(1)} collective-permute-done((bf16[256,1408]{1,0:T(8,128)(2,1)S(1)}, bf16[256,1408]{1,0:T(8,128)(2,1)S(1)}, u32[]{:S(2)}, u32[]{:S(2)}) %collective-permute-start.30) | collective-permute-done | bytes 720928 | tf_op jit(solution)/shard_map/ppermute | solution.py:126
  542.6 11.2 %multiply_reduce_fusion = (f32[4,1024]{1,0:T(4,128)S(1)}, f32[4,1024,1024]{1,2,0:T(8,128)}) fusion(f32[4,1024,1024]{1,2,0:T(8,128)} %get-tuple-element.455, f32[4,1024]{1,0:T(4,128)S(1)} %copy-done.122, bf16[1024,4,88]{0,2,1:T(8,128)(2,1)S(1)} %maximum_bitcast_fusion.1, bf16[1024,4,88]{0,2,1:T(8,128)(2,1)S(1)} %copy-done.70), kind=kOutput, calls=%fused_computation.5 | convolution fusion | flops 754970624 | bytes 35028992 | tf_op jit(solution)/shard_map/qhd,khd->hqk/dot_general | solution.py:18
  553.8 12.2 %multiply_convert_fusion = bf16[4,1024,1024]{1,2,0:T(8,128)(2,1)S(1)} fusion(f32[4,1024,1024]{1,2,0:T(8,128)} %get-tuple-element.469, f32[4,1024,1024]{1,2,0:T(8,128)} %get-tuple-element.455, f32[4,1024]{1,0:T(4,128)S(1)} %get-tuple-element.468, f32[4,1024]{1,0:T(4,128)S(1)} %copy-done.122), kind=kLoop, calls=%fused_computation.4 | loop fusion | flops 20971520 | bytes 41975808 | tf_op jit(solution)/shard_map/convert_element_type | solution.py:78
  577.1 3.9 fusion.124
  591.1 4.2 convert_add_fusion
  604.1 4.9 convolution_convert_fusion.4
  619.6 5.9 add_convert_fusion
  625.5 4.3 copy.180
  631.8 4.0 collective-permute-done.35
  637.3 7.0 collective-permute-done.36
  654.1 5.3 fusion.30
  659.3 5.6 all-to-all-done.3
  691.8 5.4 copy.170
  697.2 6.7 reshape.985
  706.7 7.1 collective-permute-done.40
  725.6 4.0 maximum_convert_fusion
  740.8 4.1 collective-permute-done.45
  782.7 6.8 fusion.10
  791.0 6.3 fusion.8
  804.1 6.5 collective-permute-done.53
  (972 shorter events, 424.2 us)
Async XLA Ops:
  7.2 71.7 %all-gather.6.cloned.1.call-start = ((), (), s32[]{:S(2)}) async-start(), calls=%async_computation.10 | async-start | bytes 2433024 | tf_op jit(solution)/shard_map/all_gather | solution.py:209
  9.3 130.1 %all-gather.8.cloned.1.call-start = ((), (), s32[]{:S(2)}) async-start(), calls=%async_computation.11 | async-start | bytes 4866048 | tf_op jit(solution)/shard_map/all_gather | solution.py:188
  13.8 34.8 %collective-permute-start = (bf16[256,2816]{1,0:T(8,128)(2,1)}, bf16[256,2816]{1,0:T(8,128)(2,1)}, u32[]{:S(2)}, u32[]{:S(2)}) collective-permute-start(bf16[256,2816]{1,0:T(8,128)(2,1)} %pad_maximum_fusion.16), channel_id=1, source_target_pairs={{0,4},{2,6},{4,0},{6,2},{1,5},{3,7},{5,1},{7,3},{8,12},{10,14},{12... | collective-permute-start | bytes 4325384 | tf_op jit(solution)/shard_map/ppermute | solution.py:126
  51.9 28.8 %collective-permute-start.1 = (bf16[512,2816]{1,0:T(8,128)(2,1)}, bf16[512,2816]{1,0:T(8,128)(2,1)}, u32[]{:S(2)}, u32[]{:S(2)}) collective-permute-start(bf16[512,2816]{1,0:T(8,128)(2,1)} %pad_maximum_fusion.4), channel_id=1, source_target_pairs={{0,2},{2,0},{4,6},{6,4},{1,3},{3,1},{5,7},{7,5},{8,10},{10,8},{12,... | collective-permute-start | bytes 8650760 | tf_op jit(solution)/shard_map/ppermute | solution.py:126
  53.8 79.4 %collective-permute-start.7 = (s32[256,2]{0,1:T(2,128)}, s32[256,2]{0,1:T(2,128)}, u32[]{:S(2)}, u32[]{:S(2)}) collective-permute-start(s32[256,2]{0,1:T(2,128)} %fusion.208), channel_id=1, source_target_pairs={{0,2},{2,0},{4,6},{6,4},{1,3},{3,1},{5,7},{7,5},{8,10},{10,8},{12,... | collective-permute-start | bytes 6152 | tf_op jit(solution)/shard_map/ppermute | solution.py:126
  54.3 66.0 %collective-permute-start.6 = (s32[256,2]{0,1:T(2,128)}, s32[256,2]{0,1:T(2,128)}, u32[]{:S(2)}, u32[]{:S(2)}) collective-permute-start(s32[256,2]{0,1:T(2,128)} %fusion.208), channel_id=1, source_target_pairs={{0,4},{2,6},{4,0},{6,2},{1,5},{3,7},{5,1},{7,3},{8,12},{10,14},{12... | collective-permute-start | bytes 6152 | tf_op jit(solution)/shard_map/ppermute | solution.py:126
  73.8 17.6 %all-to-all-start.2 = ((f32[4,1,1408]{2,1,0:T(1,128)}), f32[4,1,1408]{2,1,0:T(1,128)S(1)}, u32[]{:S(2)}, u32[]{:S(2)}) async-start(f32[4,1,1408]{2,1,0:T(1,128)} %all_to_all.32), calls=%async_computation.2 | async-start | bytes 45056 | tf_op jit(solution)/shard_map/all_to_all | solution.py:235
  94.9 91.9 %all-gather.12.cloned.1.call-start = ((), (), s32[]{:S(2)}) async-start(), calls=%async_computation.13 | async-start | bytes 2703360 | tf_op jit(solution)/shard_map/all_gather | solution.py:212
  115.0 18.0 %collective-permute-start.3 = (bf16[256,1408]{1,0:T(8,128)(2,1)}, bf16[256,1408]{1,0:T(8,128)(2,1)}, u32[]{:S(2)}, u32[]{:S(2)}) collective-permute-start(bf16[256,1408]{1,0:T(8,128)(2,1)} %add_convert_fusion.7), channel_id=1, source_target_pairs={{0,4},{2,6},{4,0},{6,2},{1,5},{3,7},{5,1},{7,3},{8,12},{10,14},{12... | collective-permute-start | bytes 2162696 | tf_op jit(solution)/shard_map/ppermute | solution.py:126
  117.0 196.4 %all-gather.14.cloned.1.call-start = ((), (), s32[]{:S(2)}) async-start(), calls=%async_computation.14 | async-start | bytes 4866048 | tf_op jit(solution)/shard_map/all_gather | solution.py:188
  153.4 26.4 %collective-permute-start.9 = (bf16[256,1408]{1,0:T(8,128)(2,1)S(1)}, bf16[256,1408]{1,0:T(8,128)(2,1)S(1)}, u32[]{:S(2)}, u32[]{:S(2)}) collective-permute-start(bf16[256,1408]{1,0:T(8,128)(2,1)S(1)} %get-tuple-element.99), channel_id=1, source_target_pairs={{0,4},{2,6},{4,0},{6,2},{1,5},{3,7},{5,1},{7,3},{8,12},{10,14},{12... | collective-permute-start | bytes 2162696 | tf_op jit(solution)/shard_map/ppermute | solution.py:126
  190.9 55.8 %collective-permute-start.13 = (bf16[1408,704]{0,1:T(8,128)(2,1)}, bf16[1408,704]{0,1:T(8,128)(2,1)}, u32[]{:S(2)}, u32[]{:S(2)}) collective-permute-start(bf16[1408,704]{0,1:T(8,128)(2,1)} %copy.152), channel_id=1, source_target_pairs={{0,1},{1,0},{2,3},{3,2},{4,5},{5,4},{6,7},{7,6},{8,9},{9,8},{10,11... | collective-permute-start | bytes 5947400 | tf_op jit(solution)/shard_map/ppermute | solution.py:118
  199.5 17.6 %collective-permute-start.12 = (bf16[256,1408]{1,0:T(8,128)(2,1)}, bf16[256,1408]{1,0:T(8,128)(2,1)S(1)}, u32[]{:S(2)}, u32[]{:S(2)}) collective-permute-start(bf16[256,1408]{1,0:T(8,128)(2,1)} %slice.958), channel_id=1, source_target_pairs={{0,4},{2,6},{4,0},{6,2},{1,5},{3,7},{5,1},{7,3},{8,12},{10,14},{12... | collective-permute-start | bytes 2162696 | tf_op jit(solution)/shard_map/ppermute | solution.py:126
  201.8 165.9 %all-gather.10.cloned.1.call-start = ((), (), s32[]{:S(2)}) async-start(), calls=%async_computation.12 | async-start | bytes 4866048 | tf_op jit(solution)/shard_map/all_gather | solution.py:188
  284.1 255.1 %reduce-scatter.13.cloned.1.call-start = ((), (), s32[]{:S(2)}) async-start(), calls=%async_computation.15 | async-start | bytes 4866048 | tf_op jit(solution)/shard_map/reduce_scatter | solution.py:335
  291.8 18.5 %collective-permute-start.18 = (bf16[256,1408]{1,0:T(8,128)(2,1)S(1)}, bf16[256,1408]{1,0:T(8,128)(2,1)S(1)}, u32[]{:S(2)}, u32[]{:S(2)}) collective-permute-start(bf16[256,1408]{1,0:T(8,128)(2,1)S(1)} %slice.957), channel_id=1, source_target_pairs={{0,4},{2,6},{4,0},{6,2},{1,5},{3,7},{5,1},{7,3},{8,12},{10,14},{12... | collective-permute-start | bytes 2162696 | tf_op jit(solution)/shard_map/ppermute | solution.py:126
  295.9 36.4 %collective-permute-start.10 = (bf16[512,1408]{1,0:T(8,128)(2,1)}, bf16[512,1408]{1,0:T(8,128)(2,1)}, u32[]{:S(2)}, u32[]{:S(2)}) collective-permute-start(bf16[512,1408]{1,0:T(8,128)(2,1)} %pad_maximum_fusion.17), channel_id=1, source_target_pairs={{0,2},{2,0},{4,6},{6,4},{1,3},{3,1},{5,7},{7,5},{8,10},{10,8},{12,... | collective-permute-start | bytes 4325384 | tf_op jit(solution)/shard_map/ppermute | solution.py:126
  314.5 17.7 %collective-permute-start.19 = (bf16[256,1408]{1,0:T(8,128)(2,1)S(1)}, bf16[256,1408]{1,0:T(8,128)(2,1)S(1)}, u32[]{:S(2)}, u32[]{:S(2)}) collective-permute-start(bf16[256,1408]{1,0:T(8,128)(2,1)S(1)} %add_convert_fusion.5), channel_id=1, source_target_pairs={{0,4},{2,6},{4,0},{6,2},{1,5},{3,7},{5,1},{7,3},{8,12},{10,14},{12... | collective-permute-start | bytes 2162696 | tf_op jit(solution)/shard_map/ppermute | solution.py:126
  318.5 16.4 %collective-permute-start.20 = (bf16[256,1408]{1,0:T(8,128)(2,1)S(1)}, bf16[256,1408]{1,0:T(8,128)(2,1)S(1)}, u32[]{:S(2)}, u32[]{:S(2)}) collective-permute-start(bf16[256,1408]{1,0:T(8,128)(2,1)S(1)} %add_convert_fusion.5), channel_id=1, source_target_pairs={{0,2},{2,0},{4,6},{6,4},{1,3},{3,1},{5,7},{7,5},{8,10},{10,8},{12,... | collective-permute-start | bytes 2162696 | tf_op jit(solution)/shard_map/ppermute | solution.py:126
  345.8 46.0 %collective-permute-start.22 = (bf16[1,2816,352]{1,2,0:T(8,128)(2,1)}, bf16[1,2816,352]{1,2,0:T(8,128)(2,1)}, u32[]{:S(2)}, u32[]{:S(2)}) collective-permute-start(bf16[1,2816,352]{1,2,0:T(8,128)(2,1)} %bitcast.451), channel_id=1, source_target_pairs={{0,4},{2,6},{4,0},{6,2},{1,5},{3,7},{5,1},{7,3},{8,12},{10,14},{12... | collective-permute-start | bytes 5947400 | tf_op jit(solution)/shard_map/ppermute | solution.py:126
  367.2 221.0 %reduce-scatter.15.cloned.1.call-start = ((), (), s32[]{:S(2)}) async-start(), calls=%async_computation.16 | async-start | bytes 4866048 | tf_op jit(solution)/shard_map/reduce_scatter | solution.py:335
  407.7 18.6 %collective-permute-start.24 = (bf16[256,1408]{1,0:T(8,128)(2,1)S(1)}, bf16[256,1408]{1,0:T(8,128)(2,1)S(1)}, u32[]{:S(2)}, u32[]{:S(2)}) collective-permute-start(bf16[256,1408]{1,0:T(8,128)(2,1)S(1)} %slice.956), channel_id=1, source_target_pairs={{0,4},{2,6},{4,0},{6,2},{1,5},{3,7},{5,1},{7,3},{8,12},{10,14},{12... | collective-permute-start | bytes 2162696 | tf_op jit(solution)/shard_map/ppermute | solution.py:126
  428.3 17.7 %collective-permute-start.25 = (bf16[256,1408]{1,0:T(8,128)(2,1)S(1)}, bf16[256,1408]{1,0:T(8,128)(2,1)S(1)}, u32[]{:S(2)}, u32[]{:S(2)}) collective-permute-start(bf16[256,1408]{1,0:T(8,128)(2,1)S(1)} %get-tuple-element.318), channel_id=1, source_target_pairs={{0,4},{2,6},{4,0},{6,2},{1,5},{3,7},{5,1},{7,3},{8,12},{10,14},{12... | collective-permute-start | bytes 2162696 | tf_op jit(solution)/shard_map/ppermute | solution.py:126
  429.7 98.1 %collective-permute-start.46 = (bf16[2,2816,352]{1,2,0:T(8,128)(2,1)}, bf16[2,2816,352]{1,2,0:T(8,128)(2,1)}, u32[]{:S(2)}, u32[]{:S(2)}) collective-permute-start(bf16[2,2816,352]{1,2,0:T(8,128)(2,1)} %pad_maximum_fusion.2), channel_id=1, source_target_pairs={{0,2},{2,0},{4,6},{6,4},{1,3},{3,1},{5,7},{7,5},{8,10},{10,8},{12,... | collective-permute-start | bytes 11894792 | tf_op jit(solution)/shard_map/ppermute | solution.py:126
  435.2 19.6 %collective-permute-start.26 = (bf16[256,1408]{1,0:T(8,128)(2,1)S(1)}, bf16[256,1408]{1,0:T(8,128)(2,1)}, u32[]{:S(2)}, u32[]{:S(2)}) collective-permute-start(bf16[256,1408]{1,0:T(8,128)(2,1)S(1)} %get-tuple-element.318), channel_id=1, source_target_pairs={{0,2},{2,0},{4,6},{6,4},{1,3},{3,1},{5,7},{7,5},{8,10},{10,8},{12,... | collective-permute-start | bytes 2162696 | tf_op jit(solution)/shard_map/ppermute | solution.py:126
  448.4 181.5 %reduce-scatter.19.cloned.1.call-start = ((), (), s32[]{:S(2)}) async-start(), calls=%async_computation.18 | async-start | bytes 1351680
  487.2 18.2 %collective-permute-start.29 = (bf16[256,1408]{1,0:T(8,128)(2,1)S(1)}, bf16[256,1408]{1,0:T(8,128)(2,1)S(1)}, u32[]{:S(2)}, u32[]{:S(2)}) collective-permute-start(bf16[256,1408]{1,0:T(8,128)(2,1)S(1)} %slice.955), channel_id=1, source_target_pairs={{0,4},{2,6},{4,0},{6,2},{1,5},{3,7},{5,1},{7,3},{8,12},{10,14},{12... | collective-permute-start | bytes 2162696 | tf_op jit(solution)/shard_map/ppermute | solution.py:126
  508.3 17.4 %collective-permute-start.30 = (bf16[256,1408]{1,0:T(8,128)(2,1)S(1)}, bf16[256,1408]{1,0:T(8,128)(2,1)S(1)}, u32[]{:S(2)}, u32[]{:S(2)}) collective-permute-start(bf16[256,1408]{1,0:T(8,128)(2,1)S(1)} %get-tuple-element.320), channel_id=1, source_target_pairs={{0,4},{2,6},{4,0},{6,2},{1,5},{3,7},{5,1},{7,3},{8,12},{10,14},{12... | collective-permute-start | bytes 2162696 | tf_op jit(solution)/shard_map/ppermute | solution.py:126
  514.0 16.4 %collective-permute-start.31 = (bf16[256,1408]{1,0:T(8,128)(2,1)S(1)}, bf16[256,1408]{1,0:T(8,128)(2,1)S(1)}, u32[]{:S(2)}, u32[]{:S(2)}) collective-permute-start(bf16[256,1408]{1,0:T(8,128)(2,1)S(1)} %get-tuple-element.320), channel_id=1, source_target_pairs={{0,2},{2,0},{4,6},{6,4},{1,3},{3,1},{5,7},{7,5},{8,10},{10,8},{12,... | collective-permute-start | bytes 2162696 | tf_op jit(solution)/shard_map/ppermute | solution.py:126
  539.2 44.4 %collective-permute-start.37 = (bf16[1,768,352]{1,2,0:T(8,128)(2,1)}, bf16[1,768,352]{1,2,0:T(8,128)(2,1)}, u32[]{:S(2)}, u32[]{:S(2)}) collective-permute-start(bf16[1,768,352]{1,2,0:T(8,128)(2,1)} %bitcast.513), channel_id=1, source_target_pairs={{0,4},{2,6},{4,0},{6,2},{1,5},{3,7},{5,1},{7,3},{8,12},{10,14},{12... | collective-permute-start | bytes 1622024 | tf_op jit(solution)/shard_map/ppermute | solution.py:126
  540.1 50.9 %collective-permute-start.39 = (bf16[512,1408]{1,0:T(8,128)(2,1)}, bf16[512,1408]{1,0:T(8,128)(2,1)}, u32[]{:S(2)}, u32[]{:S(2)}) collective-permute-start(bf16[512,1408]{1,0:T(8,128)(2,1)} %fusion.32), channel_id=1, source_target_pairs={{0,2},{2,0},{4,6},{6,4},{1,3},{3,1},{5,7},{7,5},{8,10},{10,8},{12,... | collective-permute-start | bytes 4325384 | tf_op jit(solution)/shard_map/ppermute | solution.py:126
  540.4 58.0 %collective-permute-start.33 = (bf16[1408,880]{0,1:T(8,128)(2,1)}, bf16[1408,880]{0,1:T(8,128)(2,1)}, u32[]{:S(2)}, u32[]{:S(2)}) collective-permute-start(bf16[1408,880]{0,1:T(8,128)(2,1)} %pad_maximum_fusion.11), channel_id=1, source_target_pairs={{0,1},{1,0},{2,3},{3,2},{4,5},{5,4},{6,7},{7,6},{8,9},{9,8},{10,11... | collective-permute-start | bytes 7434248 | tf_op jit(solution)/shard_map/ppermute | solution.py:118
  590.6 128.0 %reduce-scatter.21.cloned.1.call-start = ((), (), s32[]{:S(2)}) async-start(), calls=%async_computation.19 | async-start | bytes 3153920
  609.5 34.8 %collective-permute-start.36 = (bf16[1408,528]{0,1:T(8,128)(2,1)}, bf16[1408,528]{0,1:T(8,128)(2,1)}, u32[]{:S(2)}, u32[]{:S(2)}) collective-permute-start(bf16[1408,528]{0,1:T(8,128)(2,1)} %convolution_convert_fusion.4), channel_id=1, source_target_pairs={{0,1},{1,0},{2,3},{3,2},{4,5},{5,4},{6,7},{7,6},{8,9},{9,8},{10,11... | collective-permute-start | bytes 4460552 | tf_op jit(solution)/shard_map/ppermute | solution.py:118
  617.7 18.1 %collective-permute-start.35 = (bf16[256,1408]{1,0:T(8,128)(2,1)S(1)}, bf16[256,1408]{1,0:T(8,128)(2,1)S(1)}, u32[]{:S(2)}, u32[]{:S(2)}) collective-permute-start(bf16[256,1408]{1,0:T(8,128)(2,1)S(1)} %slice.954), channel_id=1, source_target_pairs={{0,4},{2,6},{4,0},{6,2},{1,5},{3,7},{5,1},{7,3},{8,12},{10,14},{12... | collective-permute-start | bytes 2162696 | tf_op jit(solution)/shard_map/ppermute | solution.py:126
  654.0 66.4 %reduce-scatter.23.cloned.1.call-start = ((), (), s32[]{:S(2)}) async-start(), calls=%async_computation.20 | async-start | bytes 2252800
  672.0 16.9 %collective-permute-start.60 = (bf16[1,352,768]{2,1,0:T(8,128)(2,1)S(1)}, bf16[1,352,768]{2,1,0:T(8,128)(2,1)}, u32[]{:S(2)}, u32[]{:S(2)}) collective-permute-start(bf16[1,352,768]{2,1,0:T(8,128)(2,1)S(1)} %bitcast.512), channel_id=1, source_target_pairs={{0,4},{2,6},{4,0},{6,2},{1,5},{3,7},{5,1},{7,3},{8,12},{10,14},{12... | collective-permute-start | bytes 1622024 | tf_op jit(solution)/shard_map/ppermute | solution.py:126
  677.1 103.6 %reduce-scatter.17.cloned.1.call-start = ((), (), s32[]{:S(2)}) async-start(), calls=%async_computation.17 | async-start | bytes 1351680 | tf_op jit(solution)/shard_map/reduce_scatter | solution.py:458
  684.7 19.2 %collective-permute-start.41 = (bf16[256,1408]{1,0:T(8,128)(2,1)}, bf16[256,1408]{1,0:T(8,128)(2,1)}, u32[]{:S(2)}, u32[]{:S(2)}) collective-permute-start(bf16[256,1408]{1,0:T(8,128)(2,1)} %slice.953), channel_id=1, source_target_pairs={{0,4},{2,6},{4,0},{6,2},{1,5},{3,7},{5,1},{7,3},{8,12},{10,14},{12... | collective-permute-start | bytes 2162696 | tf_op jit(solution)/shard_map/ppermute | solution.py:126
  688.7 25.1 %collective-permute-start.40 = (bf16[2,4,176,352]{3,2,1,0:T(8,128)(2,1)}, bf16[2,4,176,352]{3,2,1,0:T(8,128)(2,1)}, u32[]{:S(2)}, u32[]{:S(2)}) collective-permute-start(bf16[2,4,176,352]{3,2,1,0:T(8,128)(2,1)} %dynamic-slice_bitcast_fusion), channel_id=1, source_target_pairs={{0,1},{1,0},{2,3},{3,2},{4,5},{5,4},{6,7},{7,6},{8,9},{9,8},{10,11... | collective-permute-start | bytes 2973704 | tf_op jit(solution)/shard_map/ppermute | solution.py:118
  691.4 23.8 %collective-permute-start.61 = (bf16[2,352,768]{2,1,0:T(8,128)(2,1)}, bf16[2,352,768]{2,1,0:T(8,128)(2,1)}, u32[]{:S(2)}, u32[]{:S(2)}) collective-permute-start(bf16[2,352,768]{2,1,0:T(8,128)(2,1)} %pad_maximum_fusion.22), channel_id=1, source_target_pairs={{0,2},{2,0},{4,6},{6,4},{1,3},{3,1},{5,7},{7,5},{8,10},{10,8},{12,... | collective-permute-start | bytes 3244040 | tf_op jit(solution)/shard_map/ppermute | solution.py:126
  725.1 19.8 %collective-permute-start.45 = (bf16[256,1408]{1,0:T(8,128)(2,1)S(1)}, bf16[256,1408]{1,0:T(8,128)(2,1)}, u32[]{:S(2)}, u32[]{:S(2)}) collective-permute-start(bf16[256,1408]{1,0:T(8,128)(2,1)S(1)} %get-tuple-element.145), channel_id=1, source_target_pairs={{0,1},{1,0},{2,3},{3,2},{4,5},{5,4},{6,7},{7,6},{8,9},{9,8},{10,11... | collective-permute-start | bytes 2162696 | tf_op jit(solution)/shard_map/ppermute | solution.py:118
  736.5 28.5 %collective-permute-start.55 = (bf16[1,352,528]{1,2,0:T(8,128)(2,1)}, bf16[1,352,528]{1,2,0:T(8,128)(2,1)S(1)}, u32[]{:S(2)}, u32[]{:S(2)}) collective-permute-start(bf16[1,352,528]{1,2,0:T(8,128)(2,1)} %bitcast.124), channel_id=1, source_target_pairs={{0,2},{2,0},{4,6},{6,4},{1,3},{3,1},{5,7},{7,5},{8,10},{10,8},{12,... | collective-permute-start | bytes 1115144 | tf_op jit(solution)/shard_map/ppermute | solution.py:126
  739.0 24.5 %collective-permute-start.58 = (bf16[1,352,880]{2,1,0:T(8,128)(2,1)}, bf16[1,352,880]{2,1,0:T(8,128)(2,1)}, u32[]{:S(2)}, u32[]{:S(2)}) collective-permute-start(bf16[1,352,880]{2,1,0:T(8,128)(2,1)} %copy.165), channel_id=1, source_target_pairs={{0,2},{2,0},{4,6},{6,4},{1,3},{3,1},{5,7},{7,5},{8,10},{10,8},{12,... | collective-permute-start | bytes 1858568 | tf_op jit(solution)/shard_map/ppermute | solution.py:126
  739.3 22.8 %collective-permute-start.57 = (bf16[1,352,880]{2,1,0:T(8,128)(2,1)}, bf16[1,352,880]{2,1,0:T(8,128)(2,1)}, u32[]{:S(2)}, u32[]{:S(2)}) collective-permute-start(bf16[1,352,880]{2,1,0:T(8,128)(2,1)} %copy.165), channel_id=1, source_target_pairs={{0,4},{2,6},{4,0},{6,2},{1,5},{3,7},{5,1},{7,3},{8,12},{10,14},{12... | collective-permute-start | bytes 1858568 | tf_op jit(solution)/shard_map/ppermute | solution.py:126
  744.9 44.7 %collective-permute-start.44 = (f32[352,128]{1,0:T(8,128)S(1)}, f32[352,128]{1,0:T(8,128)}, u32[]{:S(2)}, u32[]{:S(2)}) collective-permute-start(f32[352,128]{1,0:T(8,128)S(1)} %add.915), channel_id=1, source_target_pairs={{0,1},{1,0},{2,3},{3,2},{4,5},{5,4},{6,7},{7,6},{8,9},{9,8},{10,11... | collective-permute-start | bytes 540680 | tf_op jit(solution)/shard_map/ppermute | solution.py:126
  780.7 18.1 %collective-permute-start.50 = (bf16[1,352,352]{2,1,0:T(8,128)(2,1)}, bf16[1,352,352]{2,1,0:T(8,128)(2,1)S(1)}, u32[]{:S(2)}, u32[]{:S(2)}) collective-permute-start(bf16[1,352,352]{2,1,0:T(8,128)(2,1)} %bitcast.523), channel_id=1, source_target_pairs={{0,2},{2,0},{4,6},{6,4},{1,3},{3,1},{5,7},{7,5},{8,10},{10,8},{12,... | collective-permute-start | bytes 743432 | tf_op jit(solution)/shard_map/ppermute | solution.py:126
  797.4 22.5 %collective-permute-start.47 = (bf16[256,1408]{1,0:T(8,128)(2,1)S(1)}, bf16[256,1408]{1,0:T(8,128)(2,1)}, u32[]{:S(2)}, u32[]{:S(2)}) collective-permute-start(bf16[256,1408]{1,0:T(8,128)(2,1)S(1)} %copy-done.68), channel_id=1, source_target_pairs={{0,1},{1,0},{2,3},{3,2},{4,5},{5,4},{6,7},{7,6},{8,9},{9,8},{10,11... | collective-permute-start | bytes 2162696 | tf_op jit(solution)/shard_map/ppermute | solution.py:118
  (252 other events, 2731.2 us)
Sparse Core Ops, SparseCore 0:
  10.8 52.5 all-gather.5
  66.0 73.3 all-gather.7
  141.5 45.2 all-gather.11
  201.9 78.1 all-gather.13
  284.2 72.7 all-gather.9
  367.3 89.0 reduce-scatter.12
  460.6 89.8 reduce-scatter.14
  590.7 23.1 reduce-scatter.18
  630.0 49.1 reduce-scatter.20
  681.9 38.4 reduce-scatter.22
  729.8 26.8 reduce-scatter.16

commit v6 on v5

--- a/solution.py
+++ b/solution.py
@@ -384,7 +384,7 @@
     resid_two_grad = grad_out + third_grads[0]
     grad_two_low = resid_two_grad.astype(BF)
     grad_two_all = gather_rows(grad_two_low)
-    down_grad = reduced(down_sum).T
+    down_grad = reduced(down_sum)
     cross_out_grad = [contract_rows(grad_two_all, p).astype(BF) for p in cross_parts]
     cross_mix_grad = to_heads([matmul(grad_two_all, w).astype(BF) for w in cross_out_full], 1)[:, 0]
     cq_back, ck_back, cv_back = attention_backward(cq, ck, cv, cross_sums, cross_mix_grad)
@@ -549,7 +549,7 @@
         triple_out,
         *small_out,
         wide_out(up_grad),
-        rows_out(down_grad),
+        wide_out(down_grad).T,
     ) + tuple(vectors[:7])
 
 

time: 840 us -> 859 us (1.023)
  waiting for transfers between devices: 227 us -> 249 us
  other arithmetic: 141 us -> 157 us
  local copies, waits for them, and re-layouts: 156 us -> 141 us
  matrix products: 227 us -> 237 us
    ppermute x54, waiting for transfers between devices: 171 us -> 203 us  [flip(): return lax.ppermute(values, axis_name, [(i, i ^ bit) for i in range(count)])]
    convert_element_type x2 -> x0, local copies, waits for them, and re-layouts: 12.1 us -> none  [rows_out(): return values.reshape(-1, rows).astype(F32)]
    reduce_sum x2, other arithmetic: 9.73 us -> 21.3 us  [attention_forward(): weight_sum = jnp.sum(exponent, -1, keepdims=True)]
    unnamed x457 -> x461, local copies, waits for them, and re-layouts: 49.9 us -> 50 us
where the time goes in v6:
time: 859 us; the launch traced here: 855 us
  waiting for transfers between devices  249 us (29%)
  matrix products  237 us (28%)
  other arithmetic  157 us (18%)
  local copies, waits for them, and re-layouts  141 us (16%)
  starting transfers between devices  53.9 us (6%)
  between operations  18.1 us (2%)
    ppermute x54, waiting for transfers between devices, flip(): return lax.ppermute(values, axis_name, [(i, i ^ bit) for i in range(count)])  203 us
    dot_general x23, matrix products, contract(): return jnp.einsum(form, left_side, right_side, preferred_element_type=F32)  74.4 us
    dot_general x17, matrix products, matmul(): return jnp.dot(left_side, right_side, preferred_element_type=F32)  60.2 us
    dot_general x26, matrix products, contract_cols(): lax.dot_general(left_side, right_side, (((1,), (1,)), ((), ())), preferre...  54.3 us
    unnamed x461, local copies, waits for them, and re-layouts  50 us
    dot_general x16, matrix products, contract_rows(): lax.dot_general(left_side, right_side, (((0,), (0,)), ((), ())), preferre...  46.1 us
    ppermute x8, waiting for transfers between devices, other(): return lax.ppermute(values, 'tensor', swap)  39.2 us
    ppermute x54, starting transfers between devices, flip(): return lax.ppermute(values, axis_name, [(i, i ^ bit) for i in range(count)])  26.6 us
  transfers between devices with their start and end apart: 77, of which 26 were waited for; matrix products, arithmetic and copies ran while one was open for 59% of the time, Pallas kernels for 0%

profile of v6, /device:TPU:0, one launch (start us, length us, event | category | flops | bytes accessed | tf_op | source)
XLA Modules:
  0.0 855.2 jit_solution(13984250223418686298)
XLA Ops:
  20.0 28.6 %collective-permute-done = bf16[256,2816]{1,0:T(8,128)(2,1)} collective-permute-done((bf16[256,2816]{1,0:T(8,128)(2,1)}, bf16[256,2816]{1,0:T(8,128)(2,1)}, u32[]{:S(2)}, u32[]{:S(2)}) %collective-permute-start) | collective-permute-done | bytes 1441824 | tf_op jit(solution)/shard_map/ppermute | solution.py:126
  56.6 4.9 all-to-all-start.1
  62.8 4.7 constant_dynamic-slice_fusion.15
  73.8 5.1 all-to-all-start.2
  120.5 12.6 %collective-permute-done.3 = bf16[256,1408]{1,0:T(8,128)(2,1)} collective-permute-done((bf16[256,1408]{1,0:T(8,128)(2,1)}, bf16[256,1408]{1,0:T(8,128)(2,1)}, u32[]{:S(2)}, u32[]{:S(2)}) %collective-permute-start.3) | collective-permute-done | bytes 720928 | tf_op jit(solution)/shard_map/ppermute | solution.py:126
  139.4 4.3 convolution_add_fusion.15
  143.7 4.3 convolution_add_fusion.16
  154.9 8.2 multiply_reduce_fusion.1
  163.1 20.3 %fusion = f32[4,1024]{1,0:T(4,128)S(1)} fusion(f32[4,1024,1024]{1,2,0:T(8,128)} %get-tuple-element.459, f32[4,1024]{1,0:T(4,128)S(1)} %get-tuple-element.458), kind=kLoop, calls=%fused_computation.9 | loop fusion | flops 12578816 | bytes 16809984 | tf_op jit(solution)/shard_map/reduce_sum | solution.py:66
  183.5 7.7 fusion.128
  197.7 4.1 copy.148
  210.9 16.9 %collective-permute-done.12 = bf16[256,1408]{1,0:T(8,128)(2,1)S(1)} collective-permute-done((bf16[256,1408]{1,0:T(8,128)(2,1)}, bf16[256,1408]{1,0:T(8,128)(2,1)S(1)}, u32[]{:S(2)}, u32[]{:S(2)}) %collective-permute-start.12) | collective-permute-done | bytes 720928 | tf_op jit(solution)/shard_map/ppermute | solution.py:126
  230.3 27.4 %collective-permute-done.13 = bf16[1408,704]{0,1:T(8,128)(2,1)} collective-permute-done((bf16[1408,704]{0,1:T(8,128)(2,1)}, bf16[1408,704]{0,1:T(8,128)(2,1)}, u32[]{:S(2)}, u32[]{:S(2)}) %collective-permute-start.13) | collective-permute-done | bytes 1982496 | tf_op jit(solution)/shard_map/ppermute | solution.py:118
  264.4 12.1 %collective-permute-done.14 = bf16[256,1408]{1,0:T(8,128)(2,1)} collective-permute-done((bf16[256,1408]{1,0:T(8,128)(2,1)}, bf16[256,1408]{1,0:T(8,128)(2,1)}, u32[]{:S(2)}, u32[]{:S(2)}) %collective-permute-start.14) | collective-permute-done | bytes 720928 | tf_op jit(solution)/shard_map/ppermute | solution.py:126
  308.3 14.8 %collective-permute-done.18 = bf16[256,1408]{1,0:T(8,128)(2,1)S(1)} collective-permute-done((bf16[256,1408]{1,0:T(8,128)(2,1)S(1)}, bf16[256,1408]{1,0:T(8,128)(2,1)S(1)}, u32[]{:S(2)}, u32[]{:S(2)}) %collective-permute-start.18) | collective-permute-done | bytes 720928 | tf_op jit(solution)/shard_map/ppermute | solution.py:126
  330.7 14.3 %collective-permute-done.19 = bf16[256,1408]{1,0:T(8,128)(2,1)S(1)} collective-permute-done((bf16[256,1408]{1,0:T(8,128)(2,1)S(1)}, bf16[256,1408]{1,0:T(8,128)(2,1)S(1)}, u32[]{:S(2)}, u32[]{:S(2)}) %collective-permute-start.19) | collective-permute-done | bytes 720928 | tf_op jit(solution)/shard_map/ppermute | solution.py:126
  348.4 5.9 pad_maximum_fusion.7
  354.3 4.5 copy.151
  359.3 7.3 multiply_convert_fusion.2
  369.1 4.7 multiply_convert_fusion.3
  380.1 7.6 fusion.29
  387.7 4.1 fusion.22
  391.8 12.9 %collective-permute-done.22 = bf16[1,2816,352]{1,2,0:T(8,128)(2,1)} collective-permute-done((bf16[1,2816,352]{1,2,0:T(8,128)(2,1)}, bf16[1,2816,352]{1,2,0:T(8,128)(2,1)}, u32[]{:S(2)}, u32[]{:S(2)}) %collective-permute-start.22) | collective-permute-done | bytes 1982496 | tf_op jit(solution)/shard_map/ppermute | solution.py:126
  427.8 11.7 %collective-permute-done.24 = bf16[256,1408]{1,0:T(8,128)(2,1)S(1)} collective-permute-done((bf16[256,1408]{1,0:T(8,128)(2,1)S(1)}, bf16[256,1408]{1,0:T(8,128)(2,1)S(1)}, u32[]{:S(2)}, u32[]{:S(2)}) %collective-permute-start.24) | collective-permute-done | bytes 720928 | tf_op jit(solution)/shard_map/ppermute | solution.py:126
  443.2 4.9 convolution_convert_fusion
  448.5 10.8 %collective-permute-done.25 = bf16[256,1408]{1,0:T(8,128)(2,1)S(1)} collective-permute-done((bf16[256,1408]{1,0:T(8,128)(2,1)S(1)}, bf16[256,1408]{1,0:T(8,128)(2,1)S(1)}, u32[]{:S(2)}, u32[]{:S(2)}) %collective-permute-start.25) | collective-permute-done | bytes 720928 | tf_op jit(solution)/shard_map/ppermute | solution.py:126
  461.7 4.5 constant_dynamic-update-slice_fusion.3
  504.8 12.4 %collective-permute-done.29 = bf16[256,1408]{1,0:T(8,128)(2,1)S(1)} collective-permute-done((bf16[256,1408]{1,0:T(8,128)(2,1)S(1)}, bf16[256,1408]{1,0:T(8,128)(2,1)S(1)}, u32[]{:S(2)}, u32[]{:S(2)}) %collective-permute-start.29) | collective-permute-done | bytes 720928 | tf_op jit(solution)/shard_map/ppermute | solution.py:126
  525.6 11.9 %collective-permute-done.30 = bf16[256,1408]{1,0:T(8,128)(2,1)S(1)} collective-permute-done((bf16[256,1408]{1,0:T(8,128)(2,1)S(1)}, bf16[256,1408]{1,0:T(8,128)(2,1)S(1)}, u32[]{:S(2)}, u32[]{:S(2)}) %collective-permute-start.30) | collective-permute-done | bytes 720928 | tf_op jit(solution)/shard_map/ppermute | solution.py:126
  552.5 11.2 %multiply_reduce_fusion = (f32[4,1024]{1,0:T(4,128)S(1)}, f32[4,1024,1024]{1,2,0:T(8,128)}) fusion(f32[4,1024,1024]{1,2,0:T(8,128)} %get-tuple-element.459, f32[4,1024]{1,0:T(4,128)S(1)} %copy-done.127, bf16[1024,4,88]{0,2,1:T(8,128)(2,1)S(1)} %maximum_bitcast_fusion.1, bf16[1024,4,88]{0,2,1:T(8,128)(2,1)S(1)} %copy-done.73), kind=kOutput, calls=%fused_computation.5 | convolution fusion | flops 754970624 | bytes 35028992 | tf_op jit(solution)/shard_map/qhd,khd->hqk/dot_general | solution.py:18
  563.8 12.4 %multiply_convert_fusion = bf16[4,1024,1024]{1,2,0:T(8,128)(2,1)S(1)} fusion(f32[4,1024,1024]{1,2,0:T(8,128)} %get-tuple-element.473, f32[4,1024,1024]{1,2,0:T(8,128)} %get-tuple-element.459, f32[4,1024]{1,0:T(4,128)S(1)} %get-tuple-element.472, f32[4,1024]{1,0:T(4,128)S(1)} %copy-done.127), kind=kLoop, calls=%fused_computation.4 | loop fusion | flops 20971520 | bytes 41975808 | tf_op jit(solution)/shard_map/convert_element_type | solution.py:78
  589.0 9.8 %fusion.124 = bf16[1024,1,4,88]{0,3,2,1:T(8,128)(2,1)} fusion(bf16[1024,4,88]{0,2,1:T(8,128)(2,1)S(1)} %copy-done.51, f32[4,1024,1024]{1,2,0:T(8,128)} %get-tuple-element.459, f32[4,1024]{1,0:T(4,128)S(1)} %copy-done.127), kind=kOutput, calls=%fused_computation.279 | convolution fusion | flops 751140864 | bytes 18235392 | tf_op jit(solution)/shard_map/hqk,qhd->khd/dot_general | solution.py:18
  611.3 4.0 convert_add_fusion
  619.5 4.1 fusion.33
  625.6 6.7 add_convert_fusion
  632.3 4.7 convolution_convert_fusion.4
  637.0 4.3 copy.175
  645.7 4.0 convert_add_fusion.1
  658.4 11.0 %collective-permute-done.35 = bf16[256,1408]{1,0:T(8,128)(2,1)} collective-permute-done((bf16[256,1408]{1,0:T(8,128)(2,1)}, bf16[256,1408]{1,0:T(8,128)(2,1)}, u32[]{:S(2)}, u32[]{:S(2)}) %collective-permute-start.35) | collective-permute-done | bytes 720928 | tf_op jit(solution)/shard_map/ppermute | solution.py:126
  671.2 5.4 collective-permute-done.36
  689.6 5.2 fusion.30
  717.4 5.4 collective-permute-done.60
  726.9 9.9 %collective-permute-done.41 = bf16[256,1408]{1,0:T(8,128)(2,1)S(1)} collective-permute-done((bf16[256,1408]{1,0:T(8,128)(2,1)S(1)}, bf16[256,1408]{1,0:T(8,128)(2,1)S(1)}, u32[]{:S(2)}, u32[]{:S(2)}) %collective-permute-start.41) | collective-permute-done | bytes 720928 | tf_op jit(solution)/shard_map/ppermute | solution.py:126
  750.9 4.0 maximum_convert_fusion
  757.4 4.3 collective-permute-done.43
  807.6 6.8 fusion.10
  815.9 6.3 fusion.8
  828.0 7.3 collective-permute-done.53
  (973 shorter events, 417.1 us)
Async XLA Ops:
  7.2 71.7 %all-gather.6.cloned.1.call-start = ((), (), s32[]{:S(2)}) async-start(), calls=%async_computation.10 | async-start | bytes 2433024 | tf_op jit(solution)/shard_map/all_gather | solution.py:209
  9.3 130.1 %all-gather.8.cloned.1.call-start = ((), (), s32[]{:S(2)}) async-start(), calls=%async_computation.11 | async-start | bytes 4866048 | tf_op jit(solution)/shard_map/all_gather | solution.py:188
  13.8 34.8 %collective-permute-start = (bf16[256,2816]{1,0:T(8,128)(2,1)}, bf16[256,2816]{1,0:T(8,128)(2,1)}, u32[]{:S(2)}, u32[]{:S(2)}) collective-permute-start(bf16[256,2816]{1,0:T(8,128)(2,1)} %pad_maximum_fusion.16), channel_id=1, source_target_pairs={{0,4},{2,6},{4,0},{6,2},{1,5},{3,7},{5,1},{7,3},{8,12},{10,14},{12... | collective-permute-start | bytes 4325384 | tf_op jit(solution)/shard_map/ppermute | solution.py:126
  51.9 28.8 %collective-permute-start.1 = (bf16[512,2816]{1,0:T(8,128)(2,1)}, bf16[512,2816]{1,0:T(8,128)(2,1)}, u32[]{:S(2)}, u32[]{:S(2)}) collective-permute-start(bf16[512,2816]{1,0:T(8,128)(2,1)} %pad_maximum_fusion.4), channel_id=1, source_target_pairs={{0,2},{2,0},{4,6},{6,4},{1,3},{3,1},{5,7},{7,5},{8,10},{10,8},{12,... | collective-permute-start | bytes 8650760 | tf_op jit(solution)/shard_map/ppermute | solution.py:126
  53.8 79.5 %collective-permute-start.7 = (s32[256,2]{0,1:T(2,128)}, s32[256,2]{0,1:T(2,128)}, u32[]{:S(2)}, u32[]{:S(2)}) collective-permute-start(s32[256,2]{0,1:T(2,128)} %fusion.208), channel_id=1, source_target_pairs={{0,2},{2,0},{4,6},{6,4},{1,3},{3,1},{5,7},{7,5},{8,10},{10,8},{12,... | collective-permute-start | bytes 6152 | tf_op jit(solution)/shard_map/ppermute | solution.py:126
  54.3 65.7 %collective-permute-start.6 = (s32[256,2]{0,1:T(2,128)}, s32[256,2]{0,1:T(2,128)}, u32[]{:S(2)}, u32[]{:S(2)}) collective-permute-start(s32[256,2]{0,1:T(2,128)} %fusion.208), channel_id=1, source_target_pairs={{0,4},{2,6},{4,0},{6,2},{1,5},{3,7},{5,1},{7,3},{8,12},{10,14},{12... | collective-permute-start | bytes 6152 | tf_op jit(solution)/shard_map/ppermute | solution.py:126
  73.8 17.6 %all-to-all-start.2 = ((f32[4,1,1408]{2,1,0:T(1,128)}), f32[4,1,1408]{2,1,0:T(1,128)S(1)}, u32[]{:S(2)}, u32[]{:S(2)}) async-start(f32[4,1,1408]{2,1,0:T(1,128)} %all_to_all.32), calls=%async_computation.2 | async-start | bytes 45056 | tf_op jit(solution)/shard_map/all_to_all | solution.py:235
  94.9 102.8 %all-gather.12.cloned.1.call-start = ((), (), s32[]{:S(2)}) async-start(), calls=%async_computation.13 | async-start | bytes 2703360 | tf_op jit(solution)/shard_map/all_gather | solution.py:212
  115.1 18.0 %collective-permute-start.3 = (bf16[256,1408]{1,0:T(8,128)(2,1)}, bf16[256,1408]{1,0:T(8,128)(2,1)}, u32[]{:S(2)}, u32[]{:S(2)}) collective-permute-start(bf16[256,1408]{1,0:T(8,128)(2,1)} %add_convert_fusion.7), channel_id=1, source_target_pairs={{0,4},{2,6},{4,0},{6,2},{1,5},{3,7},{5,1},{7,3},{8,12},{10,14},{12... | collective-permute-start | bytes 2162696 | tf_op jit(solution)/shard_map/ppermute | solution.py:126
  116.7 209.5 %all-gather.14.cloned.1.call-start = ((), (), s32[]{:S(2)}) async-start(), calls=%async_computation.14 | async-start | bytes 4866048 | tf_op jit(solution)/shard_map/all_gather | solution.py:188
  153.4 37.8 %collective-permute-start.9 = (bf16[256,1408]{1,0:T(8,128)(2,1)S(1)}, bf16[256,1408]{1,0:T(8,128)(2,1)S(1)}, u32[]{:S(2)}, u32[]{:S(2)}) collective-permute-start(bf16[256,1408]{1,0:T(8,128)(2,1)S(1)} %get-tuple-element.99), channel_id=1, source_target_pairs={{0,4},{2,6},{4,0},{6,2},{1,5},{3,7},{5,1},{7,3},{8,12},{10,14},{12... | collective-permute-start | bytes 2162696 | tf_op jit(solution)/shard_map/ppermute | solution.py:126
  201.8 55.9 %collective-permute-start.13 = (bf16[1408,704]{0,1:T(8,128)(2,1)}, bf16[1408,704]{0,1:T(8,128)(2,1)}, u32[]{:S(2)}, u32[]{:S(2)}) collective-permute-start(bf16[1408,704]{0,1:T(8,128)(2,1)} %copy.148), channel_id=1, source_target_pairs={{0,1},{1,0},{2,3},{3,2},{4,5},{5,4},{6,7},{7,6},{8,9},{9,8},{10,11... | collective-permute-start | bytes 5947400 | tf_op jit(solution)/shard_map/ppermute | solution.py:118
  209.4 18.5 %collective-permute-start.12 = (bf16[256,1408]{1,0:T(8,128)(2,1)}, bf16[256,1408]{1,0:T(8,128)(2,1)S(1)}, u32[]{:S(2)}, u32[]{:S(2)}) collective-permute-start(bf16[256,1408]{1,0:T(8,128)(2,1)} %slice.978), channel_id=1, source_target_pairs={{0,4},{2,6},{4,0},{6,2},{1,5},{3,7},{5,1},{7,3},{8,12},{10,14},{12... | collective-permute-start | bytes 2162696 | tf_op jit(solution)/shard_map/ppermute | solution.py:126
  210.9 169.2 %all-gather.10.cloned.1.call-start = ((), (), s32[]{:S(2)}) async-start(), calls=%async_computation.12 | async-start | bytes 4866048 | tf_op jit(solution)/shard_map/all_gather | solution.py:188
  259.4 17.1 %collective-permute-start.14 = (bf16[256,1408]{1,0:T(8,128)(2,1)}, bf16[256,1408]{1,0:T(8,128)(2,1)}, u32[]{:S(2)}, u32[]{:S(2)}) collective-permute-start(bf16[256,1408]{1,0:T(8,128)(2,1)} %add_convert_fusion.6), channel_id=1, source_target_pairs={{0,4},{2,6},{4,0},{6,2},{1,5},{3,7},{5,1},{7,3},{8,12},{10,14},{12... | collective-permute-start | bytes 2162696 | tf_op jit(solution)/shard_map/ppermute | solution.py:126
  296.9 254.3 %reduce-scatter.13.cloned.1.call-start = ((), (), s32[]{:S(2)}) async-start(), calls=%async_computation.15 | async-start | bytes 4866048 | tf_op jit(solution)/shard_map/reduce_scatter | solution.py:335
  304.6 18.5 %collective-permute-start.18 = (bf16[256,1408]{1,0:T(8,128)(2,1)S(1)}, bf16[256,1408]{1,0:T(8,128)(2,1)S(1)}, u32[]{:S(2)}, u32[]{:S(2)}) collective-permute-start(bf16[256,1408]{1,0:T(8,128)(2,1)S(1)} %slice.977), channel_id=1, source_target_pairs={{0,4},{2,6},{4,0},{6,2},{1,5},{3,7},{5,1},{7,3},{8,12},{10,14},{12... | collective-permute-start | bytes 2162696 | tf_op jit(solution)/shard_map/ppermute | solution.py:126
  308.0 37.0 %collective-permute-start.10 = (bf16[512,1408]{1,0:T(8,128)(2,1)}, bf16[512,1408]{1,0:T(8,128)(2,1)}, u32[]{:S(2)}, u32[]{:S(2)}) collective-permute-start(bf16[512,1408]{1,0:T(8,128)(2,1)} %pad_maximum_fusion.17), channel_id=1, source_target_pairs={{0,2},{2,0},{4,6},{6,4},{1,3},{3,1},{5,7},{7,5},{8,10},{10,8},{12,... | collective-permute-start | bytes 4325384 | tf_op jit(solution)/shard_map/ppermute | solution.py:126
  327.3 17.7 %collective-permute-start.19 = (bf16[256,1408]{1,0:T(8,128)(2,1)S(1)}, bf16[256,1408]{1,0:T(8,128)(2,1)S(1)}, u32[]{:S(2)}, u32[]{:S(2)}) collective-permute-start(bf16[256,1408]{1,0:T(8,128)(2,1)S(1)} %add_convert_fusion.5), channel_id=1, source_target_pairs={{0,4},{2,6},{4,0},{6,2},{1,5},{3,7},{5,1},{7,3},{8,12},{10,14},{12... | collective-permute-start | bytes 2162696 | tf_op jit(solution)/shard_map/ppermute | solution.py:126
  358.8 45.9 %collective-permute-start.22 = (bf16[1,2816,352]{1,2,0:T(8,128)(2,1)}, bf16[1,2816,352]{1,2,0:T(8,128)(2,1)}, u32[]{:S(2)}, u32[]{:S(2)}) collective-permute-start(bf16[1,2816,352]{1,2,0:T(8,128)(2,1)} %bitcast.451), channel_id=1, source_target_pairs={{0,4},{2,6},{4,0},{6,2},{1,5},{3,7},{5,1},{7,3},{8,12},{10,14},{12... | collective-permute-start | bytes 5947400 | tf_op jit(solution)/shard_map/ppermute | solution.py:126
  379.8 229.1 %reduce-scatter.15.cloned.1.call-start = ((), (), s32[]{:S(2)}) async-start(), calls=%async_computation.16 | async-start | bytes 4866048 | tf_op jit(solution)/shard_map/reduce_scatter | solution.py:335
  420.9 18.6 %collective-permute-start.24 = (bf16[256,1408]{1,0:T(8,128)(2,1)S(1)}, bf16[256,1408]{1,0:T(8,128)(2,1)S(1)}, u32[]{:S(2)}, u32[]{:S(2)}) collective-permute-start(bf16[256,1408]{1,0:T(8,128)(2,1)S(1)} %slice.976), channel_id=1, source_target_pairs={{0,4},{2,6},{4,0},{6,2},{1,5},{3,7},{5,1},{7,3},{8,12},{10,14},{12... | collective-permute-start | bytes 2162696 | tf_op jit(solution)/shard_map/ppermute | solution.py:126
  441.5 17.7 %collective-permute-start.25 = (bf16[256,1408]{1,0:T(8,128)(2,1)S(1)}, bf16[256,1408]{1,0:T(8,128)(2,1)S(1)}, u32[]{:S(2)}, u32[]{:S(2)}) collective-permute-start(bf16[256,1408]{1,0:T(8,128)(2,1)S(1)} %get-tuple-element.318), channel_id=1, source_target_pairs={{0,4},{2,6},{4,0},{6,2},{1,5},{3,7},{5,1},{7,3},{8,12},{10,14},{12... | collective-permute-start | bytes 2162696 | tf_op jit(solution)/shard_map/ppermute | solution.py:126
  442.5 97.1 %collective-permute-start.46 = (bf16[2,2816,352]{1,2,0:T(8,128)(2,1)}, bf16[2,2816,352]{1,2,0:T(8,128)(2,1)}, u32[]{:S(2)}, u32[]{:S(2)}) collective-permute-start(bf16[2,2816,352]{1,2,0:T(8,128)(2,1)} %pad_maximum_fusion.2), channel_id=1, source_target_pairs={{0,2},{2,0},{4,6},{6,4},{1,3},{3,1},{5,7},{7,5},{8,10},{10,8},{12,... | collective-permute-start | bytes 11894792 | tf_op jit(solution)/shard_map/ppermute | solution.py:126
  448.1 18.8 %collective-permute-start.26 = (bf16[256,1408]{1,0:T(8,128)(2,1)S(1)}, bf16[256,1408]{1,0:T(8,128)(2,1)}, u32[]{:S(2)}, u32[]{:S(2)}) collective-permute-start(bf16[256,1408]{1,0:T(8,128)(2,1)S(1)} %get-tuple-element.318), channel_id=1, source_target_pairs={{0,2},{2,0},{4,6},{6,4},{1,3},{3,1},{5,7},{7,5},{8,10},{10,8},{12,... | collective-permute-start | bytes 2162696 | tf_op jit(solution)/shard_map/ppermute | solution.py:126
  461.6 195.0 %reduce-scatter.19.cloned.1.call-start = ((), (), s32[]{:S(2)}) async-start(), calls=%async_computation.18 | async-start | bytes 1351680
  499.0 18.2 %collective-permute-start.29 = (bf16[256,1408]{1,0:T(8,128)(2,1)S(1)}, bf16[256,1408]{1,0:T(8,128)(2,1)S(1)}, u32[]{:S(2)}, u32[]{:S(2)}) collective-permute-start(bf16[256,1408]{1,0:T(8,128)(2,1)S(1)} %slice.975), channel_id=1, source_target_pairs={{0,4},{2,6},{4,0},{6,2},{1,5},{3,7},{5,1},{7,3},{8,12},{10,14},{12... | collective-permute-start | bytes 2162696 | tf_op jit(solution)/shard_map/ppermute | solution.py:126
  520.2 17.4 %collective-permute-start.30 = (bf16[256,1408]{1,0:T(8,128)(2,1)S(1)}, bf16[256,1408]{1,0:T(8,128)(2,1)S(1)}, u32[]{:S(2)}, u32[]{:S(2)}) collective-permute-start(bf16[256,1408]{1,0:T(8,128)(2,1)S(1)} %get-tuple-element.320), channel_id=1, source_target_pairs={{0,4},{2,6},{4,0},{6,2},{1,5},{3,7},{5,1},{7,3},{8,12},{10,14},{12... | collective-permute-start | bytes 2162696 | tf_op jit(solution)/shard_map/ppermute | solution.py:126
  551.2 54.6 %collective-permute-start.37 = (bf16[1,352,768]{2,1,0:T(8,128)(2,1)}, bf16[1,352,768]{2,1,0:T(8,128)(2,1)}, u32[]{:S(2)}, u32[]{:S(2)}) collective-permute-start(bf16[1,352,768]{2,1,0:T(8,128)(2,1)} %bitcast.511), channel_id=1, source_target_pairs={{0,4},{2,6},{4,0},{6,2},{1,5},{3,7},{5,1},{7,3},{8,12},{10,14},{12... | collective-permute-start | bytes 1622024 | tf_op jit(solution)/shard_map/ppermute | solution.py:126
  551.7 59.6 %collective-permute-start.39 = (bf16[512,1408]{1,0:T(8,128)(2,1)}, bf16[512,1408]{1,0:T(8,128)(2,1)}, u32[]{:S(2)}, u32[]{:S(2)}) collective-permute-start(bf16[512,1408]{1,0:T(8,128)(2,1)} %fusion.32), channel_id=1, source_target_pairs={{0,2},{2,0},{4,6},{6,4},{1,3},{3,1},{5,7},{7,5},{8,10},{10,8},{12,... | collective-permute-start | bytes 4325384 | tf_op jit(solution)/shard_map/ppermute | solution.py:126
  551.9 63.5 %collective-permute-start.33 = (bf16[1408,880]{0,1:T(8,128)(2,1)}, bf16[1408,880]{0,1:T(8,128)(2,1)}, u32[]{:S(2)}, u32[]{:S(2)}) collective-permute-start(bf16[1408,880]{0,1:T(8,128)(2,1)} %pad_maximum_fusion.11), channel_id=1, source_target_pairs={{0,1},{1,0},{2,3},{3,2},{4,5},{5,4},{6,7},{7,6},{8,9},{9,8},{10,11... | collective-permute-start | bytes 7434248 | tf_op jit(solution)/shard_map/ppermute | solution.py:118
  608.8 43.6 %collective-permute-start.38 = (bf16[2,352,768]{2,1,0:T(8,128)(2,1)}, bf16[2,352,768]{2,1,0:T(8,128)(2,1)}, u32[]{:S(2)}, u32[]{:S(2)}) collective-permute-start(bf16[2,352,768]{2,1,0:T(8,128)(2,1)} %pad_maximum_fusion.20), channel_id=1, source_target_pairs={{0,2},{2,0},{4,6},{6,4},{1,3},{3,1},{5,7},{7,5},{8,10},{10,8},{12,... | collective-permute-start | bytes 3244040 | tf_op jit(solution)/shard_map/ppermute | solution.py:126
  611.2 132.7 %reduce-scatter.21.cloned.1.call-start = ((), (), s32[]{:S(2)}) async-start(), calls=%async_computation.19 | async-start | bytes 3153920
  623.6 22.0 %collective-permute-start.34 = (bf16[512,1408]{1,0:T(8,128)(2,1)}, bf16[512,1408]{1,0:T(8,128)(2,1)}, u32[]{:S(2)}, u32[]{:S(2)}) collective-permute-start(bf16[512,1408]{1,0:T(8,128)(2,1)} %fusion.33), channel_id=1, source_target_pairs={{0,2},{2,0},{4,6},{6,4},{1,3},{3,1},{5,7},{7,5},{8,10},{10,8},{12,... | collective-permute-start | bytes 4325384 | tf_op jit(solution)/shard_map/ppermute | solution.py:126
  641.4 35.2 %collective-permute-start.36 = (bf16[1408,528]{0,1:T(8,128)(2,1)}, bf16[1408,528]{0,1:T(8,128)(2,1)}, u32[]{:S(2)}, u32[]{:S(2)}) collective-permute-start(bf16[1408,528]{0,1:T(8,128)(2,1)} %convolution_convert_fusion.4), channel_id=1, source_target_pairs={{0,1},{1,0},{2,3},{3,2},{4,5},{5,4},{6,7},{7,6},{8,9},{9,8},{10,11... | collective-permute-start | bytes 4460552 | tf_op jit(solution)/shard_map/ppermute | solution.py:118
  650.6 18.8 %collective-permute-start.35 = (bf16[256,1408]{1,0:T(8,128)(2,1)}, bf16[256,1408]{1,0:T(8,128)(2,1)}, u32[]{:S(2)}, u32[]{:S(2)}) collective-permute-start(bf16[256,1408]{1,0:T(8,128)(2,1)} %slice.974), channel_id=1, source_target_pairs={{0,4},{2,6},{4,0},{6,2},{1,5},{3,7},{5,1},{7,3},{8,12},{10,14},{12... | collective-permute-start | bytes 2162696 | tf_op jit(solution)/shard_map/ppermute | solution.py:126
  689.5 55.9 %reduce-scatter.23.cloned.1.call-start = ((), (), s32[]{:S(2)}) async-start(), calls=%async_computation.20 | async-start | bytes 2252800
  698.5 107.5 %reduce-scatter.17.cloned.1.call-start = ((), (), s32[]{:S(2)}) async-start(), calls=%async_computation.17 | async-start | bytes 1351680 | tf_op jit(solution)/shard_map/reduce_scatter | solution.py:458
  712.9 23.9 %collective-permute-start.41 = (bf16[256,1408]{1,0:T(8,128)(2,1)S(1)}, bf16[256,1408]{1,0:T(8,128)(2,1)S(1)}, u32[]{:S(2)}, u32[]{:S(2)}) collective-permute-start(bf16[256,1408]{1,0:T(8,128)(2,1)S(1)} %slice.973), channel_id=1, source_target_pairs={{0,4},{2,6},{4,0},{6,2},{1,5},{3,7},{5,1},{7,3},{8,12},{10,14},{12... | collective-permute-start | bytes 2162696 | tf_op jit(solution)/shard_map/ppermute | solution.py:126
  715.7 24.8 %collective-permute-start.40 = (bf16[2,4,176,352]{3,2,1,0:T(8,128)(2,1)S(1)}, bf16[2,4,176,352]{3,2,1,0:T(8,128)(2,1)S(1)}, u32[]{:S(2)}, u32[]{:S(2)}) collective-permute-start(bf16[2,4,176,352]{3,2,1,0:T(8,128)(2,1)S(1)} %dynamic-slice_bitcast_fusion), channel_id=1, source_target_pairs={{0,1},{1,0},{2,3},{3,2},{4,5},{5,4},{6,7},{7,6},{8,9},{9,8},{10,11... | collective-permute-start | bytes 2973704 | tf_op jit(solution)/shard_map/ppermute | solution.py:118
  724.1 17.8 %collective-permute-start.61 = (bf16[2,352,768]{2,1,0:T(8,128)(2,1)S(1)}, bf16[2,352,768]{2,1,0:T(8,128)(2,1)S(1)}, u32[]{:S(2)}, u32[]{:S(2)}) collective-permute-start(bf16[2,352,768]{2,1,0:T(8,128)(2,1)S(1)} %pad_maximum_fusion.22), channel_id=1, source_target_pairs={{0,2},{2,0},{4,6},{6,4},{1,3},{3,1},{5,7},{7,5},{8,10},{10,8},{12,... | collective-permute-start | bytes 3244040 | tf_op jit(solution)/shard_map/ppermute | solution.py:126
  750.4 19.5 %collective-permute-start.45 = (bf16[256,1408]{1,0:T(8,128)(2,1)S(1)}, bf16[256,1408]{1,0:T(8,128)(2,1)}, u32[]{:S(2)}, u32[]{:S(2)}) collective-permute-start(bf16[256,1408]{1,0:T(8,128)(2,1)S(1)} %get-tuple-element.145), channel_id=1, source_target_pairs={{0,1},{1,0},{2,3},{3,2},{4,5},{5,4},{6,7},{7,6},{8,9},{9,8},{10,11... | collective-permute-start | bytes 2162696 | tf_op jit(solution)/shard_map/ppermute | solution.py:118
  761.7 28.5 %collective-permute-start.55 = (bf16[1,352,528]{1,2,0:T(8,128)(2,1)}, bf16[1,352,528]{1,2,0:T(8,128)(2,1)S(1)}, u32[]{:S(2)}, u32[]{:S(2)}) collective-permute-start(bf16[1,352,528]{1,2,0:T(8,128)(2,1)} %bitcast.123), channel_id=1, source_target_pairs={{0,2},{2,0},{4,6},{6,4},{1,3},{3,1},{5,7},{7,5},{8,10},{10,8},{12,... | collective-permute-start | bytes 1115144 | tf_op jit(solution)/shard_map/ppermute | solution.py:126
  763.9 24.9 %collective-permute-start.58 = (bf16[1,352,880]{2,1,0:T(8,128)(2,1)}, bf16[1,352,880]{2,1,0:T(8,128)(2,1)}, u32[]{:S(2)}, u32[]{:S(2)}) collective-permute-start(bf16[1,352,880]{2,1,0:T(8,128)(2,1)} %copy.161), channel_id=1, source_target_pairs={{0,2},{2,0},{4,6},{6,4},{1,3},{3,1},{5,7},{7,5},{8,10},{10,8},{12,... | collective-permute-start | bytes 1858568 | tf_op jit(solution)/shard_map/ppermute | solution.py:126
  764.2 23.2 %collective-permute-start.57 = (bf16[1,352,880]{2,1,0:T(8,128)(2,1)}, bf16[1,352,880]{2,1,0:T(8,128)(2,1)}, u32[]{:S(2)}, u32[]{:S(2)}) collective-permute-start(bf16[1,352,880]{2,1,0:T(8,128)(2,1)} %copy.161), channel_id=1, source_target_pairs={{0,4},{2,6},{4,0},{6,2},{1,5},{3,7},{5,1},{7,3},{8,12},{10,14},{12... | collective-permute-start | bytes 1858568 | tf_op jit(solution)/shard_map/ppermute | solution.py:126
  769.8 44.6 %collective-permute-start.44 = (f32[352,128]{1,0:T(8,128)S(1)}, f32[352,128]{1,0:T(8,128)}, u32[]{:S(2)}, u32[]{:S(2)}) collective-permute-start(f32[352,128]{1,0:T(8,128)S(1)} %add.915), channel_id=1, source_target_pairs={{0,1},{1,0},{2,3},{3,2},{4,5},{5,4},{6,7},{7,6},{8,9},{9,8},{10,11... | collective-permute-start | bytes 540680 | tf_op jit(solution)/shard_map/ppermute | solution.py:126
  806.0 17.6 %collective-permute-start.50 = (bf16[1,352,352]{2,1,0:T(8,128)(2,1)}, bf16[1,352,352]{2,1,0:T(8,128)(2,1)S(1)}, u32[]{:S(2)}, u32[]{:S(2)}) collective-permute-start(bf16[1,352,352]{2,1,0:T(8,128)(2,1)} %bitcast.520), channel_id=1, source_target_pairs={{0,2},{2,0},{4,6},{6,4},{1,3},{3,1},{5,7},{7,5},{8,10},{10,8},{12,... | collective-permute-start | bytes 743432 | tf_op jit(solution)/shard_map/ppermute | solution.py:126
  822.2 22.3 %collective-permute-start.47 = (bf16[256,1408]{1,0:T(8,128)(2,1)S(1)}, bf16[256,1408]{1,0:T(8,128)(2,1)}, u32[]{:S(2)}, u32[]{:S(2)}) collective-permute-start(bf16[256,1408]{1,0:T(8,128)(2,1)S(1)} %copy-done.71), channel_id=1, source_target_pairs={{0,1},{1,0},{2,3},{3,2},{4,5},{5,4},{6,7},{7,6},{8,9},{9,8},{10,11... | collective-permute-start | bytes 2162696 | tf_op jit(solution)/shard_map/ppermute | solution.py:118
  (254 other events, 2953.9 us)
Sparse Core Ops, SparseCore 0:
  10.8 52.5 all-gather.5
  66.0 73.3 all-gather.7
  141.5 45.2 all-gather.11
  211.0 80.6 all-gather.13
  297.0 71.5 all-gather.9
  379.9 88.2 reduce-scatter.12
  472.3 89.9 reduce-scatter.14
  611.3 23.5 reduce-scatter.18
  642.6 48.9 reduce-scatter.20
  698.6 38.1 reduce-scatter.22
  755.0 25.8 reduce-scatter.16
